TPU v7x, 32 devices: a whole 2x2x4 slice. The times are simulated.
32 devices in a mesh: grp: 2 (over x), role: 2 (over core), tp: 8 (over z, y).
Axes of the slice: x: 2, y: 2, z: 4, core: 2. Of those that a mesh axis runs over, the one named last changes fastest.
Arguments:
- stretch_tokens: bfloat16 [2, 1024, 8192], P('role', ('grp', 'tp')), parts along dimension 1, may hold values from -60 to 60
- norm_gain: bfloat16 [8192], replicated, may hold values from 0.5 to 8
- q_weight: bfloat16 [8192, 8192], P(None, 'tp'), may hold values from -0.0625 to 0.0625
- kv_weight: bfloat16 [8192, 2048], P(None, 'tp'), may hold values from -1 to 1
- dec_query: bfloat16 [128, 8192], P(('grp', 'role', 'tp')), parts along dimension 0, may hold values from -70 to 70
- dec_new_kv: bfloat16 [128, 2048], P(('grp', 'role', 'tp')), parts along dimension 0, may hold values from -6 to 6
- kv_pool: bfloat16 [3072, 16, 2048], P(('grp', 'role', 'tp')), parts along dimension 0, may hold values from -6 to 6
- page_table: int32 [128, 24], P(('grp', 'role', 'tp')), parts along dimension 0, may hold values from 0 to 95, as said below
- cache_lengths: int32 [128], P(('grp', 'role', 'tp')), parts along dimension 0, may hold values from 64 to 384, as said below
- handoff_slot: int32 [32, 4], P(('grp', 'role', 'tp')), parts along dimension 0, may hold values from 0 to 95, as said below
Outputs:
- prefill_context: bfloat16 [2, 1024, 8192], P('role', 'grp', 'tp'), parts along dimension 1
- decode_output: bfloat16 [128, 8192], P(('grp', 'role', 'tp')), parts along dimension 0
There are 2 independent parts, one for each index of `grp`. A program takes and returns all parts, laid end to end along the dimension named above; an argument that names none is the same for every part. Nothing has to cross between parts.
Inputs may be any that keep to these rules, and one draw needn't show every extreme that they name: `page_table`: the 4 rows of each pool list distinct pages of that pool; together they list every page of it once. `cache_lengths`: some row of every draw holds 384 tokens. `handoff_slot`: the 4 pages of a pool are distinct, and each is a page that some row of that pool lists at a page-table entry lying wholly below its cache length.
All inputs are finite; a program needn't handle non-finite values.
Results may differ from a plain program's by a relative error of at most 0.017.
The roundings to bfloat16 on the way count: a program that leaves them out, or rounds other values in their place, can miss the bound.
Values may be sent and summed in bfloat16 or wider, within the bound.
No kernel may reach another device: no remote copies, remote signals or barrier semaphores. Data moves between devices by JAX's collectives and lax.ppermute only.
A program may use at most 192 MiB of HBM per device.

v0:
```python
import functools

import jax
import jax.numpy as jnp
from jax import lax
from jax.experimental import pallas as pl
from jax.experimental.pallas import tpu as pltpu
from jax.sharding import PartitionSpec as P

KVH = 8
HD = 128
GROUP = 8
MASKED = -1e30

norm_eps = 1e-05
rope_base = 500000.0


LOG2E = 1.4426950408889634
VMEM_LIMIT = 14 * 2**20


def swapped(value, axis, bit):
    mask = 2**bit
    pairs = [(source, source ^ mask) for source in range(lax.axis_size(axis))]
    return lax.ppermute(value, axis, pairs)


def from_behind(value, axis, steps):
    count = lax.axis_size(axis)
    pairs = [(source, (source + steps) % count) for source in range(count)]
    return lax.ppermute(value, axis, pairs)


def ordered_pair(mine, other, upper, axis):
    first = jnp.where(upper == 1, other, mine)
    second = jnp.where(upper == 1, mine, other)
    return jnp.concatenate((first, second), axis=axis)


def spread_members(blocks, member, low_bit, member_bits, mover):
    members = blocks.shape[0]
    order = jnp.bitwise_xor(member, jnp.arange(members))
    buffer = blocks[order]
    for step in range(member_bits):
        width = 2**step
        view = buffer.reshape(members // (2 * width), 2, width, blocks.shape[1], blocks.shape[2])
        arrived = mover(view[:, 1], low_bit + step)
        buffer = jnp.stack((view[:, 0], arrived), axis=1).reshape(blocks.shape)
    return buffer[order]


def rotation_tables(count, width, first_col, only_keys):
    columns = first_col + jnp.arange(width)
    pair_index = columns % HD // 2
    inverse = jnp.exp(
        -(2.0 * pair_index.astype(jnp.float32) / HD) * jnp.log(jnp.float32(rope_base))
    )
    angle = jnp.arange(count).astype(jnp.float32)[:, None] * inverse[None, :]
    cosine = jnp.cos(angle)
    sine = jnp.where(columns % 2 == 0, -1.0, 1.0)[None, :] * jnp.sin(angle)
    if only_keys:
        is_key = (columns % (2 * HD) < HD)[None, :]
        cosine = jnp.where(is_key, cosine, 1.0)
        sine = jnp.where(is_key, sine, 0.0)
    return cosine, sine


def turned(tile, cosine, sine):
    lane = lax.broadcasted_iota(jnp.int32, tile.shape, 1)
    after = pltpu.roll(tile, HD - 1, 1)
    before = pltpu.roll(tile, 1, 1)
    return tile * cosine + jnp.where(lane % 2 == 0, after, before) * sine


def normalize(x_refs, chunk_rows, gain, normed):
    width = normed.shape[1]
    part = 512
    first = 0
    for x_ref, rows in zip(x_refs, chunk_rows):

        def add(i, total, x_ref=x_ref):
            tile = x_ref[:, pl.ds(pl.multiple_of(i * part, part), part)].astype(jnp.float32)
            tile = tile * tile
            sums = [tile[:, col : col + 128] for col in range(0, part, 128)]
            return total + ((sums[0] + sums[1]) + (sums[2] + sums[3]))

        total = lax.fori_loop(
            0, width // part, add, jnp.zeros((rows, 128), jnp.float32), unroll=4
        )
        mean_sq = jnp.sum(total, axis=1, keepdims=True) / width
        scale = lax.rsqrt(mean_sq + norm_eps)

        def write(i, carry, x_ref=x_ref, rows=rows, first=first, scale=scale):
            here = pl.ds(pl.multiple_of(i * part, part), part)
            normed[first : first + rows, here] = (
                x_ref[:, here].astype(jnp.float32) * scale * gain[:, here].astype(jnp.float32)
            ).astype(jnp.bfloat16)
            return carry

        lax.fori_loop(0, width // part, write, 0, unroll=4)
        first += rows


def project_kernel(chunk_rows, rotated, blocks, place, ready, member, *refs):
    jobs = len(rotated)
    n = 1 if ready else len(chunk_rows)
    x_refs, gain = refs[:n], refs[n]
    job_refs = refs[n + 1 : n + 1 + 3 * jobs]
    outs = refs[n + 1 + 3 * jobs :]
    starts = place(member[0])
    if ready:
        normed = x_refs[0]
    else:
        normed = refs[-1]
        normalize(x_refs, chunk_rows, gain, normed)
    for j in range(jobs):
        weight, cos_ref, sin_ref = job_refs[3 * j : 3 * j + 3]
        table = cos_ref.shape[1]
        columns = weight.shape[1]
        tile = min(256, columns)
        own_outs, outs = outs[: blocks[j]], outs[blocks[j] :]
        per_out = sum(chunk_rows) // blocks[j]
        for low in range(0, columns, tile):
            product = jnp.dot(
                normed[...], weight[:, low : low + tile], preferred_element_type=jnp.float32
            )
            first = 0
            for i, rows in enumerate(chunk_rows):
                where = pl.ds(pl.multiple_of(starts[i], rows), rows)
                for col in range(low, low + tile, HD):
                    here = product[first : first + rows, col - low : col - low + HD]
                    if rotated[j][col // HD]:
                        at = col % table
                        here = turned(
                            here, cos_ref[where, at : at + HD], sin_ref[where, at : at + HD]
                        )
                    at = first % per_out
                    own_outs[first // per_out][at : at + rows, col : col + HD] = here.astype(
                        jnp.bfloat16
                    )
                first += rows


def project(chunks, place, member, gain, jobs, ready=None, keep=False):
    chunk_rows = tuple(chunk.shape[0] for chunk in chunks)
    rows = sum(chunk_rows)
    width = chunks[0].shape[1]
    columns = [job[0].shape[1] for job in jobs]
    rows_in = [ready] if ready is not None else list(chunks)
    operands = [*rows_in, gain, *(part for job in jobs for part in job[:3])]
    vmem = pl.BlockSpec(memory_space=pltpu.VMEM)
    blocks = [job[4] for job in jobs]
    outs = [
        jax.ShapeDtypeStruct((rows // n, c), jnp.bfloat16)
        for n, c in zip(blocks, columns)
        for _ in range(n)
    ]
    normed = (rows, width)
    scratch = []
    if keep:
        outs.append(jax.ShapeDtypeStruct(normed, jnp.bfloat16))
    elif ready is None:
        scratch.append(pltpu.VMEM(normed, jnp.bfloat16))
    return pl.pallas_call(
        functools.partial(
            project_kernel,
            chunk_rows,
            [job[3] for job in jobs],
            blocks,
            place,
            ready is not None,
        ),
        out_shape=outs,
        in_specs=[pl.BlockSpec(memory_space=pltpu.SMEM)] + [vmem] * len(operands),
        out_specs=[vmem] * len(outs),
        scratch_shapes=scratch,
        compiler_params=pltpu.CompilerParams(vmem_limit_bytes=VMEM_LIMIT),
        cost_estimate=pl.CostEstimate(
            flops=2 * rows * width * sum(columns),
            bytes_accessed=2 * width * (rows + sum(columns)),
            transcendentals=0,
        ),
        name="project",
    )(member, *operands)


def attend_kernel(chunk_rows, n, place, member, *refs):
    starts = place(member[0])
    q_refs, kv_refs, (out, q_all, kv_all, keys_t, scores) = refs[:n], refs[n:-5], refs[-5:]
    count, columns = out.shape
    heads = columns // HD
    tile = scores.shape[0] // heads
    for sources, target in ((q_refs, q_all), (kv_refs, kv_all)):
        i = 0
        for source in sources:
            first = 0
            while first < source.shape[0]:
                rows = chunk_rows[i]
                where = pl.ds(pl.multiple_of(starts[i], rows), rows)
                target[where, :] = source[first : first + rows, :]
                first += rows
                i += 1
    keys_t[...] = kv_all[:, :HD].astype(jnp.float32).T.astype(jnp.bfloat16)
    scale = HD ** (-0.5) * LOG2E
    row = lax.broadcasted_iota(jnp.int32, (tile, tile), 0)
    col = lax.broadcasted_iota(jnp.int32, (tile, tile), 1)
    triangle = row >= col
    for low in range(0, count, tile):
        top = low + tile
        query = jnp.concatenate(
            [q_all[low:top, h * HD : (h + 1) * HD] for h in range(heads)], axis=0
        )
        scores[:, :top] = jnp.dot(query, keys_t[:, :top], preferred_element_type=jnp.float32)
        for h in range(heads):
            mine = slice(h * tile, (h + 1) * tile)
            edge = jnp.where(triangle, scores[mine, low:top], MASKED)
            highest = jnp.max(edge, axis=1, keepdims=True)
            if low:
                body = scores[mine, :low]
                highest = jnp.maximum(highest, jnp.max(body, axis=1, keepdims=True))
                body = jnp.exp2((body - highest) * scale)
            edge = jnp.exp2((edge - highest) * scale)
            total = jnp.sum(edge, axis=1, keepdims=True)
            if low:
                total = total + jnp.sum(body, axis=1, keepdims=True)
            share = 1.0 / total
            mixed = jnp.dot(
                (edge * share).astype(jnp.bfloat16),
                kv_all[low:top, HD:],
                preferred_element_type=jnp.float32,
            )
            if low:
                mixed = mixed + jnp.dot(
                    (body * share).astype(jnp.bfloat16),
                    kv_all[:low, HD:],
                    preferred_element_type=jnp.float32,
                )
            out[low:top, h * HD : (h + 1) * HD] = mixed.astype(jnp.bfloat16)


def attend(queries, kvs, chunk_rows, place, member):
    count = sum(chunk_rows)
    q_width = queries[0].shape[1]
    tile = min(256, count)
    vmem = pl.BlockSpec(memory_space=pltpu.VMEM)
    return pl.pallas_call(
        functools.partial(
            attend_kernel, tuple(chunk_rows), len(queries), place
        ),
        out_shape=jax.ShapeDtypeStruct((count, q_width), jnp.bfloat16),
        in_specs=[pl.BlockSpec(memory_space=pltpu.SMEM)] + [vmem] * (len(queries) + len(kvs)),
        out_specs=vmem,
        scratch_shapes=[
            pltpu.VMEM((count, q_width), jnp.bfloat16),
            pltpu.VMEM((count, 2 * HD), jnp.bfloat16),
            pltpu.VMEM((HD, count), jnp.bfloat16),
            pltpu.VMEM((tile * (q_width // HD), count), jnp.float32),
        ],
        compiler_params=pltpu.CompilerParams(vmem_limit_bytes=VMEM_LIMIT),
        cost_estimate=pl.CostEstimate(
            flops=2 * count * count * q_width,
            bytes_accessed=4 * count * (q_width + 2 * HD),
            transcendentals=count * count * q_width // HD // 2,
        ),
        name="attend",
    )(member, *queries, *kvs)


def decode_old_kernel(
    tables,
    lengths,
    slots,
    query_ref,
    own_ref,
    pool,
    acc_ref,
    state_ref,
    queries,
    allowed,
    limits,
    scores,
    own,
):
    rows, pages = tables.shape
    handed = slots.shape[1]
    total_pages, page, width = pool.shape
    columns = queries.shape[1]
    per_head = columns // KVH
    scale = HD ** (-0.5) * LOG2E
    lane = lax.broadcasted_iota(jnp.int32, (1, columns), 1)
    lane_row = lane % rows

    limits[...] = jnp.zeros_like(limits)

    def one_entry(e, owners):
        for r in range(rows):
            at = tables[r, e]
            count = jnp.clip(lengths[r] - e * page, 0, page)
            for j in range(handed):
                taken = slots[0, j] == at
                count = jnp.where(taken, 0, count)
                owners = owners[:j] + (jnp.where(taken, r, owners[j]),) + owners[j + 1 :]
            limits[pl.ds(at, 1), :] = jnp.where(lane_row == r, count, 0)
        return owners

    owners = lax.fori_loop(0, pages, one_entry, (jnp.int32(-1),) * handed)
    for j in range(handed):
        allowed[j * page : (j + 1) * page, :] = jnp.broadcast_to(
            jnp.where(lane_row == owners[j], 1.0, 0.0), (page, columns)
        )

    stacked = jnp.concatenate(
        [query_ref[:, i * HD : (i + 1) * HD].astype(jnp.float32) for i in range(KVH * GROUP)],
        axis=0,
    )
    turned_q = stacked.T.astype(jnp.bfloat16)
    for h in range(KVH):
        queries[2 * h * HD : (2 * h + 1) * HD, :] = jnp.where(
            lane // per_head == h, turned_q, jnp.zeros_like(turned_q)
        )
        queries[(2 * h + 1) * HD : (2 * h + 2) * HD, :] = jnp.zeros((HD, columns), jnp.bfloat16)

    own[...] = jnp.zeros_like(own)
    own[0:rows, :] = own_ref[...]
    own_score = jnp.dot(own[...], queries[...], preferred_element_type=jnp.float32)
    own_line = lax.broadcasted_iota(jnp.int32, own_score.shape, 0)
    own_score = jnp.where(own_line == lane_row, own_score, MASKED)
    highest = jnp.max(own_score, axis=0, keepdims=True)
    step = total_pages // 4
    line = lax.broadcasted_iota(jnp.int32, (step, page, columns), 1)
    for first in range(0, total_pages, step):
        score = jnp.dot(
            pool[first : first + step].reshape(step * page, width),
            queries[...],
            preferred_element_type=jnp.float32,
        ).reshape(step, page, columns)
        limit = limits[first : first + step, :].reshape(step, 1, columns)
        score = jnp.where(line < limit, score, MASKED)
        score = score.reshape(step * page, columns)
        scores[first * page : (first + step) * page, :] = score
        highest = jnp.maximum(highest, jnp.max(score, axis=0, keepdims=True))

    weight = jnp.exp2((own_score - highest) * scale)
    total = jnp.sum(weight, axis=0, keepdims=True)
    weight = weight.T.astype(jnp.bfloat16)
    mixed = [
        jnp.dot(
            weight[h * per_head : (h + 1) * per_head],
            own[:, (2 * h + 1) * HD : (2 * h + 2) * HD],
            preferred_element_type=jnp.float32,
        )
        for h in range(KVH)
    ]
    for first in range(0, total_pages, step):
        weight = jnp.exp2((scores[first * page : (first + step) * page, :] - highest) * scale)
        total = total + jnp.sum(weight, axis=0, keepdims=True)
        weight = weight.T.astype(jnp.bfloat16)
        for h in range(KVH):
            value = pool[first : first + step, :, (2 * h + 1) * HD : (2 * h + 2) * HD]
            mixed[h] = mixed[h] + jnp.dot(
                weight[h * per_head : (h + 1) * per_head],
                value.reshape(step * page, HD),
                preferred_element_type=jnp.float32,
            )
    for h in range(KVH):
        acc_ref[h] = mixed[h]
    state_ref[0:1, :] = highest
    state_ref[1:2, :] = total


def decode_old(pool, tables, lengths, slots, queries, new_kv):
    rows = tables.shape[0]
    columns = KVH * GROUP * rows
    total_pages, page, width = pool.shape
    vmem = pl.BlockSpec(memory_space=pltpu.VMEM)
    smem = pl.BlockSpec(memory_space=pltpu.SMEM)
    return pl.pallas_call(
        decode_old_kernel,
        out_shape=[
            jax.ShapeDtypeStruct((KVH, GROUP * rows, HD), jnp.float32),
            jax.ShapeDtypeStruct((2, columns), jnp.float32),
            jax.ShapeDtypeStruct((width, columns), jnp.bfloat16),
            jax.ShapeDtypeStruct((slots.shape[1] * page, columns), jnp.float32),
        ],
        in_specs=[smem, smem, smem, vmem, vmem, vmem],
        out_specs=[vmem] * 4,
        scratch_shapes=[
            pltpu.VMEM((total_pages, columns), jnp.int32),
            pltpu.VMEM((total_pages * page, columns), jnp.float32),
            pltpu.VMEM((page, width), jnp.bfloat16),
        ],
        compiler_params=pltpu.CompilerParams(vmem_limit_bytes=VMEM_LIMIT),
        cost_estimate=pl.CostEstimate(
            flops=4 * total_pages * page * width * columns,
            bytes_accessed=2 * total_pages * page * width,
            transcendentals=total_pages * page * columns,
        ),
        name="decode_old",
    )(tables, lengths, slots, queries, new_kv, pool)


def decode_new_kernel(heads_of, member, q_ref, allowed_ref, acc_ref, state_ref, *refs):
    pieces, out, weights, keeps = refs[:-3], *refs[-3:]
    scale = HD ** (-0.5) * LOG2E
    columns = q_ref.shape[1]
    per_head = columns // KVH
    rows = out.shape[0]
    heads = heads_of(member[0])
    score = jnp.zeros((pieces[0].shape[0], columns), jnp.float32)
    for k in range(KVH):
        where = pl.ds(pl.multiple_of(heads[k] * 2 * HD, 2 * HD), 2 * HD)
        score = score + jnp.dot(pieces[k][...], q_ref[where, :], preferred_element_type=jnp.float32)
    score = jnp.where(allowed_ref[...] > 0.0, score, MASKED)
    before = state_ref[0:1, :]
    highest = jnp.maximum(before, jnp.max(score, axis=0, keepdims=True))
    keep = jnp.exp2((before - highest) * scale)
    weight = jnp.exp2((score - highest) * scale)
    share = 1.0 / (state_ref[1:2, :] * keep + jnp.sum(weight, axis=0, keepdims=True))
    weights[...] = (weight * share).T
    keeps[...] = jnp.broadcast_to(keep * share, (8, columns)).T
    for k in range(KVH):
        h = heads[k]
        mine = pl.ds(pl.multiple_of(h * per_head, per_head), per_head)
        mixed = acc_ref[h] * keeps[mine, 0:1] + jnp.dot(
            weights[mine, :].astype(jnp.bfloat16),
            pieces[k][:, HD:],
            preferred_element_type=jnp.float32,
        )
        for j in range(GROUP):
            lanes = pl.ds(pl.multiple_of((h * GROUP + j) * HD, HD), HD)
            out[:, lanes] = mixed[j * rows : (j + 1) * rows, :].astype(jnp.bfloat16)


def decode_new(pieces, heads_of, member, rows, acc, state, queries, allowed):
    vmem = pl.BlockSpec(memory_space=pltpu.VMEM)
    columns = queries.shape[1]
    return pl.pallas_call(
        functools.partial(decode_new_kernel, heads_of),
        out_shape=jax.ShapeDtypeStruct((rows, KVH * GROUP * HD), jnp.bfloat16),
        in_specs=[pl.BlockSpec(memory_space=pltpu.SMEM)] + [vmem] * (4 + len(pieces)),
        out_specs=vmem,
        scratch_shapes=[
            pltpu.VMEM((columns, pieces[0].shape[0]), jnp.float32),
            pltpu.VMEM((columns, 8), jnp.float32),
        ],
        compiler_params=pltpu.CompilerParams(vmem_limit_bytes=VMEM_LIMIT),
        name="decode_new",
    )(member, queries, allowed, acc, state, *pieces)


def exchange_plan(members, subs):
    def pairs(links):
        return [
            (source * subs + sub, target * subs + sub)
            for source, target in links
            for sub in range(subs)
        ]

    side = [(m, m ^ 1) for m in range(members)]
    outer = [(m, m ^ 2) for m in range(members)]
    outward = [(m, m ^ 2) for m in range(members) if m // 2 in (1, 2)]
    inner = [(m, m ^ 6) for m in range(members) if m // 2 in (1, 2)]
    return pairs(side), pairs(outer), pairs(outward), pairs(inner)


def local(
    stretch_tokens,
    norm_gain,
    q_weight,
    kv_weight,
    dec_query,
    dec_new_kv,
    kv_pool,
    page_table,
    cache_lengths,
    handoff_slot,
):
    devices_tp = lax.axis_size("tp")
    members = min(16, devices_tp)
    subs = devices_tp // members
    sub_bits = subs.bit_length() - 1
    member_bits = members.bit_length() - 1
    headmates = members // KVH
    position = lax.axis_index("tp")
    member = position // subs
    tokens = stretch_tokens[0]
    block_rows, width = tokens.shape
    count = members * block_rows
    gain = norm_gain.reshape(1, width)

    member_ref = member.reshape(1).astype(jnp.int32)
    rows = page_table.shape[0]

    q_block = q_weight
    kv_block = kv_weight
    for bit in range(sub_bits):
        other_q = swapped(q_block, "tp", bit)
        other_kv = swapped(kv_block, "tp", bit)
        upper = position // 2**bit % 2
        q_block = ordered_pair(q_block, other_q, upper, 1)
        kv_block = ordered_pair(kv_block, other_kv, upper, 1)
    q_cos, q_sin = rotation_tables(count, HD, 0, False)
    kv_width = kv_block.shape[1]
    if kv_width % (2 * HD) == 0:
        kv_job = (kv_block, q_cos, q_sin, (True, False) * (kv_width // (2 * HD)), 1)
    else:
        kv_cos, kv_sin = rotation_tables(count, kv_width, member * kv_width, True)
        kv_job = (kv_block, kv_cos, kv_sin, (True,) * max(1, kv_width // HD), 1)
    q_job = (q_block, q_cos, q_sin, (True,) * (q_block.shape[1] // HD), 1)
    kv_pair = kv_job[:4] + (2,)
    bar = lax.optimization_barrier

    def old_state():
        return decode_old(
            kv_pool, page_table, cache_lengths, handoff_slot, dec_query, dec_new_kv
        )

    if members == 8 and headmates == 1 and block_rows % 32 == 0:
        half = block_rows // 2
        side, outer, outward, inner = exchange_plan(members, subs)

        def move(value, pairs):
            return lax.ppermute(value, "tp", pairs)

        row = member // 2
        at_end = (row == 0) | (row == 3)

        def place(offsets):
            return lambda m: [
                jnp.bitwise_xor(m, offset) * block_rows + c * half
                for offset in offsets
                for c in range(2)
            ]

        def hand(kv, offset):
            pairs = [
                (r * devices_tp + m * subs + s, (1 - r) * devices_tp + (m ^ offset) * subs + s)
                for r in range(2)
                for m in range(members)
                for s in range(subs)
            ]
            return lax.ppermute(kv, ("role", "tp"), pairs)

        own = [tokens[:half]]
        own.append(bar((tokens, own[0]))[0][half:])
        y, e1, e2 = {}, {}, {}
        for c in range(2):
            y[c] = move(own[c], side)
            e1[c] = move(own[c], outer)
            e2[c] = move(own[c], inner)
        state = old_state()
        q0, kv0 = project([tokens], lambda m: [m * block_rows], member_ref, gain, [q_job, kv_job])
        piece = {0: hand(kv0, 0)}
        for c in range(2):
            e1[c], e2[c], y[c] = bar((e1[c], e2[c], y[c]))
            e1[2 + c] = move(e2[c], outward)
            e2[2 + c] = move(e1[c], inner)
            y[2 + c] = move(e1[c], side)
        qa, kv2, kv1 = project(
            [e1[0], e1[1], y[0], y[1]], place((2, 1)), member_ref, gain, [q_job, kv_pair]
        )
        piece[2], piece[1] = hand(kv2, 2), hand(kv1, 1)
        two, three = {}, {}
        for c in range(2):
            e1[2 + c], e2[2 + c], y[2 + c] = bar((e1[2 + c], e2[2 + c], y[2 + c]))
            two[c] = jnp.where(at_end, e1[2 + c], e2[2 + c])
            e1[4 + c] = move(e2[2 + c], outward)
            y[4 + c] = move(two[c], side)
        qb, kv4, kv3 = project(
            [two[0], two[1], y[2], y[3]], place((4, 3)), member_ref, gain, [q_job, kv_pair]
        )
        piece[4], piece[3] = hand(kv4, 4), hand(kv3, 3)
        for c in range(2):
            e1[4 + c], y[4 + c] = bar((e1[4 + c], y[4 + c]))
            three[c] = jnp.where(at_end, e1[4 + c], e2[c])
            if c == 0:
                e1[6] = move(y[4], outer)
            else:
                y[6] = move(three[1], side)
        qc, kv6, kv5 = project(
            [three[0], three[1], y[4], y[5]], place((6, 5)), member_ref, gain, [q_job, kv_pair]
        )
        piece[6], piece[5] = hand(kv6, 6), hand(kv5, 5)
        last = [e1[6], y[6]]
        kv7, normed = project(last, place((7,)), member_ref, gain, [kv_job], keep=True)
        piece[7] = hand(kv7, 7)
        (qd,) = project(last, place((7,)), member_ref, gain, [q_job], ready=normed)
        context = attend(
            [q0, qa, qb, qc, qd],
            [kv0, kv2, kv1, kv4, kv3, kv6, kv5, kv7],
            [half] * (2 * members),
            place((0, 2, 1, 4, 3, 6, 5, 7)),
            member_ref,
        )
        pieces = [piece[k] for k in range(members)]
        heads_of = lambda m: [jnp.bitwise_xor(m, k) for k in range(members)]
    else:
        state = old_state()
        moving = tokens
        queries, local_kvs, order = [], [], []
        group, group_steps = [tokens], [0]
        for step in range(members):
            if step:
                moving = from_behind(moving, "tp", subs)
                group.append(moving)
                group_steps.append(step)
            if len(group) == min(4, members) or step == members - 1:
                place = lambda m, steps=tuple(group_steps): [
                    jnp.bitwise_and(m - back, members - 1) * block_rows for back in steps
                ]
                q_part, kv_part = project(group, place, member_ref, gain, [q_job, kv_job])
                queries.append(q_part)
                local_kvs.append(kv_part)
                order += [(member - back) % members for back in group_steps]
                group, group_steps = [], []
        arrived_kv = jnp.concatenate(local_kvs, axis=0).reshape(members, block_rows, kv_width)
        local_kv = arrived_kv[jnp.argsort(jnp.stack(order))].reshape(count, kv_width)
        head_kv = local_kv
        for step in range(headmates.bit_length() - 1):
            other = swapped(head_kv, "tp", sub_bits + step)
            head_kv = ordered_pair(head_kv, other, member // 2**step % 2, 1)
        arrived_q = jnp.concatenate(queries, axis=0).reshape(members, block_rows, -1)
        all_q = arrived_q[jnp.argsort(jnp.stack(order))].reshape(count, -1)
        context = attend([all_q], [head_kv], [count], lambda m: [0], member_ref)
        crossed = swapped(local_kv, "role", 0)
        received = spread_members(
            crossed.reshape(members, block_rows, kv_width),
            member,
            sub_bits,
            member_bits,
            lambda part, bit: swapped(part, "tp", bit),
        )
        arrived = jnp.transpose(received, (1, 0, 2)).reshape(block_rows, members * kv_width)
        pieces = [arrived[:, k * 2 * HD : (k + 1) * 2 * HD] for k in range(KVH)]
        heads_of = lambda m: list(range(KVH))

    decoded = decode_new(pieces, heads_of, member_ref, rows, *state)
    return (context[None], decoded)


def solution(mesh):
    in_specs = (
        P("role", ("grp", "tp"), None),
        P(),
        P(None, "tp"),
        P(None, "tp"),
        P(("grp", "role", "tp"), None),
        P(("grp", "role", "tp"), None),
        P(("grp", "role", "tp"), None, None),
        P(("grp", "role", "tp"), None),
        P(("grp", "role", "tp")),
        P(("grp", "role", "tp"), None),
    )
    out_specs = (P("role", "grp", "tp"), P(("grp", "role", "tp"), None))
    return jax.shard_map(local, mesh=mesh, in_specs=in_specs, out_specs=out_specs, check_vma=False)
```

profile of v0, /device:TPU:0, one launch (start us, length us, event | category | flops | bytes accessed | tf_op | source)
XLA Modules:
  0.0 124.9 jit_solution(4837512844205859761)
XLA Ops:
  0.6 1.1 slice_bitcast_fusion
  1.7 3.1 %collective-permute-start = (bf16[32,8192]{1,0:T(8,128)(2,1)S(1)}, bf16[32,8192]{1,0:T(8,128)(2,1)S(1)}, u32[]{:S(2)}, u32[]{:S(2)}) collective-permute-start(bf16[32,8192]{1,0:T(8,128)(2,1)S(1)} %slice_bitcast_fusion), channel_id=1, source_target_pairs={{0,2},{1,3},{2,0},{3,1},{4,6},{5,7},{6,4},{7,5},{8,10},{9,11},{10,... | collective-permute-start | bytes 1572872 | tf_op jit(solution)/shard_map/ppermute | solution.py:524
  4.8 0.7 collective-permute-start.1
  5.5 1.6 %collective-permute-start.2 = (bf16[32,8192]{1,0:T(8,128)(2,1)S(1)}, bf16[32,8192]{1,0:T(8,128)(2,1)S(1)}, u32[]{:S(2)}, u32[]{:S(2)}) collective-permute-start(bf16[32,8192]{1,0:T(8,128)(2,1)S(1)} %slice_bitcast_fusion), channel_id=1, source_target_pairs={{0,1},{1,0},{2,3},{3,2},{4,5},{5,4},{6,7},{7,6},{8,9},{9,8},{10,11... | collective-permute-start | bytes 1572872 | tf_op jit(solution)/shard_map/ppermute | solution.py:524
  7.1 1.1 slice.11
  8.2 4.4 %collective-permute-start.3 = (bf16[32,8192]{1,0:T(8,128)(2,1)S(1)}, bf16[32,8192]{1,0:T(8,128)(2,1)S(1)}, u32[]{:S(2)}, u32[]{:S(2)}) collective-permute-start(bf16[32,8192]{1,0:T(8,128)(2,1)S(1)} %slice.11), channel_id=1, source_target_pairs={{0,2},{1,3},{2,0},{3,1},{4,6},{5,7},{6,4},{7,5},{8,10},{9,11},{10,... | collective-permute-start | bytes 1572872 | tf_op jit(solution)/shard_map/ppermute | solution.py:524
  12.6 1.5 %collective-permute-start.4 = (bf16[32,8192]{1,0:T(8,128)(2,1)S(1)}, bf16[32,8192]{1,0:T(8,128)(2,1)}, u32[]{:S(2)}, u32[]{:S(2)}) collective-permute-start(bf16[32,8192]{1,0:T(8,128)(2,1)S(1)} %slice.11), channel_id=1, source_target_pairs={{2,4},{3,5},{4,2},{5,3},{10,12},{11,13},{12,10},{13,11},{18,20},{1... | collective-permute-start | bytes 1572872 | tf_op jit(solution)/shard_map/ppermute | solution.py:524
  14.1 3.5 %collective-permute-done.refs_0_ = bf16[32,8192]{1,0:T(8,128)(2,1)S(1)} collective-permute-done((bf16[32,8192]{1,0:T(8,128)(2,1)S(1)}, bf16[32,8192]{1,0:T(8,128)(2,1)S(1)}, u32[]{:S(2)}, u32[]{:S(2)}) %collective-permute-start) | collective-permute-done | bytes 524320 | tf_op jit(solution)/shard_map/ppermute | solution.py:524
  17.6 2.0 %collective-permute-start.5 = (bf16[32,8192]{1,0:T(8,128)(2,1)S(1)}, bf16[32,8192]{1,0:T(8,128)(2,1)S(1)}, u32[]{:S(2)}, u32[]{:S(2)}) collective-permute-start(bf16[32,8192]{1,0:T(8,128)(2,1)S(1)} %slice.11), channel_id=1, source_target_pairs={{0,1},{1,0},{2,3},{3,2},{4,5},{5,4},{6,7},{7,6},{8,9},{9,8},{10,11... | collective-permute-start | bytes 1572872 | tf_op jit(solution)/shard_map/ppermute | solution.py:524
  19.6 0.0 collective-permute-done.1
  19.6 0.0 collective-permute-done.2.refs_2_
  19.6 1.3 %collective-permute-start.6 = (bf16[32,8192]{1,0:T(8,128)(2,1)S(1)}, bf16[32,8192]{1,0:T(8,128)(2,1)S(1)}, u32[]{:S(2)}, u32[]{:S(2)}) collective-permute-start(bf16[32,8192]{1,0:T(8,128)(2,1)S(1)} %collective-permute-done.1), channel_id=1, source_target_pairs={{2,0},{3,1},{4,6},{5,7},{10,8},{11,9},{12,14},{13,15},{18,16},{19,... | collective-permute-start | bytes 1572872 | tf_op jit(solution)/shard_map/ppermute | solution.py:524
  20.9 1.5 %collective-permute-start.7 = (bf16[32,8192]{1,0:T(8,128)(2,1)S(1)}, bf16[32,8192]{1,0:T(8,128)(2,1)}, u32[]{:S(2)}, u32[]{:S(2)}) collective-permute-start(bf16[32,8192]{1,0:T(8,128)(2,1)S(1)} %collective-permute-done.refs_0_), channel_id=1, source_target_pairs={{2,4},{3,5},{4,2},{5,3},{10,12},{11,13},{12,10},{13,11},{18,20},{1... | collective-permute-start | bytes 1572872 | tf_op jit(solution)/shard_map/ppermute | solution.py:524
  22.4 6.5 %collective-permute-done.3.refs_1_ = bf16[32,8192]{1,0:T(8,128)(2,1)S(1)} collective-permute-done((bf16[32,8192]{1,0:T(8,128)(2,1)S(1)}, bf16[32,8192]{1,0:T(8,128)(2,1)S(1)}, u32[]{:S(2)}, u32[]{:S(2)}) %collective-permute-start.3) | collective-permute-done | bytes 524320 | tf_op jit(solution)/shard_map/ppermute | solution.py:524
  28.8 2.0 %collective-permute-start.8 = (bf16[32,8192]{1,0:T(8,128)(2,1)S(1)}, bf16[32,8192]{1,0:T(8,128)(2,1)S(1)}, u32[]{:S(2)}, u32[]{:S(2)}) collective-permute-start(bf16[32,8192]{1,0:T(8,128)(2,1)S(1)} %collective-permute-done.refs_0_), channel_id=1, source_target_pairs={{0,1},{1,0},{2,3},{3,2},{4,5},{5,4},{6,7},{7,6},{8,9},{9,8},{10,11... | collective-permute-start | bytes 1572872 | tf_op jit(solution)/shard_map/ppermute | solution.py:524
  30.8 1.5 %collective-permute-start.10 = (bf16[32,8192]{1,0:T(8,128)(2,1)S(1)}, bf16[32,8192]{1,0:T(8,128)(2,1)}, u32[]{:S(2)}, u32[]{:S(2)}) collective-permute-start(bf16[32,8192]{1,0:T(8,128)(2,1)S(1)} %collective-permute-done.3.refs_1_), channel_id=1, source_target_pairs={{2,4},{3,5},{4,2},{5,3},{10,12},{11,13},{12,10},{13,11},{18,20},{1... | collective-permute-start | bytes 1572872 | tf_op jit(solution)/shard_map/ppermute | solution.py:524
  32.3 1.4 %collective-permute-start.11 = (bf16[32,8192]{1,0:T(8,128)(2,1)S(1)}, bf16[32,8192]{1,0:T(8,128)(2,1)S(1)}, u32[]{:S(2)}, u32[]{:S(2)}) collective-permute-start(bf16[32,8192]{1,0:T(8,128)(2,1)S(1)} %collective-permute-done.3.refs_1_), channel_id=1, source_target_pairs={{0,1},{1,0},{2,3},{3,2},{4,5},{5,4},{6,7},{7,6},{8,9},{9,8},{10,11... | collective-permute-start | bytes 1572872 | tf_op jit(solution)/shard_map/ppermute | solution.py:524
  33.6 5.6 %collective-permute-done.6 = bf16[32,8192]{1,0:T(8,128)(2,1)S(1)} collective-permute-done((bf16[32,8192]{1,0:T(8,128)(2,1)S(1)}, bf16[32,8192]{1,0:T(8,128)(2,1)S(1)}, u32[]{:S(2)}, u32[]{:S(2)}) %collective-permute-start.6) | collective-permute-done | bytes 524320 | tf_op jit(solution)/shard_map/ppermute | solution.py:524
  39.2 0.8 copy-done.12
  40.0 1.3 %collective-permute-start.9 = (bf16[32,8192]{1,0:T(8,128)(2,1)}, bf16[32,8192]{1,0:T(8,128)(2,1)}, u32[]{:S(2)}, u32[]{:S(2)}) collective-permute-start(bf16[32,8192]{1,0:T(8,128)(2,1)} %collective-permute-done.4), channel_id=1, source_target_pairs={{2,0},{3,1},{4,6},{5,7},{10,8},{11,9},{12,14},{13,15},{18,16},{19,... | collective-permute-start | bytes 1572872 | tf_op jit(solution)/shard_map/ppermute | solution.py:524
  41.3 0.7 reshape.56.refs_1_.refs_4_.refs_2_
  42.1 1.0 fusion
  43.1 0.0 copy-start
  43.1 5.8 %copy-done = bf16[8192,1024]{1,0:T(8,128)(2,1)S(1)} copy-done((bf16[8192,1024]{1,0:T(8,128)(2,1)S(1)}, bf16[8192,1024]{1,0:T(8,128)(2,1)}, u32[]{:S(2)}) %copy-start) | copy-done | bytes 16777240
  48.9 2.2 %copy-done.1 = bf16[8192,256]{1,0:T(8,128)(2,1)S(1)} copy-done((bf16[8192,256]{1,0:T(8,128)(2,1)S(1)}, bf16[8192,256]{1,0:T(8,128)(2,1)}, u32[]{:S(2)}) %copy-start.1) | copy-done | bytes 4194328
  51.1 1.2 copy-done.3
  52.3 0.0 copy-start.7
  52.3 0.0 copy-start.8
  52.3 0.0 copy-start.9
  52.4 4.6 %project.6 = (bf16[64,1024]{1,0:T(8,128)(2,1)S(1)}, bf16[64,256]{1,0:T(8,128)(2,1)S(1)}) custom-call(s32[1]{0:T(128)} %bitcast.member, bf16[64,8192]{1,0:T(8,128)(2,1)S(1)} %bitcast.8, bf16[1,8192]{1,0:T(2,128)(2,1)S(1)} %reshape.56.refs_1_.refs_4_.refs_2_, bf16[8192,1024]{1,0:T(8,128)(2,1)S(1)} %copy-done, ...), custom_call_target="tpu_custom_call" | custom-call | flops 1342177280 | bytes 22020096 | tf_op jit(solution)/shard_map/project/pallas_call | solution.py:165
  57.0 0.1 collective-permute-start.18
  57.1 1.6 %collective-permute-start.12 = (bf16[32,8192]{1,0:T(8,128)(2,1)}, bf16[32,8192]{1,0:T(8,128)(2,1)S(1)}, u32[]{:S(2)}, u32[]{:S(2)}) collective-permute-start(bf16[32,8192]{1,0:T(8,128)(2,1)} %collective-permute-done.7), channel_id=1, source_target_pairs={{2,0},{3,1},{4,6},{5,7},{10,8},{11,9},{12,14},{13,15},{18,16},{19,... | collective-permute-start | bytes 1572872 | tf_op jit(solution)/shard_map/ppermute | solution.py:524
  58.6 1.5 %collective-permute-start.14 = (bf16[32,8192]{1,0:T(8,128)(2,1)}, bf16[32,8192]{1,0:T(8,128)(2,1)S(1)}, u32[]{:S(2)}, u32[]{:S(2)}) collective-permute-start(bf16[32,8192]{1,0:T(8,128)(2,1)} %collective-permute-done.10), channel_id=1, source_target_pairs={{2,0},{3,1},{4,6},{5,7},{10,8},{11,9},{12,14},{13,15},{18,16},{19,... | collective-permute-start | bytes 1572872 | tf_op jit(solution)/shard_map/ppermute | solution.py:524
  60.1 0.1 broadcast_select_fusion.3.refs_0_
  60.2 1.1 broadcast_select_fusion.2.refs_1_
  61.3 0.0 slice-start.3
  61.3 0.0 copy-start.2
  61.4 1.7 %collective-permute-start.13 = (bf16[32,8192]{1,0:T(8,128)(2,1)S(1)}, bf16[32,8192]{1,0:T(8,128)(2,1)S(1)}, u32[]{:S(2)}, u32[]{:S(2)}) collective-permute-start(bf16[32,8192]{1,0:T(8,128)(2,1)S(1)} %broadcast_select_fusion.3.refs_0_), channel_id=1, source_target_pairs={{0,1},{1,0},{2,3},{3,2},{4,5},{5,4},{6,7},{7,6},{8,9},{9,8},{10,11... | collective-permute-start | bytes 1572872 | tf_op jit(solution)/shard_map/ppermute | solution.py:524
  63.1 0.3 collective-permute-start.15
  63.5 4.8 %decode_old.1 = (f32[8,32,128]{2,1,0:T(8,128)S(1)}, f32[2,256]{1,0:T(2,128)S(1)}, bf16[2048,256]{1,0:T(8,128)(2,1)S(1)}, f32[64,256]{1,0:T(8,128)S(1)}) custom-call(s32[4,24]{1,0:T(4,128)S(1)} %copy-done.7, s32[4]{0:T(128)S(1)} %copy-done.8, s32[1,4]{1,0:T(1,128)S(1)} %copy-done.9, bf16[4,8192]{1,0:T(4,128)(2,1)S(1)} %copy-done.5, ...), custom_call_target="tpu_custom_call" | custom-call | flops 3221225472 | bytes 6291456 | tf_op jit(solution)/shard_map/decode_old/pallas_call | solution.py:378
  68.3 0.0 slice-done.1
  68.3 4.9 %project.7 = (bf16[128,1024]{1,0:T(8,128)(2,1)S(1)}, bf16[64,256]{1,0:T(8,128)(2,1)S(1)}, bf16[64,256]{1,0:T(8,128)(2,1)S(1)}) custom-call(s32[1]{0:T(128)} %bitcast.member, bf16[32,8192]{1,0:T(8,128)(2,1)S(1)} %collective-permute-done.refs_0_, bf16[32,8192]{1,0:T(8,128)(2,1)S(1)} %collective-permute-done.3.refs_1_, ...), custom_call_target="tpu_custom_call" | custom-call | flops 2684354560 | bytes 23068672 | tf_op jit(solution)/shard_map/project/pallas_call | solution.py:165
  73.2 4.9 %project.8 = (bf16[128,1024]{1,0:T(8,128)(2,1)S(1)}, bf16[64,256]{1,0:T(8,128)(2,1)S(1)}, bf16[64,256]{1,0:T(8,128)(2,1)S(1)}) custom-call(s32[1]{0:T(128)} %bitcast.member, bf16[32,8192]{1,0:T(8,128)(2,1)S(1)} %broadcast_select_fusion.3.refs_0_, bf16[32,8192]{1,0:T(8,128)(2,1)S(1)} %broadcast_select_fusion.2.refs_1_, ...), custom_call_target="tpu_custom_call" | custom-call | flops 2684354560 | bytes 23068672 | tf_op jit(solution)/shard_map/project/pallas_call | solution.py:165
  78.1 1.0 collective-permute-start.19
  79.1 5.0 %collective-permute-start.20 = (bf16[64,256]{1,0:T(8,128)(2,1)S(1)}, bf16[64,256]{1,0:T(8,128)(2,1)S(1)}, u32[]{:S(2)}, u32[]{:S(2)}) collective-permute-start(bf16[64,256]{1,0:T(8,128)(2,1)S(1)} %get-tuple-element.59.refs_6_), channel_id=1, source_target_pairs={{0,10},{1,11},{2,8},{3,9},{4,14},{5,15},{6,12},{7,13},{8,2},{9,3},... | collective-permute-start | bytes 98312 | tf_op jit(solution)/shard_map/ppermute | solution.py:543
  84.1 2.0 %collective-permute-done.14 = bf16[32,8192]{1,0:T(8,128)(2,1)S(1)} collective-permute-done((bf16[32,8192]{1,0:T(8,128)(2,1)}, bf16[32,8192]{1,0:T(8,128)(2,1)S(1)}, u32[]{:S(2)}, u32[]{:S(2)}) %collective-permute-start.14) | collective-permute-done | bytes 524320 | tf_op jit(solution)/shard_map/ppermute | solution.py:524
  86.1 0.9 collective-permute-done.15.refs_3_
  87.0 0.1 broadcast_select_fusion.refs_1_
  87.1 5.6 %collective-permute-start.16 = (bf16[32,8192]{1,0:T(8,128)(2,1)S(1)}, bf16[32,8192]{1,0:T(8,128)(2,1)S(1)}, u32[]{:S(2)}, u32[]{:S(2)}) collective-permute-start(bf16[32,8192]{1,0:T(8,128)(2,1)S(1)} %collective-permute-done.13.refs_2_), channel_id=1, source_target_pairs={{0,2},{1,3},{2,0},{3,1},{4,6},{5,7},{6,4},{7,5},{8,10},{9,11},{10,... | collective-permute-start | bytes 1572872 | tf_op jit(solution)/shard_map/ppermute | solution.py:524
  92.7 1.7 %collective-permute-start.17 = (bf16[32,8192]{1,0:T(8,128)(2,1)S(1)}, bf16[32,8192]{1,0:T(8,128)(2,1)S(1)}, u32[]{:S(2)}, u32[]{:S(2)}) collective-permute-start(bf16[32,8192]{1,0:T(8,128)(2,1)S(1)} %broadcast_select_fusion.refs_1_), channel_id=1, source_target_pairs={{0,1},{1,0},{2,3},{3,2},{4,5},{5,4},{6,7},{7,6},{8,9},{9,8},{10,11... | collective-permute-start | bytes 1572872 | tf_op jit(solution)/shard_map/ppermute | solution.py:524
  94.4 0.1 broadcast_select_fusion.1.refs_0_
  94.5 5.1 %project.9 = (bf16[128,1024]{1,0:T(8,128)(2,1)S(1)}, bf16[64,256]{1,0:T(8,128)(2,1)S(1)}, bf16[64,256]{1,0:T(8,128)(2,1)S(1)}) custom-call(s32[1]{0:T(128)} %bitcast.member, bf16[32,8192]{1,0:T(8,128)(2,1)S(1)} %broadcast_select_fusion.1.refs_0_, bf16[32,8192]{1,0:T(8,128)(2,1)S(1)} %broadcast_select_fusion.refs_1_, ...), custom_call_target="tpu_custom_call" | custom-call | flops 2684354560 | bytes 23068672 | tf_op jit(solution)/shard_map/project/pallas_call | solution.py:165
  99.6 4.3 %collective-permute-done.16.refs_0_ = bf16[32,8192]{1,0:T(8,128)(2,1)S(1)} collective-permute-done((bf16[32,8192]{1,0:T(8,128)(2,1)S(1)}, bf16[32,8192]{1,0:T(8,128)(2,1)S(1)}, u32[]{:S(2)}, u32[]{:S(2)}) %collective-permute-start.16) | collective-permute-done | bytes 524320 | tf_op jit(solution)/shard_map/ppermute | solution.py:524
  103.8 0.6 collective-permute-start.21
  104.4 0.8 collective-permute-done.17.refs_1_
  105.3 3.5 %collective-permute-start.22 = (bf16[64,256]{1,0:T(8,128)(2,1)S(1)}, bf16[64,256]{1,0:T(8,128)(2,1)S(1)}, u32[]{:S(2)}, u32[]{:S(2)}) collective-permute-start(bf16[64,256]{1,0:T(8,128)(2,1)S(1)} %get-tuple-element.61.refs_8_), channel_id=1, source_target_pairs={{0,12},{1,13},{2,14},{3,15},{4,8},{5,9},{6,10},{7,11},{8,4},{9,5},... | collective-permute-start | bytes 98312 | tf_op jit(solution)/shard_map/ppermute | solution.py:543
  108.8 1.6 %project.10 = (bf16[64,256]{1,0:T(8,128)(2,1)S(1)}, bf16[64,8192]{1,0:T(8,128)(2,1)S(1)}) custom-call(s32[1]{0:T(128)} %bitcast.member, bf16[32,8192]{1,0:T(8,128)(2,1)S(1)} %collective-permute-done.16.refs_0_, bf16[32,8192]{1,0:T(8,128)(2,1)S(1)} %collective-permute-done.17.refs_1_, bf16[1,8192]{1,0:T(2,128)(2,1)S(1)} %reshape.56.refs_1_.refs_4_.refs_2_, ...), custom_call_target="tpu_custom_call" | custom-call | flops 268435456 | bytes 5242880 | tf_op jit(solution)/shard_map/project/pallas_call | solution.py:165
  110.5 3.2 %project.11.refs_4_ = bf16[64,1024]{1,0:T(8,128)(2,1)S(1)} custom-call(s32[1]{0:T(128)} %bitcast.member, bf16[64,8192]{1,0:T(8,128)(2,1)S(1)} %get-tuple-element.57.refs_0_, bf16[1,8192]{1,0:T(2,128)(2,1)S(1)} %reshape.56.refs_1_.refs_4_.refs_2_, bf16[8192,1024]{1,0:T(8,128)(2,1)S(1)} %bitcast.6, ...), custom_call_target="tpu_custom_call" | custom-call | flops 1073741824 | bytes 17825792 | tf_op jit(solution)/shard_map/project/pallas_call | solution.py:165
  113.7 0.3 collective-permute-start.23
  113.9 3.6 %collective-permute-start.24 = (bf16[64,256]{1,0:T(8,128)(2,1)S(1)}, bf16[64,256]{1,0:T(8,128)(2,1)S(1)}, u32[]{:S(2)}, u32[]{:S(2)}) collective-permute-start(bf16[64,256]{1,0:T(8,128)(2,1)S(1)} %get-tuple-element.63.refs_10_), channel_id=1, source_target_pairs={{0,14},{1,15},{2,12},{3,13},{4,10},{5,11},{6,8},{7,9},{8,6},{9,7},... | collective-permute-start | bytes 98312 | tf_op jit(solution)/shard_map/ppermute | solution.py:543
  117.5 1.0 collective-permute-start.25
  118.5 3.7 %attend.1 = bf16[512,1024]{1,0:T(8,128)(2,1)} custom-call(s32[1]{0:T(128)} %bitcast.member, bf16[64,1024]{1,0:T(8,128)(2,1)S(1)} %get-tuple-element.36.refs_0_, bf16[128,1024]{1,0:T(8,128)(2,1)S(1)} %get-tuple-element.42.refs_1_, bf16[128,1024]{1,0:T(8,128)(2,1)S(1)} %get-tuple-element.51.refs_2_, bf16[128,1024]{1,0:T(8,128)(2,1)S(1)} %get-tuple-element.56.refs_3_, ...), custom_call_target="tpu_custom_call" | custom-call | flops 536870912 | bytes 2621440 | tf_op jit(solution)/shard_map/attend/pallas_call | solution.py:247
  122.2 1.3 %collective-permute-done.25.refs_7_ = bf16[64,256]{1,0:T(8,128)(2,1)S(1)} collective-permute-done((bf16[64,256]{1,0:T(8,128)(2,1)S(1)}, bf16[64,256]{1,0:T(8,128)(2,1)S(1)}, u32[]{:S(2)}, u32[]{:S(2)}) %collective-permute-start.25) | collective-permute-done | bytes 32800 | tf_op jit(solution)/shard_map/ppermute | solution.py:543
  123.5 1.3 %decode_new.1 = bf16[4,8192]{1,0:T(4,128)(2,1)} custom-call(s32[1]{0:T(128)} %bitcast.member, bf16[2048,256]{1,0:T(8,128)(2,1)S(1)} %get-tuple-element.66.q_ref, f32[64,256]{1,0:T(8,128)S(1)} %get-tuple-element.67.allowed_ref, f32[8,32,128]{2,1,0:T(8,128)S(1)} %get-tuple-element.68.acc_ref, f32[2,256]{1,0:T(2,128)S(1)} %get-tuple-element.69.state_ref, ...), custom_call_target="tpu_custom_call" | custom-call | tf_op jit(solution)/shard_map/decode_new/pallas_call | solution.py:438
  (44 shorter events, 0.1 us)
Async XLA Ops:
  1.7 15.9 %collective-permute-start = (bf16[32,8192]{1,0:T(8,128)(2,1)S(1)}, bf16[32,8192]{1,0:T(8,128)(2,1)S(1)}, u32[]{:S(2)}, u32[]{:S(2)}) collective-permute-start(bf16[32,8192]{1,0:T(8,128)(2,1)S(1)} %slice_bitcast_fusion), channel_id=1, source_target_pairs={{0,2},{1,3},{2,0},{3,1},{4,6},{5,7},{6,4},{7,5},{8,10},{9,11},{10,... | collective-permute-start | bytes 1572872 | tf_op jit(solution)/shard_map/ppermute | solution.py:524
  4.8 14.7 %collective-permute-start.1 = (bf16[32,8192]{1,0:T(8,128)(2,1)S(1)}, bf16[32,8192]{1,0:T(8,128)(2,1)S(1)}, u32[]{:S(2)}, u32[]{:S(2)}) collective-permute-start(bf16[32,8192]{1,0:T(8,128)(2,1)S(1)} %slice_bitcast_fusion), channel_id=1, source_target_pairs={{2,4},{3,5},{4,2},{5,3},{10,12},{11,13},{12,10},{13,11},{18,20},{1... | collective-permute-start | bytes 1572872 | tf_op jit(solution)/shard_map/ppermute | solution.py:524
  5.5 14.1 %collective-permute-start.2 = (bf16[32,8192]{1,0:T(8,128)(2,1)S(1)}, bf16[32,8192]{1,0:T(8,128)(2,1)S(1)}, u32[]{:S(2)}, u32[]{:S(2)}) collective-permute-start(bf16[32,8192]{1,0:T(8,128)(2,1)S(1)} %slice_bitcast_fusion), channel_id=1, source_target_pairs={{0,1},{1,0},{2,3},{3,2},{4,5},{5,4},{6,7},{7,6},{8,9},{9,8},{10,11... | collective-permute-start | bytes 1572872 | tf_op jit(solution)/shard_map/ppermute | solution.py:524
  8.2 20.7 %collective-permute-start.3 = (bf16[32,8192]{1,0:T(8,128)(2,1)S(1)}, bf16[32,8192]{1,0:T(8,128)(2,1)S(1)}, u32[]{:S(2)}, u32[]{:S(2)}) collective-permute-start(bf16[32,8192]{1,0:T(8,128)(2,1)S(1)} %slice.11), channel_id=1, source_target_pairs={{0,2},{1,3},{2,0},{3,1},{4,6},{5,7},{6,4},{7,5},{8,10},{9,11},{10,... | collective-permute-start | bytes 1572872 | tf_op jit(solution)/shard_map/ppermute | solution.py:524
  12.6 18.2 %collective-permute-start.4 = (bf16[32,8192]{1,0:T(8,128)(2,1)S(1)}, bf16[32,8192]{1,0:T(8,128)(2,1)}, u32[]{:S(2)}, u32[]{:S(2)}) collective-permute-start(bf16[32,8192]{1,0:T(8,128)(2,1)S(1)} %slice.11), channel_id=1, source_target_pairs={{2,4},{3,5},{4,2},{5,3},{10,12},{11,13},{12,10},{13,11},{18,20},{1... | collective-permute-start | bytes 1572872 | tf_op jit(solution)/shard_map/ppermute | solution.py:524
  17.6 13.2 %collective-permute-start.5 = (bf16[32,8192]{1,0:T(8,128)(2,1)S(1)}, bf16[32,8192]{1,0:T(8,128)(2,1)S(1)}, u32[]{:S(2)}, u32[]{:S(2)}) collective-permute-start(bf16[32,8192]{1,0:T(8,128)(2,1)S(1)} %slice.11), channel_id=1, source_target_pairs={{0,1},{1,0},{2,3},{3,2},{4,5},{5,4},{6,7},{7,6},{8,9},{9,8},{10,11... | collective-permute-start | bytes 1572872 | tf_op jit(solution)/shard_map/ppermute | solution.py:524
  19.6 11.2 %copy-start.10 = (bf16[32,8192]{1,0:T(8,128)(2,1)}, bf16[32,8192]{1,0:T(8,128)(2,1)S(1)}, u32[]{:S(2)}) copy-start(bf16[32,8192]{1,0:T(8,128)(2,1)S(1)} %collective-permute-done.1) | copy-start | bytes 1572868
  19.6 19.6 %collective-permute-start.6 = (bf16[32,8192]{1,0:T(8,128)(2,1)S(1)}, bf16[32,8192]{1,0:T(8,128)(2,1)S(1)}, u32[]{:S(2)}, u32[]{:S(2)}) collective-permute-start(bf16[32,8192]{1,0:T(8,128)(2,1)S(1)} %collective-permute-done.1), channel_id=1, source_target_pairs={{2,0},{3,1},{4,6},{5,7},{10,8},{11,9},{12,14},{13,15},{18,16},{19,... | collective-permute-start | bytes 1572872 | tf_op jit(solution)/shard_map/ppermute | solution.py:524
  20.9 36.1 %collective-permute-start.7 = (bf16[32,8192]{1,0:T(8,128)(2,1)S(1)}, bf16[32,8192]{1,0:T(8,128)(2,1)}, u32[]{:S(2)}, u32[]{:S(2)}) collective-permute-start(bf16[32,8192]{1,0:T(8,128)(2,1)S(1)} %collective-permute-done.refs_0_), channel_id=1, source_target_pairs={{2,4},{3,5},{4,2},{5,3},{10,12},{11,13},{12,10},{13,11},{18,20},{1... | collective-permute-start | bytes 1572872 | tf_op jit(solution)/shard_map/ppermute | solution.py:524
  28.8 28.2 %collective-permute-start.8 = (bf16[32,8192]{1,0:T(8,128)(2,1)S(1)}, bf16[32,8192]{1,0:T(8,128)(2,1)S(1)}, u32[]{:S(2)}, u32[]{:S(2)}) collective-permute-start(bf16[32,8192]{1,0:T(8,128)(2,1)S(1)} %collective-permute-done.refs_0_), channel_id=1, source_target_pairs={{0,1},{1,0},{2,3},{3,2},{4,5},{5,4},{6,7},{7,6},{8,9},{9,8},{10,11... | collective-permute-start | bytes 1572872 | tf_op jit(solution)/shard_map/ppermute | solution.py:524
  30.8 26.3 %collective-permute-start.10 = (bf16[32,8192]{1,0:T(8,128)(2,1)S(1)}, bf16[32,8192]{1,0:T(8,128)(2,1)}, u32[]{:S(2)}, u32[]{:S(2)}) collective-permute-start(bf16[32,8192]{1,0:T(8,128)(2,1)S(1)} %collective-permute-done.3.refs_1_), channel_id=1, source_target_pairs={{2,4},{3,5},{4,2},{5,3},{10,12},{11,13},{12,10},{13,11},{18,20},{1... | collective-permute-start | bytes 1572872 | tf_op jit(solution)/shard_map/ppermute | solution.py:524
  32.3 24.8 %collective-permute-start.11 = (bf16[32,8192]{1,0:T(8,128)(2,1)S(1)}, bf16[32,8192]{1,0:T(8,128)(2,1)S(1)}, u32[]{:S(2)}, u32[]{:S(2)}) collective-permute-start(bf16[32,8192]{1,0:T(8,128)(2,1)S(1)} %collective-permute-done.3.refs_1_), channel_id=1, source_target_pairs={{0,1},{1,0},{2,3},{3,2},{4,5},{5,4},{6,7},{7,6},{8,9},{9,8},{10,11... | collective-permute-start | bytes 1572872 | tf_op jit(solution)/shard_map/ppermute | solution.py:524
  39.2 0.8 copy-start.12
  40.0 17.0 %collective-permute-start.9 = (bf16[32,8192]{1,0:T(8,128)(2,1)}, bf16[32,8192]{1,0:T(8,128)(2,1)}, u32[]{:S(2)}, u32[]{:S(2)}) collective-permute-start(bf16[32,8192]{1,0:T(8,128)(2,1)} %collective-permute-done.4), channel_id=1, source_target_pairs={{2,0},{3,1},{4,6},{5,7},{10,8},{11,9},{12,14},{13,15},{18,16},{19,... | collective-permute-start | bytes 1572872 | tf_op jit(solution)/shard_map/ppermute | solution.py:524
  43.1 5.8 %copy-start = (bf16[8192,1024]{1,0:T(8,128)(2,1)S(1)}, bf16[8192,1024]{1,0:T(8,128)(2,1)}, u32[]{:S(2)}) copy-start(bf16[8192,1024]{1,0:T(8,128)(2,1)} %refs_2_.3) | copy-start | bytes 50331652
  48.9 2.2 %copy-start.1 = (bf16[8192,256]{1,0:T(8,128)(2,1)S(1)}, bf16[8192,256]{1,0:T(8,128)(2,1)}, u32[]{:S(2)}) copy-start(bf16[8192,256]{1,0:T(8,128)(2,1)} %refs_3_.1) | copy-start | bytes 12582916
  51.1 1.2 copy-start.3
  52.3 7.8 %copy-start.13 = (bf16[32,8192]{1,0:T(8,128)(2,1)S(1)}, bf16[32,8192]{1,0:T(8,128)(2,1)}, u32[]{:S(2)}) copy-start(bf16[32,8192]{1,0:T(8,128)(2,1)} %copy-done.12) | copy-start | bytes 1572868
  52.3 11.2 %copy-start.4 = (bf16[96,16,2048]{2,1,0:T(8,128)(2,1)S(1)}, bf16[96,16,2048]{2,1,0:T(8,128)(2,1)}, u32[]{:S(2)}) copy-start(bf16[96,16,2048]{2,1,0:T(8,128)(2,1)} %pool.1) | copy-start | bytes 18874372
  52.3 11.2 %copy-start.5 = (bf16[4,8192]{1,0:T(4,128)(2,1)S(1)}, bf16[4,8192]{1,0:T(4,128)(2,1)}, u32[]{:S(2)}) copy-start(bf16[4,8192]{1,0:T(4,128)(2,1)} %query_ref.1) | copy-start | bytes 196612
  52.3 11.2 %copy-start.6 = (bf16[4,2048]{1,0:T(4,128)(2,1)S(1)}, bf16[4,2048]{1,0:T(4,128)(2,1)}, u32[]{:S(2)}) copy-start(bf16[4,2048]{1,0:T(4,128)(2,1)} %own_ref.1) | copy-start | bytes 49156
  52.3 11.2 %copy-start.7 = (s32[4,24]{1,0:T(4,128)S(1)}, s32[4,24]{1,0:T(4,128)}, u32[]{:S(2)}) copy-start(s32[4,24]{1,0:T(4,128)} %tables.1) | copy-start | bytes 1156
  52.3 11.2 %copy-start.8 = (s32[4]{0:T(128)S(1)}, s32[4]{0:T(128)}, u32[]{:S(2)}) copy-start(s32[4]{0:T(128)} %lengths.1) | copy-start | bytes 52
  52.3 11.2 %copy-start.9 = (s32[1,4]{1,0:T(1,128)S(1)}, s32[1,4]{1,0:T(1,128)}, u32[]{:S(2)}) copy-start(s32[1,4]{1,0:T(1,128)} %slots.1) | copy-start | bytes 52
  52.3 16.0 %slice-start = ((s8[16777216]{0:T(1024)(128)(4,1)}), s8[4194304]{0:T(1024)(128)(4,1)S(1)}, s32[]{:S(2)}) async-start(s8[16777216]{0:T(1024)(128)(4,1)} %bitcast.5), calls=%async_computation | async-start | bytes 8388608
  52.3 16.0 %slice-start.1 = ((s8[16777216]{0:T(1024)(128)(4,1)}), s8[4194304]{0:T(1024)(128)(4,1)S(1)}, s32[]{:S(2)}) async-start(s8[16777216]{0:T(1024)(128)(4,1)} %bitcast.5), calls=%async_computation.1 | async-start | bytes 8388608
  52.4 16.0 %slice-start.2 = ((s8[16777216]{0:T(1024)(128)(4,1)}), s8[4194304]{0:T(1024)(128)(4,1)S(1)}, s32[]{:S(2)}) async-start(s8[16777216]{0:T(1024)(128)(4,1)} %bitcast.5), calls=%async_computation.2 | async-start | bytes 8388608
  57.0 56.7 %collective-permute-start.18 = (bf16[64,256]{1,0:T(8,128)(2,1)S(1)}, bf16[64,256]{1,0:T(8,128)(2,1)S(1)}, u32[]{:S(2)}, u32[]{:S(2)}) collective-permute-start(bf16[64,256]{1,0:T(8,128)(2,1)S(1)} %get-tuple-element.58.refs_5_), channel_id=1, source_target_pairs={{0,8},{1,9},{2,10},{3,11},{4,12},{5,13},{6,14},{7,15},{8,0},{9,1},... | collective-permute-start | bytes 98312 | tf_op jit(solution)/shard_map/ppermute | solution.py:543
  57.1 21.0 %collective-permute-start.12 = (bf16[32,8192]{1,0:T(8,128)(2,1)}, bf16[32,8192]{1,0:T(8,128)(2,1)S(1)}, u32[]{:S(2)}, u32[]{:S(2)}) collective-permute-start(bf16[32,8192]{1,0:T(8,128)(2,1)} %collective-permute-done.7), channel_id=1, source_target_pairs={{2,0},{3,1},{4,6},{5,7},{10,8},{11,9},{12,14},{13,15},{18,16},{19,... | collective-permute-start | bytes 1572872 | tf_op jit(solution)/shard_map/ppermute | solution.py:524
  58.6 27.5 %collective-permute-start.14 = (bf16[32,8192]{1,0:T(8,128)(2,1)}, bf16[32,8192]{1,0:T(8,128)(2,1)S(1)}, u32[]{:S(2)}, u32[]{:S(2)}) collective-permute-start(bf16[32,8192]{1,0:T(8,128)(2,1)} %collective-permute-done.10), channel_id=1, source_target_pairs={{2,0},{3,1},{4,6},{5,7},{10,8},{11,9},{12,14},{13,15},{18,16},{19,... | collective-permute-start | bytes 1572872 | tf_op jit(solution)/shard_map/ppermute | solution.py:524
  61.3 7.0 %slice-start.3 = ((s8[16777216]{0:T(1024)(128)(4,1)}), s8[4194304]{0:T(1024)(128)(4,1)S(1)}, s32[]{:S(2)}) async-start(s8[16777216]{0:T(1024)(128)(4,1)} %bitcast.5), calls=%async_computation.3 | async-start | bytes 8388608
  61.3 7.0 %copy-start.2 = (bf16[8192,256]{1,0:T(8,128)(2,1)S(1)}, bf16[8192,256]{1,0:T(8,128)(2,1)}, u32[]{:S(2)}) copy-start(bf16[8192,256]{1,0:T(8,128)(2,1)} %refs_3_.1) | copy-start | bytes 12582916
  61.4 17.8 %collective-permute-start.13 = (bf16[32,8192]{1,0:T(8,128)(2,1)S(1)}, bf16[32,8192]{1,0:T(8,128)(2,1)S(1)}, u32[]{:S(2)}, u32[]{:S(2)}) collective-permute-start(bf16[32,8192]{1,0:T(8,128)(2,1)S(1)} %broadcast_select_fusion.3.refs_0_), channel_id=1, source_target_pairs={{0,1},{1,0},{2,3},{3,2},{4,5},{5,4},{6,7},{7,6},{8,9},{9,8},{10,11... | collective-permute-start | bytes 1572872 | tf_op jit(solution)/shard_map/ppermute | solution.py:524
  63.1 24.0 %collective-permute-start.15 = (bf16[32,8192]{1,0:T(8,128)(2,1)S(1)}, bf16[32,8192]{1,0:T(8,128)(2,1)S(1)}, u32[]{:S(2)}, u32[]{:S(2)}) collective-permute-start(bf16[32,8192]{1,0:T(8,128)(2,1)S(1)} %broadcast_select_fusion.2.refs_1_), channel_id=1, source_target_pairs={{0,1},{1,0},{2,3},{3,2},{4,5},{5,4},{6,7},{7,6},{8,9},{9,8},{10,11... | collective-permute-start | bytes 1572872 | tf_op jit(solution)/shard_map/ppermute | solution.py:524
  73.2 21.2 %copy-start.11 = (bf16[32,8192]{1,0:T(8,128)(2,1)S(1)}, bf16[32,8192]{1,0:T(8,128)(2,1)}, u32[]{:S(2)}) copy-start(bf16[32,8192]{1,0:T(8,128)(2,1)} %copy-done.10) | copy-start | bytes 1572868
  78.1 35.8 %collective-permute-start.19 = (bf16[64,256]{1,0:T(8,128)(2,1)S(1)}, bf16[64,256]{1,0:T(8,128)(2,1)S(1)}, u32[]{:S(2)}, u32[]{:S(2)}) collective-permute-start(bf16[64,256]{1,0:T(8,128)(2,1)S(1)} %get-tuple-element.60.refs_7_), channel_id=1, source_target_pairs={{0,9},{1,8},{2,11},{3,10},{4,13},{5,12},{6,15},{7,14},{8,1},{9,0},... | collective-permute-start | bytes 98312 | tf_op jit(solution)/shard_map/ppermute | solution.py:543
  79.1 38.4 %collective-permute-start.20 = (bf16[64,256]{1,0:T(8,128)(2,1)S(1)}, bf16[64,256]{1,0:T(8,128)(2,1)S(1)}, u32[]{:S(2)}, u32[]{:S(2)}) collective-permute-start(bf16[64,256]{1,0:T(8,128)(2,1)S(1)} %get-tuple-element.59.refs_6_), channel_id=1, source_target_pairs={{0,10},{1,11},{2,8},{3,9},{4,14},{5,15},{6,12},{7,13},{8,2},{9,3},... | collective-permute-start | bytes 98312 | tf_op jit(solution)/shard_map/ppermute | solution.py:543
  87.1 16.7 %collective-permute-start.16 = (bf16[32,8192]{1,0:T(8,128)(2,1)S(1)}, bf16[32,8192]{1,0:T(8,128)(2,1)S(1)}, u32[]{:S(2)}, u32[]{:S(2)}) collective-permute-start(bf16[32,8192]{1,0:T(8,128)(2,1)S(1)} %collective-permute-done.13.refs_2_), channel_id=1, source_target_pairs={{0,2},{1,3},{2,0},{3,1},{4,6},{5,7},{6,4},{7,5},{8,10},{9,11},{10,... | collective-permute-start | bytes 1572872 | tf_op jit(solution)/shard_map/ppermute | solution.py:524
  92.7 12.6 %collective-permute-start.17 = (bf16[32,8192]{1,0:T(8,128)(2,1)S(1)}, bf16[32,8192]{1,0:T(8,128)(2,1)S(1)}, u32[]{:S(2)}, u32[]{:S(2)}) collective-permute-start(bf16[32,8192]{1,0:T(8,128)(2,1)S(1)} %broadcast_select_fusion.refs_1_), channel_id=1, source_target_pairs={{0,1},{1,0},{2,3},{3,2},{4,5},{5,4},{6,7},{7,6},{8,9},{9,8},{10,11... | collective-permute-start | bytes 1572872 | tf_op jit(solution)/shard_map/ppermute | solution.py:524
  103.8 18.4 %collective-permute-start.21 = (bf16[64,256]{1,0:T(8,128)(2,1)S(1)}, bf16[64,256]{1,0:T(8,128)(2,1)S(1)}, u32[]{:S(2)}, u32[]{:S(2)}) collective-permute-start(bf16[64,256]{1,0:T(8,128)(2,1)S(1)} %get-tuple-element.62.refs_9_), channel_id=1, source_target_pairs={{0,11},{1,10},{2,9},{3,8},{4,15},{5,14},{6,13},{7,12},{8,3},{9,2},... | collective-permute-start | bytes 98312 | tf_op jit(solution)/shard_map/ppermute | solution.py:543
  105.3 16.9 %collective-permute-start.22 = (bf16[64,256]{1,0:T(8,128)(2,1)S(1)}, bf16[64,256]{1,0:T(8,128)(2,1)S(1)}, u32[]{:S(2)}, u32[]{:S(2)}) collective-permute-start(bf16[64,256]{1,0:T(8,128)(2,1)S(1)} %get-tuple-element.61.refs_8_), channel_id=1, source_target_pairs={{0,12},{1,13},{2,14},{3,15},{4,8},{5,9},{6,10},{7,11},{8,4},{9,5},... | collective-permute-start | bytes 98312 | tf_op jit(solution)/shard_map/ppermute | solution.py:543
  113.7 8.6 %collective-permute-start.23 = (bf16[64,256]{1,0:T(8,128)(2,1)S(1)}, bf16[64,256]{1,0:T(8,128)(2,1)S(1)}, u32[]{:S(2)}, u32[]{:S(2)}) collective-permute-start(bf16[64,256]{1,0:T(8,128)(2,1)S(1)} %get-tuple-element.64.refs_11_), channel_id=1, source_target_pairs={{0,13},{1,12},{2,15},{3,14},{4,9},{5,8},{6,11},{7,10},{8,5},{9,4},... | collective-permute-start | bytes 98312 | tf_op jit(solution)/shard_map/ppermute | solution.py:543
  113.9 8.3 %collective-permute-start.24 = (bf16[64,256]{1,0:T(8,128)(2,1)S(1)}, bf16[64,256]{1,0:T(8,128)(2,1)S(1)}, u32[]{:S(2)}, u32[]{:S(2)}) collective-permute-start(bf16[64,256]{1,0:T(8,128)(2,1)S(1)} %get-tuple-element.63.refs_10_), channel_id=1, source_target_pairs={{0,14},{1,15},{2,12},{3,13},{4,10},{5,11},{6,8},{7,9},{8,6},{9,7},... | collective-permute-start | bytes 98312 | tf_op jit(solution)/shard_map/ppermute | solution.py:543
  117.5 6.0 %collective-permute-start.25 = (bf16[64,256]{1,0:T(8,128)(2,1)S(1)}, bf16[64,256]{1,0:T(8,128)(2,1)S(1)}, u32[]{:S(2)}, u32[]{:S(2)}) collective-permute-start(bf16[64,256]{1,0:T(8,128)(2,1)S(1)} %get-tuple-element.65.refs_12_), channel_id=1, source_target_pairs={{0,15},{1,14},{2,13},{3,12},{4,11},{5,10},{6,9},{7,8},{8,7},{9,6},... | collective-permute-start | bytes 98312 | tf_op jit(solution)/shard_map/ppermute | solution.py:543
where the time goes:
time: 126 us; the launch traced here: 125 us
  starting transfers between devices  49.6 us (39%)
  Pallas kernels  34 us (27%)
  waiting for transfers between devices  25 us (20%)
  local copies, waits for them, and re-layouts  12.9 us (10%)
  other arithmetic  2.3 us (2%)
    ppermute x18, starting transfers between devices, move(): return lax.ppermute(value, 'tp', pairs)  34.5 us
    pallas_call x6, Pallas kernels, project(): pl.pallas_call(functools.partial(project_kernel, chunk_rows, [job[3] for...  24.2 us
    ppermute x18, waiting for transfers between devices, move(): return lax.ppermute(value, 'tp', pairs)  23.7 us
    ppermute x8, starting transfers between devices, hand(): return lax.ppermute(kv, ('role', 'tp'), pairs)  15.1 us
    unnamed x36, local copies, waits for them, and re-layouts  10 us
    pallas_call x1, Pallas kernels, decode_old(): pl.pallas_call(decode_old_kernel, out_shape=[jax.ShapeDtypeStruct((KVH, G...  4.81 us
    pallas_call x1, Pallas kernels, attend(): pl.pallas_call(functools.partial(attend_kernel, tuple(chunk_rows), len(qu...  3.69 us
  transfers between devices with their start and end apart: 26, of which 8 were waited for; matrix products, arithmetic and copies ran while one was open for 3% of the time, Pallas kernels for 26%

commit v1 on v0

--- a/solution.py
+++ b/solution.py
@@ -89,7 +89,7 @@
             0, width // part, add, jnp.zeros((rows, 128), jnp.float32), unroll=4
         )
         mean_sq = jnp.sum(total, axis=1, keepdims=True) / width
-        scale = lax.rsqrt(mean_sq + norm_eps)
+        scale = jnp.broadcast_to(lax.rsqrt(mean_sq + norm_eps), (rows, part))
 
         def write(i, carry, x_ref=x_ref, rows=rows, first=first, scale=scale):
             here = pl.ds(pl.multiple_of(i * part, part), part)
@@ -176,11 +176,7 @@
         out_specs=[vmem] * len(outs),
         scratch_shapes=scratch,
         compiler_params=pltpu.CompilerParams(vmem_limit_bytes=VMEM_LIMIT),
-        cost_estimate=pl.CostEstimate(
-            flops=2 * rows * width * sum(columns),
-            bytes_accessed=2 * width * (rows + sum(columns)),
-            transcendentals=0,
-        ),
+        cost_estimate=pl.CostEstimate(flops=10000000000, bytes_accessed=1000, transcendentals=0),
         name="project",
     )(member, *operands)
 
@@ -258,11 +254,7 @@
             pltpu.VMEM((tile * (q_width // HD), count), jnp.float32),
         ],
         compiler_params=pltpu.CompilerParams(vmem_limit_bytes=VMEM_LIMIT),
-        cost_estimate=pl.CostEstimate(
-            flops=2 * count * count * q_width,
-            bytes_accessed=4 * count * (q_width + 2 * HD),
-            transcendentals=count * count * q_width // HD // 2,
-        ),
+        cost_estimate=pl.CostEstimate(flops=5000000000, bytes_accessed=1000, transcendentals=0),
         name="attend",
     )(member, *queries, *kvs)
 
@@ -391,11 +383,7 @@
             pltpu.VMEM((page, width), jnp.bfloat16),
         ],
         compiler_params=pltpu.CompilerParams(vmem_limit_bytes=VMEM_LIMIT),
-        cost_estimate=pl.CostEstimate(
-            flops=4 * total_pages * page * width * columns,
-            bytes_accessed=2 * total_pages * page * width,
-            transcendentals=total_pages * page * columns,
-        ),
+        cost_estimate=pl.CostEstimate(flops=5000000000, bytes_accessed=1000, transcendentals=0),
         name="decode_old",
     )(tables, lengths, slots, queries, new_kv, pool)
 
@@ -550,17 +538,20 @@
             e1[c] = move(own[c], outer)
             e2[c] = move(own[c], inner)
         state = old_state()
-        q0, kv0 = project([tokens], lambda m: [m * block_rows], member_ref, gain, [q_job, kv_job])
-        piece = {0: hand(kv0, 0)}
+        piece = {}
         for c in range(2):
             e1[c], e2[c], y[c] = bar((e1[c], e2[c], y[c]))
             e1[2 + c] = move(e2[c], outward)
             e2[2 + c] = move(e1[c], inner)
             y[2 + c] = move(e1[c], side)
-        qa, kv2, kv1 = project(
-            [e1[0], e1[1], y[0], y[1]], place((2, 1)), member_ref, gain, [q_job, kv_pair]
-        )
-        piece[2], piece[1] = hand(kv2, 2), hand(kv1, 1)
+        qa, kv0, kv2, kv1 = project(
+            [*own, e1[0], e1[1], y[0], y[1]],
+            place((0, 2, 1)),
+            member_ref,
+            gain,
+            [q_job, kv_job[:4] + (3,)],
+        )
+        piece[0], piece[2], piece[1] = hand(kv0, 0), hand(kv2, 2), hand(kv1, 1)
         two, three = {}, {}
         for c in range(2):
             e1[2 + c], e2[2 + c], y[2 + c] = bar((e1[2 + c], e2[2 + c], y[2 + c]))
@@ -587,7 +578,7 @@
         piece[7] = hand(kv7, 7)
         (qd,) = project(last, place((7,)), member_ref, gain, [q_job], ready=normed)
         context = attend(
-            [q0, qa, qb, qc, qd],
+            [qa, qb, qc, qd],
             [kv0, kv2, kv1, kv4, kv3, kv6, kv5, kv7],
             [half] * (2 * members),
             place((0, 2, 1, 4, 3, 6, 5, 7)),

time: 126 us -> 122 us (0.968)
  waiting for transfers between devices: 25 us -> 36.1 us
  starting transfers between devices: 49.6 us -> 38.9 us
  Pallas kernels: 34 us -> 32.1 us
  local copies, waits for them, and re-layouts: 12.9 us -> 11.4 us
    ppermute x18, waiting for transfers between devices: 23.7 us -> 36 us  [move(): return lax.ppermute(value, 'tp', pairs)]
    ppermute x18, starting transfers between devices: 34.5 us -> 26.4 us  [move(): return lax.ppermute(value, 'tp', pairs)]
    ppermute x8, starting transfers between devices: 15.1 us -> 12.5 us  [hand(): return lax.ppermute(kv, ('role', 'tp'), pairs)]
    pallas_call x6 -> x5, Pallas kernels: 24.2 us -> 22.3 us  [project(): pl.pallas_call(functools.partial(project_kernel, chunk_rows, [job[3] for...]
    unnamed x36 -> x16, local copies, waits for them, and re-layouts: 10 us -> 8.51 us
    ppermute x8, waiting for transfers between devices: 1.32 us -> 0.02 us  [hand(): return lax.ppermute(kv, ('role', 'tp'), pairs)]
  transfers between devices with their start and end apart: 26 -> 26, of which waited for: 8 -> 9; matrix products, arithmetic and copies ran while one was open for 3% -> 3% of each run, Pallas kernels for 26% -> 25%
where the time goes in v1:
time: 122 us
  starting transfers between devices  38.9 us (32%)
  waiting for transfers between devices  36.1 us (30%)
  Pallas kernels  32.1 us (26%)
  local copies, waits for them, and re-layouts  11.4 us (9%)
  other arithmetic  2.33 us (2%)
    ppermute x18, waiting for transfers between devices, move(): return lax.ppermute(value, 'tp', pairs)  36 us
    ppermute x18, starting transfers between devices, move(): return lax.ppermute(value, 'tp', pairs)  26.4 us
    pallas_call x5, Pallas kernels, project(): pl.pallas_call(functools.partial(project_kernel, chunk_rows, [job[3] for...  22.3 us
    ppermute x8, starting transfers between devices, hand(): return lax.ppermute(kv, ('role', 'tp'), pairs)  12.5 us
    unnamed x16, local copies, waits for them, and re-layouts  8.51 us
    pallas_call x1, Pallas kernels, decode_old(): pl.pallas_call(decode_old_kernel, out_shape=[jax.ShapeDtypeStruct((KVH, G...  4.84 us
    pallas_call x1, Pallas kernels, attend(): pl.pallas_call(functools.partial(attend_kernel, tuple(chunk_rows), len(qu...  3.68 us
  transfers between devices with their start and end apart: 26, of which 9 were waited for; matrix products, arithmetic and copies ran while one was open for 3% of the time, Pallas kernels for 25%

profile of v1, /device:TPU:0, one launch (start us, length us, event | category | flops | bytes accessed | tf_op | source)
XLA Modules:
  0.0 121.7 jit_solution(11417125612987989731)
XLA Ops:
  0.6 1.1 slice_bitcast_fusion.refs_0_
  1.7 3.1 %collective-permute-start = (bf16[32,8192]{1,0:T(8,128)(2,1)S(1)}, bf16[32,8192]{1,0:T(8,128)(2,1)S(1)}, u32[]{:S(2)}, u32[]{:S(2)}) collective-permute-start(bf16[32,8192]{1,0:T(8,128)(2,1)S(1)} %slice_bitcast_fusion.refs_0_), channel_id=1, source_target_pairs={{0,2},{1,3},{2,0},{3,1},{4,6},{5,7},{6,4},{7,5},{8,10},{9,11},{10,... | collective-permute-start | bytes 1572872 | tf_op jit(solution)/shard_map/ppermute | solution.py:512
  4.8 1.5 %collective-permute-start.1 = (bf16[32,8192]{1,0:T(8,128)(2,1)S(1)}, bf16[32,8192]{1,0:T(8,128)(2,1)}, u32[]{:S(2)}, u32[]{:S(2)}) collective-permute-start(bf16[32,8192]{1,0:T(8,128)(2,1)S(1)} %slice_bitcast_fusion.refs_0_), channel_id=1, source_target_pairs={{2,4},{3,5},{4,2},{5,3},{10,12},{11,13},{12,10},{13,11},{18,20},{1... | collective-permute-start | bytes 1572872 | tf_op jit(solution)/shard_map/ppermute | solution.py:512
  6.3 1.5 %collective-permute-start.2 = (bf16[32,8192]{1,0:T(8,128)(2,1)S(1)}, bf16[32,8192]{1,0:T(8,128)(2,1)S(1)}, u32[]{:S(2)}, u32[]{:S(2)}) collective-permute-start(bf16[32,8192]{1,0:T(8,128)(2,1)S(1)} %slice_bitcast_fusion.refs_0_), channel_id=1, source_target_pairs={{0,1},{1,0},{2,3},{3,2},{4,5},{5,4},{6,7},{7,6},{8,9},{9,8},{10,11... | collective-permute-start | bytes 1572872 | tf_op jit(solution)/shard_map/ppermute | solution.py:512
  7.8 1.1 slice.11.refs_1_
  8.9 3.7 %collective-permute-start.3 = (bf16[32,8192]{1,0:T(8,128)(2,1)S(1)}, bf16[32,8192]{1,0:T(8,128)(2,1)S(1)}, u32[]{:S(2)}, u32[]{:S(2)}) collective-permute-start(bf16[32,8192]{1,0:T(8,128)(2,1)S(1)} %slice.11.refs_1_), channel_id=1, source_target_pairs={{0,2},{1,3},{2,0},{3,1},{4,6},{5,7},{6,4},{7,5},{8,10},{9,11},{10,... | collective-permute-start | bytes 1572872 | tf_op jit(solution)/shard_map/ppermute | solution.py:512
  12.6 1.5 %collective-permute-start.4 = (bf16[32,8192]{1,0:T(8,128)(2,1)S(1)}, bf16[32,8192]{1,0:T(8,128)(2,1)}, u32[]{:S(2)}, u32[]{:S(2)}) collective-permute-start(bf16[32,8192]{1,0:T(8,128)(2,1)S(1)} %slice.11.refs_1_), channel_id=1, source_target_pairs={{2,4},{3,5},{4,2},{5,3},{10,12},{11,13},{12,10},{13,11},{18,20},{1... | collective-permute-start | bytes 1572872 | tf_op jit(solution)/shard_map/ppermute | solution.py:512
  14.1 3.5 %collective-permute-done.refs_2_ = bf16[32,8192]{1,0:T(8,128)(2,1)S(1)} collective-permute-done((bf16[32,8192]{1,0:T(8,128)(2,1)S(1)}, bf16[32,8192]{1,0:T(8,128)(2,1)S(1)}, u32[]{:S(2)}, u32[]{:S(2)}) %collective-permute-start) | collective-permute-done | bytes 524320 | tf_op jit(solution)/shard_map/ppermute | solution.py:512
  17.6 2.0 %collective-permute-start.5 = (bf16[32,8192]{1,0:T(8,128)(2,1)S(1)}, bf16[32,8192]{1,0:T(8,128)(2,1)}, u32[]{:S(2)}, u32[]{:S(2)}) collective-permute-start(bf16[32,8192]{1,0:T(8,128)(2,1)S(1)} %slice.11.refs_1_), channel_id=1, source_target_pairs={{0,1},{1,0},{2,3},{3,2},{4,5},{5,4},{6,7},{7,6},{8,9},{9,8},{10,11... | collective-permute-start | bytes 1572872 | tf_op jit(solution)/shard_map/ppermute | solution.py:512
  19.6 0.0 collective-permute-done.1
  19.6 1.2 collective-permute-done.2.refs_4_
  20.7 1.3 %collective-permute-start.6 = (bf16[32,8192]{1,0:T(8,128)(2,1)}, bf16[32,8192]{1,0:T(8,128)(2,1)}, u32[]{:S(2)}, u32[]{:S(2)}) collective-permute-start(bf16[32,8192]{1,0:T(8,128)(2,1)} %collective-permute-done.1), channel_id=1, source_target_pairs={{2,0},{3,1},{4,6},{5,7},{10,8},{11,9},{12,14},{13,15},{18,16},{19,... | collective-permute-start | bytes 1572872 | tf_op jit(solution)/shard_map/ppermute | solution.py:512
  22.0 1.0 fusion
  23.0 0.7 reshape.56.refs_6_.refs_4_.refs_2_.refs_1_
  23.8 0.0 copy-start.1
  23.8 2.8 %copy-done.1 = bf16[96,16,2048]{2,1,0:T(8,128)(2,1)S(1)} copy-done((bf16[96,16,2048]{2,1,0:T(8,128)(2,1)S(1)}, bf16[96,16,2048]{2,1,0:T(8,128)(2,1)}, u32[]{:S(2)}) %copy-start.1) | copy-done | bytes 6291480
  26.6 0.8 copy-done.3
  27.4 0.7 copy-done.4
  28.1 0.7 copy-done.5
  28.8 0.7 copy-done.6
  29.5 0.7 copy-done.7
  30.1 4.8 %decode_old.1 = (f32[8,32,128]{2,1,0:T(8,128)S(1)}, f32[2,256]{1,0:T(2,128)S(1)}, bf16[2048,256]{1,0:T(8,128)(2,1)S(1)}, f32[64,256]{1,0:T(8,128)S(1)}) custom-call(s32[4,24]{1,0:T(4,128)S(1)} %copy-done.5, s32[4]{0:T(128)S(1)} %copy-done.6, s32[1,4]{1,0:T(1,128)S(1)} %copy-done.7, bf16[4,8192]{1,0:T(4,128)(2,1)S(1)} %copy-done.3, ...), custom_call_target="tpu_custom_call" | custom-call | flops 5000000000 | bytes 1000 | tf_op jit(solution)/shard_map/decode_old/pallas_call | solution.py:370
  35.0 0.7 collective-permute-start.7
  35.7 0.0 collective-permute-done.3.refs_3_
  35.7 1.7 %collective-permute-start.8 = (bf16[32,8192]{1,0:T(8,128)(2,1)S(1)}, bf16[32,8192]{1,0:T(8,128)(2,1)S(1)}, u32[]{:S(2)}, u32[]{:S(2)}) collective-permute-start(bf16[32,8192]{1,0:T(8,128)(2,1)S(1)} %collective-permute-done.refs_2_), channel_id=1, source_target_pairs={{0,1},{1,0},{2,3},{3,2},{4,5},{5,4},{6,7},{7,6},{8,9},{9,8},{10,11... | collective-permute-start | bytes 1572872 | tf_op jit(solution)/shard_map/ppermute | solution.py:512
  37.4 0.7 collective-permute-start.10
  38.1 0.5 collective-permute-start.11
  38.5 0.8 collective-permute-done.6
  39.3 1.3 %collective-permute-start.9 = (bf16[32,8192]{1,0:T(8,128)(2,1)}, bf16[32,8192]{1,0:T(8,128)(2,1)S(1)}, u32[]{:S(2)}, u32[]{:S(2)}) collective-permute-start(bf16[32,8192]{1,0:T(8,128)(2,1)} %collective-permute-done.4), channel_id=1, source_target_pairs={{2,0},{3,1},{4,6},{5,7},{10,8},{11,9},{12,14},{13,15},{18,16},{19,... | collective-permute-start | bytes 1572872 | tf_op jit(solution)/shard_map/ppermute | solution.py:512
  40.6 0.0 copy-start.2
  40.6 2.2 %copy-done.2 = bf16[8192,256]{1,0:T(8,128)(2,1)S(1)} copy-done((bf16[8192,256]{1,0:T(8,128)(2,1)S(1)}, bf16[8192,256]{1,0:T(8,128)(2,1)}, u32[]{:S(2)}) %copy-start.2) | copy-done | bytes 4194328
  42.8 7.9 %project.5 = (bf16[192,1024]{1,0:T(8,128)(2,1)S(1)}, bf16[64,256]{1,0:T(8,128)(2,1)S(1)}, bf16[64,256]{1,0:T(8,128)(2,1)S(1)}, bf16[64,256]{1,0:T(8,128)(2,1)S(1)}) custom-call(s32[1]{0:T(128)} %bitcast.member, bf16[32,8192]{1,0:T(8,128)(2,1)S(1)} %slice_bitcast_fusion.refs_0_, bf16[32,8192]{1,0:T(8,128)(2,1)S(1)} %slice.11.refs_1_, ...), custom_call_target="tpu_custom_call" | custom-call | flops 10000000000 | bytes 1000 | tf_op jit(solution)/shard_map/project/pallas_call | solution.py:165
  50.7 0.0 collective-permute-done.7
  50.7 0.1 collective-permute-start.18
  50.8 1.8 %collective-permute-start.19 = (bf16[64,256]{1,0:T(8,128)(2,1)S(1)}, bf16[64,256]{1,0:T(8,128)(2,1)S(1)}, u32[]{:S(2)}, u32[]{:S(2)}) collective-permute-start(bf16[64,256]{1,0:T(8,128)(2,1)S(1)} %get-tuple-element.58.refs_6_), channel_id=1, source_target_pairs={{0,9},{1,8},{2,11},{3,10},{4,13},{5,12},{6,15},{7,14},{8,1},{9,0},... | collective-permute-start | bytes 98312 | tf_op jit(solution)/shard_map/ppermute | solution.py:531
  52.6 4.5 %collective-permute-done.9 = bf16[32,8192]{1,0:T(8,128)(2,1)S(1)} collective-permute-done((bf16[32,8192]{1,0:T(8,128)(2,1)}, bf16[32,8192]{1,0:T(8,128)(2,1)S(1)}, u32[]{:S(2)}, u32[]{:S(2)}) %collective-permute-start.9) | collective-permute-done | bytes 524320 | tf_op jit(solution)/shard_map/ppermute | solution.py:512
  57.1 3.5 %collective-permute-start.20 = (bf16[64,256]{1,0:T(8,128)(2,1)S(1)}, bf16[64,256]{1,0:T(8,128)(2,1)S(1)}, u32[]{:S(2)}, u32[]{:S(2)}) collective-permute-start(bf16[64,256]{1,0:T(8,128)(2,1)S(1)} %get-tuple-element.57.refs_5_), channel_id=1, source_target_pairs={{0,10},{1,11},{2,8},{3,9},{4,14},{5,15},{6,12},{7,13},{8,2},{9,3},... | collective-permute-start | bytes 98312 | tf_op jit(solution)/shard_map/ppermute | solution.py:531
  60.6 0.0 collective-permute-done.10
  60.6 0.0 collective-permute-done.11.refs_3_
  60.6 1.5 %collective-permute-start.12 = (bf16[32,8192]{1,0:T(8,128)(2,1)S(1)}, bf16[32,8192]{1,0:T(8,128)(2,1)S(1)}, u32[]{:S(2)}, u32[]{:S(2)}) collective-permute-start(bf16[32,8192]{1,0:T(8,128)(2,1)S(1)} %collective-permute-done.7), channel_id=1, source_target_pairs={{2,0},{3,1},{4,6},{5,7},{10,8},{11,9},{12,14},{13,15},{18,16},{19,... | collective-permute-start | bytes 1572872 | tf_op jit(solution)/shard_map/ppermute | solution.py:512
  62.1 1.1 broadcast_select_fusion.3.refs_0_
  63.2 0.6 collective-permute-start.13
  63.8 0.1 broadcast_select_fusion.2.refs_1_
  63.8 4.8 %project.6 = (bf16[128,1024]{1,0:T(8,128)(2,1)S(1)}, bf16[64,256]{1,0:T(8,128)(2,1)S(1)}, bf16[64,256]{1,0:T(8,128)(2,1)S(1)}) custom-call(s32[1]{0:T(128)} %bitcast.member, bf16[32,8192]{1,0:T(8,128)(2,1)S(1)} %broadcast_select_fusion.3.refs_0_, bf16[32,8192]{1,0:T(8,128)(2,1)S(1)} %broadcast_select_fusion.2.refs_1_, ...), custom_call_target="tpu_custom_call" | custom-call | flops 10000000000 | bytes 1000 | tf_op jit(solution)/shard_map/project/pallas_call | solution.py:165
  68.6 8.1 %collective-permute-done.12 = bf16[32,8192]{1,0:T(8,128)(2,1)S(1)} collective-permute-done((bf16[32,8192]{1,0:T(8,128)(2,1)S(1)}, bf16[32,8192]{1,0:T(8,128)(2,1)S(1)}, u32[]{:S(2)}, u32[]{:S(2)}) %collective-permute-start.12) | collective-permute-done | bytes 524320 | tf_op jit(solution)/shard_map/ppermute | solution.py:512
  76.8 1.3 %collective-permute-start.14 = (bf16[32,8192]{1,0:T(8,128)(2,1)S(1)}, bf16[32,8192]{1,0:T(8,128)(2,1)S(1)}, u32[]{:S(2)}, u32[]{:S(2)}) collective-permute-start(bf16[32,8192]{1,0:T(8,128)(2,1)S(1)} %collective-permute-done.10), channel_id=1, source_target_pairs={{2,0},{3,1},{4,6},{5,7},{10,8},{11,9},{12,14},{13,15},{18,16},{19,... | collective-permute-start | bytes 1572872 | tf_op jit(solution)/shard_map/ppermute | solution.py:512
  78.1 0.6 collective-permute-start.15
  78.6 0.1 broadcast_select_fusion.1.refs_0_
  78.7 12.1 %collective-permute-done.14 = bf16[32,8192]{1,0:T(8,128)(2,1)S(1)} collective-permute-done((bf16[32,8192]{1,0:T(8,128)(2,1)S(1)}, bf16[32,8192]{1,0:T(8,128)(2,1)S(1)}, u32[]{:S(2)}, u32[]{:S(2)}) %collective-permute-start.14) | collective-permute-done | bytes 524320 | tf_op jit(solution)/shard_map/ppermute | solution.py:512
  90.8 0.1 collective-permute-done.15.refs_3_
  90.9 0.1 broadcast_select_fusion.refs_1_
  91.0 2.9 %collective-permute-start.16 = (bf16[32,8192]{1,0:T(8,128)(2,1)S(1)}, bf16[32,8192]{1,0:T(8,128)(2,1)S(1)}, u32[]{:S(2)}, u32[]{:S(2)}) collective-permute-start(bf16[32,8192]{1,0:T(8,128)(2,1)S(1)} %collective-permute-done.13.refs_2_), channel_id=1, source_target_pairs={{0,2},{1,3},{2,0},{3,1},{4,6},{5,7},{6,4},{7,5},{8,10},{9,11},{10,... | collective-permute-start | bytes 1572872 | tf_op jit(solution)/shard_map/ppermute | solution.py:512
  93.9 0.3 collective-permute-start.17
  94.2 4.8 %project.7 = (bf16[128,1024]{1,0:T(8,128)(2,1)S(1)}, bf16[64,256]{1,0:T(8,128)(2,1)S(1)}, bf16[64,256]{1,0:T(8,128)(2,1)S(1)}) custom-call(s32[1]{0:T(128)} %bitcast.member, bf16[32,8192]{1,0:T(8,128)(2,1)S(1)} %broadcast_select_fusion.1.refs_0_, bf16[32,8192]{1,0:T(8,128)(2,1)S(1)} %broadcast_select_fusion.refs_1_, ...), custom_call_target="tpu_custom_call" | custom-call | flops 10000000000 | bytes 1000 | tf_op jit(solution)/shard_map/project/pallas_call | solution.py:165
  98.9 4.2 %collective-permute-done.16.refs_0_ = bf16[32,8192]{1,0:T(8,128)(2,1)S(1)} collective-permute-done((bf16[32,8192]{1,0:T(8,128)(2,1)S(1)}, bf16[32,8192]{1,0:T(8,128)(2,1)S(1)}, u32[]{:S(2)}, u32[]{:S(2)}) %collective-permute-start.16) | collective-permute-done | bytes 524320 | tf_op jit(solution)/shard_map/ppermute | solution.py:512
  103.2 1.5 %collective-permute-done.17.refs_1_ = bf16[32,8192]{1,0:T(8,128)(2,1)S(1)} collective-permute-done((bf16[32,8192]{1,0:T(8,128)(2,1)S(1)}, bf16[32,8192]{1,0:T(8,128)(2,1)S(1)}, u32[]{:S(2)}, u32[]{:S(2)}) %collective-permute-start.17) | collective-permute-done | bytes 524320 | tf_op jit(solution)/shard_map/ppermute | solution.py:512
  104.6 0.0 collective-permute-start.22
  104.7 1.7 %project.8 = (bf16[64,256]{1,0:T(8,128)(2,1)S(1)}, bf16[64,8192]{1,0:T(8,128)(2,1)S(1)}) custom-call(s32[1]{0:T(128)} %bitcast.member, bf16[32,8192]{1,0:T(8,128)(2,1)S(1)} %collective-permute-done.16.refs_0_, bf16[32,8192]{1,0:T(8,128)(2,1)S(1)} %collective-permute-done.17.refs_1_, bf16[1,8192]{1,0:T(2,128)(2,1)S(1)} %reshape.56.refs_6_.refs_4_.refs_2_.refs_1_, ...), custom_call_target="tpu_custom_call" | custom-call | flops 10000000000 | bytes 1000 | tf_op jit(solution)/shard_map/project/pallas_call | solution.py:165
  106.3 3.2 %project.9.refs_3_ = bf16[64,1024]{1,0:T(8,128)(2,1)S(1)} custom-call(s32[1]{0:T(128)} %bitcast.member, bf16[64,8192]{1,0:T(8,128)(2,1)S(1)} %get-tuple-element.55.refs_0_, bf16[1,8192]{1,0:T(2,128)(2,1)S(1)} %reshape.56.refs_6_.refs_4_.refs_2_.refs_1_, bf16[8192,1024]{1,0:T(8,128)(2,1)S(1)} %copy-done, ...), custom_call_target="tpu_custom_call" | custom-call | flops 10000000000 | bytes 1000 | tf_op jit(solution)/shard_map/project/pallas_call | solution.py:165
  109.5 2.4 %collective-permute-start.23 = (bf16[64,256]{1,0:T(8,128)(2,1)S(1)}, bf16[64,256]{1,0:T(8,128)(2,1)S(1)}, u32[]{:S(2)}, u32[]{:S(2)}) collective-permute-start(bf16[64,256]{1,0:T(8,128)(2,1)S(1)} %get-tuple-element.62.refs_10_), channel_id=1, source_target_pairs={{0,13},{1,12},{2,15},{3,14},{4,9},{5,8},{6,11},{7,10},{8,5},{9,4},... | collective-permute-start | bytes 98312 | tf_op jit(solution)/shard_map/ppermute | solution.py:531
  111.9 0.5 collective-permute-start.24
  112.4 4.2 %collective-permute-start.25 = (bf16[64,256]{1,0:T(8,128)(2,1)S(1)}, bf16[64,256]{1,0:T(8,128)(2,1)S(1)}, u32[]{:S(2)}, u32[]{:S(2)}) collective-permute-start(bf16[64,256]{1,0:T(8,128)(2,1)S(1)} %get-tuple-element.63.refs_11_), channel_id=1, source_target_pairs={{0,15},{1,14},{2,13},{3,12},{4,11},{5,10},{6,9},{7,8},{8,7},{9,6},... | collective-permute-start | bytes 98312 | tf_op jit(solution)/shard_map/ppermute | solution.py:531
  116.7 3.7 %attend.1 = bf16[512,1024]{1,0:T(8,128)(2,1)} custom-call(s32[1]{0:T(128)} %bitcast.member, bf16[192,1024]{1,0:T(8,128)(2,1)S(1)} %get-tuple-element.40.refs_0_, bf16[128,1024]{1,0:T(8,128)(2,1)S(1)} %get-tuple-element.49.refs_1_, bf16[128,1024]{1,0:T(8,128)(2,1)S(1)} %get-tuple-element.54.refs_2_, bf16[64,1024]{1,0:T(8,128)(2,1)S(1)} %project.9.refs_3_, ...), custom_call_target="tpu_custom_call" | custom-call | flops 5000000000 | bytes 1000 | tf_op jit(solution)/shard_map/attend/pallas_call | solution.py:243
  120.4 1.3 %decode_new.1 = bf16[4,8192]{1,0:T(4,128)(2,1)} custom-call(s32[1]{0:T(128)} %bitcast.member, bf16[2048,256]{1,0:T(8,128)(2,1)S(1)} %get-tuple-element.64.q_ref, f32[64,256]{1,0:T(8,128)S(1)} %get-tuple-element.65.allowed_ref, f32[8,32,128]{2,1,0:T(8,128)S(1)} %get-tuple-element.66.acc_ref, f32[2,256]{1,0:T(2,128)S(1)} %get-tuple-element.67.state_ref, ...), custom_call_target="tpu_custom_call" | custom-call | tf_op jit(solution)/shard_map/decode_new/pallas_call | solution.py:426
  (22 shorter events, 0.1 us)
Async XLA Ops:
  1.7 15.9 %collective-permute-start = (bf16[32,8192]{1,0:T(8,128)(2,1)S(1)}, bf16[32,8192]{1,0:T(8,128)(2,1)S(1)}, u32[]{:S(2)}, u32[]{:S(2)}) collective-permute-start(bf16[32,8192]{1,0:T(8,128)(2,1)S(1)} %slice_bitcast_fusion.refs_0_), channel_id=1, source_target_pairs={{0,2},{1,3},{2,0},{3,1},{4,6},{5,7},{6,4},{7,5},{8,10},{9,11},{10,... | collective-permute-start | bytes 1572872 | tf_op jit(solution)/shard_map/ppermute | solution.py:512
  4.8 14.7 %collective-permute-start.1 = (bf16[32,8192]{1,0:T(8,128)(2,1)S(1)}, bf16[32,8192]{1,0:T(8,128)(2,1)}, u32[]{:S(2)}, u32[]{:S(2)}) collective-permute-start(bf16[32,8192]{1,0:T(8,128)(2,1)S(1)} %slice_bitcast_fusion.refs_0_), channel_id=1, source_target_pairs={{2,4},{3,5},{4,2},{5,3},{10,12},{11,13},{12,10},{13,11},{18,20},{1... | collective-permute-start | bytes 1572872 | tf_op jit(solution)/shard_map/ppermute | solution.py:512
  6.3 14.4 %collective-permute-start.2 = (bf16[32,8192]{1,0:T(8,128)(2,1)S(1)}, bf16[32,8192]{1,0:T(8,128)(2,1)S(1)}, u32[]{:S(2)}, u32[]{:S(2)}) collective-permute-start(bf16[32,8192]{1,0:T(8,128)(2,1)S(1)} %slice_bitcast_fusion.refs_0_), channel_id=1, source_target_pairs={{0,1},{1,0},{2,3},{3,2},{4,5},{5,4},{6,7},{7,6},{8,9},{9,8},{10,11... | collective-permute-start | bytes 1572872 | tf_op jit(solution)/shard_map/ppermute | solution.py:512
  8.9 26.8 %collective-permute-start.3 = (bf16[32,8192]{1,0:T(8,128)(2,1)S(1)}, bf16[32,8192]{1,0:T(8,128)(2,1)S(1)}, u32[]{:S(2)}, u32[]{:S(2)}) collective-permute-start(bf16[32,8192]{1,0:T(8,128)(2,1)S(1)} %slice.11.refs_1_), channel_id=1, source_target_pairs={{0,2},{1,3},{2,0},{3,1},{4,6},{5,7},{6,4},{7,5},{8,10},{9,11},{10,... | collective-permute-start | bytes 1572872 | tf_op jit(solution)/shard_map/ppermute | solution.py:512
  12.6 24.8 %collective-permute-start.4 = (bf16[32,8192]{1,0:T(8,128)(2,1)S(1)}, bf16[32,8192]{1,0:T(8,128)(2,1)}, u32[]{:S(2)}, u32[]{:S(2)}) collective-permute-start(bf16[32,8192]{1,0:T(8,128)(2,1)S(1)} %slice.11.refs_1_), channel_id=1, source_target_pairs={{2,4},{3,5},{4,2},{5,3},{10,12},{11,13},{12,10},{13,11},{18,20},{1... | collective-permute-start | bytes 1572872 | tf_op jit(solution)/shard_map/ppermute | solution.py:512
  17.6 19.8 %collective-permute-start.5 = (bf16[32,8192]{1,0:T(8,128)(2,1)S(1)}, bf16[32,8192]{1,0:T(8,128)(2,1)}, u32[]{:S(2)}, u32[]{:S(2)}) collective-permute-start(bf16[32,8192]{1,0:T(8,128)(2,1)S(1)} %slice.11.refs_1_), channel_id=1, source_target_pairs={{0,1},{1,0},{2,3},{3,2},{4,5},{5,4},{6,7},{7,6},{8,9},{9,8},{10,11... | collective-permute-start | bytes 1572872 | tf_op jit(solution)/shard_map/ppermute | solution.py:512
  20.7 18.6 %collective-permute-start.6 = (bf16[32,8192]{1,0:T(8,128)(2,1)}, bf16[32,8192]{1,0:T(8,128)(2,1)}, u32[]{:S(2)}, u32[]{:S(2)}) collective-permute-start(bf16[32,8192]{1,0:T(8,128)(2,1)} %collective-permute-done.1), channel_id=1, source_target_pairs={{2,0},{3,1},{4,6},{5,7},{10,8},{11,9},{12,14},{13,15},{18,16},{19,... | collective-permute-start | bytes 1572872 | tf_op jit(solution)/shard_map/ppermute | solution.py:512
  23.8 2.8 %copy-start.1 = (bf16[96,16,2048]{2,1,0:T(8,128)(2,1)S(1)}, bf16[96,16,2048]{2,1,0:T(8,128)(2,1)}, u32[]{:S(2)}) copy-start(bf16[96,16,2048]{2,1,0:T(8,128)(2,1)} %pool.1) | copy-start | bytes 18874372
  26.6 0.8 copy-start.3
  27.4 0.7 copy-start.4
  28.1 0.7 copy-start.5
  28.8 0.7 copy-start.6
  29.5 0.7 copy-start.7
  30.1 10.5 %copy-start = (bf16[8192,1024]{1,0:T(8,128)(2,1)S(1)}, bf16[8192,1024]{1,0:T(8,128)(2,1)}, u32[]{:S(2)}) copy-start(bf16[8192,1024]{1,0:T(8,128)(2,1)} %refs_2_.1) | copy-start | bytes 50331652
  35.0 15.7 %collective-permute-start.7 = (bf16[32,8192]{1,0:T(8,128)(2,1)S(1)}, bf16[32,8192]{1,0:T(8,128)(2,1)S(1)}, u32[]{:S(2)}, u32[]{:S(2)}) collective-permute-start(bf16[32,8192]{1,0:T(8,128)(2,1)S(1)} %collective-permute-done.refs_2_), channel_id=1, source_target_pairs={{2,4},{3,5},{4,2},{5,3},{10,12},{11,13},{12,10},{13,11},{18,20},{1... | collective-permute-start | bytes 1572872 | tf_op jit(solution)/shard_map/ppermute | solution.py:512
  35.7 15.1 %collective-permute-start.8 = (bf16[32,8192]{1,0:T(8,128)(2,1)S(1)}, bf16[32,8192]{1,0:T(8,128)(2,1)S(1)}, u32[]{:S(2)}, u32[]{:S(2)}) collective-permute-start(bf16[32,8192]{1,0:T(8,128)(2,1)S(1)} %collective-permute-done.refs_2_), channel_id=1, source_target_pairs={{0,1},{1,0},{2,3},{3,2},{4,5},{5,4},{6,7},{7,6},{8,9},{9,8},{10,11... | collective-permute-start | bytes 1572872 | tf_op jit(solution)/shard_map/ppermute | solution.py:512
  37.4 23.2 %collective-permute-start.10 = (bf16[32,8192]{1,0:T(8,128)(2,1)S(1)}, bf16[32,8192]{1,0:T(8,128)(2,1)S(1)}, u32[]{:S(2)}, u32[]{:S(2)}) collective-permute-start(bf16[32,8192]{1,0:T(8,128)(2,1)S(1)} %collective-permute-done.3.refs_3_), channel_id=1, source_target_pairs={{2,4},{3,5},{4,2},{5,3},{10,12},{11,13},{12,10},{13,11},{18,20},{1... | collective-permute-start | bytes 1572872 | tf_op jit(solution)/shard_map/ppermute | solution.py:512
  38.1 22.5 %collective-permute-start.11 = (bf16[32,8192]{1,0:T(8,128)(2,1)S(1)}, bf16[32,8192]{1,0:T(8,128)(2,1)S(1)}, u32[]{:S(2)}, u32[]{:S(2)}) collective-permute-start(bf16[32,8192]{1,0:T(8,128)(2,1)S(1)} %collective-permute-done.3.refs_3_), channel_id=1, source_target_pairs={{0,1},{1,0},{2,3},{3,2},{4,5},{5,4},{6,7},{7,6},{8,9},{9,8},{10,11... | collective-permute-start | bytes 1572872 | tf_op jit(solution)/shard_map/ppermute | solution.py:512
  39.3 17.8 %collective-permute-start.9 = (bf16[32,8192]{1,0:T(8,128)(2,1)}, bf16[32,8192]{1,0:T(8,128)(2,1)S(1)}, u32[]{:S(2)}, u32[]{:S(2)}) collective-permute-start(bf16[32,8192]{1,0:T(8,128)(2,1)} %collective-permute-done.4), channel_id=1, source_target_pairs={{2,0},{3,1},{4,6},{5,7},{10,8},{11,9},{12,14},{13,15},{18,16},{19,... | collective-permute-start | bytes 1572872 | tf_op jit(solution)/shard_map/ppermute | solution.py:512
  40.6 2.2 %copy-start.2 = (bf16[8192,256]{1,0:T(8,128)(2,1)S(1)}, bf16[8192,256]{1,0:T(8,128)(2,1)}, u32[]{:S(2)}) copy-start(bf16[8192,256]{1,0:T(8,128)(2,1)} %refs_3_.1) | copy-start | bytes 12582916
  50.7 58.8 %collective-permute-start.18 = (bf16[64,256]{1,0:T(8,128)(2,1)S(1)}, bf16[64,256]{1,0:T(8,128)(2,1)S(1)}, u32[]{:S(2)}, u32[]{:S(2)}) collective-permute-start(bf16[64,256]{1,0:T(8,128)(2,1)S(1)} %get-tuple-element.56.refs_4_), channel_id=1, source_target_pairs={{0,8},{1,9},{2,10},{3,11},{4,12},{5,13},{6,14},{7,15},{8,0},{9,1},... | collective-permute-start | bytes 98312 | tf_op jit(solution)/shard_map/ppermute | solution.py:531
  50.8 61.2 %collective-permute-start.19 = (bf16[64,256]{1,0:T(8,128)(2,1)S(1)}, bf16[64,256]{1,0:T(8,128)(2,1)S(1)}, u32[]{:S(2)}, u32[]{:S(2)}) collective-permute-start(bf16[64,256]{1,0:T(8,128)(2,1)S(1)} %get-tuple-element.58.refs_6_), channel_id=1, source_target_pairs={{0,9},{1,8},{2,11},{3,10},{4,13},{5,12},{6,15},{7,14},{8,1},{9,0},... | collective-permute-start | bytes 98312 | tf_op jit(solution)/shard_map/ppermute | solution.py:531
  57.1 55.3 %collective-permute-start.20 = (bf16[64,256]{1,0:T(8,128)(2,1)S(1)}, bf16[64,256]{1,0:T(8,128)(2,1)S(1)}, u32[]{:S(2)}, u32[]{:S(2)}) collective-permute-start(bf16[64,256]{1,0:T(8,128)(2,1)S(1)} %get-tuple-element.57.refs_5_), channel_id=1, source_target_pairs={{0,10},{1,11},{2,8},{3,9},{4,14},{5,15},{6,12},{7,13},{8,2},{9,3},... | collective-permute-start | bytes 98312 | tf_op jit(solution)/shard_map/ppermute | solution.py:531
  60.6 16.1 %collective-permute-start.12 = (bf16[32,8192]{1,0:T(8,128)(2,1)S(1)}, bf16[32,8192]{1,0:T(8,128)(2,1)S(1)}, u32[]{:S(2)}, u32[]{:S(2)}) collective-permute-start(bf16[32,8192]{1,0:T(8,128)(2,1)S(1)} %collective-permute-done.7), channel_id=1, source_target_pairs={{2,0},{3,1},{4,6},{5,7},{10,8},{11,9},{12,14},{13,15},{18,16},{19,... | collective-permute-start | bytes 1572872 | tf_op jit(solution)/shard_map/ppermute | solution.py:512
  63.2 14.8 %collective-permute-start.13 = (bf16[32,8192]{1,0:T(8,128)(2,1)S(1)}, bf16[32,8192]{1,0:T(8,128)(2,1)S(1)}, u32[]{:S(2)}, u32[]{:S(2)}) collective-permute-start(bf16[32,8192]{1,0:T(8,128)(2,1)S(1)} %broadcast_select_fusion.3.refs_0_), channel_id=1, source_target_pairs={{0,1},{1,0},{2,3},{3,2},{4,5},{5,4},{6,7},{7,6},{8,9},{9,8},{10,11... | collective-permute-start | bytes 1572872 | tf_op jit(solution)/shard_map/ppermute | solution.py:512
  76.8 14.1 %collective-permute-start.14 = (bf16[32,8192]{1,0:T(8,128)(2,1)S(1)}, bf16[32,8192]{1,0:T(8,128)(2,1)S(1)}, u32[]{:S(2)}, u32[]{:S(2)}) collective-permute-start(bf16[32,8192]{1,0:T(8,128)(2,1)S(1)} %collective-permute-done.10), channel_id=1, source_target_pairs={{2,0},{3,1},{4,6},{5,7},{10,8},{11,9},{12,14},{13,15},{18,16},{19,... | collective-permute-start | bytes 1572872 | tf_op jit(solution)/shard_map/ppermute | solution.py:512
  78.1 12.9 %collective-permute-start.15 = (bf16[32,8192]{1,0:T(8,128)(2,1)S(1)}, bf16[32,8192]{1,0:T(8,128)(2,1)S(1)}, u32[]{:S(2)}, u32[]{:S(2)}) collective-permute-start(bf16[32,8192]{1,0:T(8,128)(2,1)S(1)} %broadcast_select_fusion.2.refs_1_), channel_id=1, source_target_pairs={{0,1},{1,0},{2,3},{3,2},{4,5},{5,4},{6,7},{7,6},{8,9},{9,8},{10,11... | collective-permute-start | bytes 1572872 | tf_op jit(solution)/shard_map/ppermute | solution.py:512
  91.0 12.2 %collective-permute-start.16 = (bf16[32,8192]{1,0:T(8,128)(2,1)S(1)}, bf16[32,8192]{1,0:T(8,128)(2,1)S(1)}, u32[]{:S(2)}, u32[]{:S(2)}) collective-permute-start(bf16[32,8192]{1,0:T(8,128)(2,1)S(1)} %collective-permute-done.13.refs_2_), channel_id=1, source_target_pairs={{0,2},{1,3},{2,0},{3,1},{4,6},{5,7},{6,4},{7,5},{8,10},{9,11},{10,... | collective-permute-start | bytes 1572872 | tf_op jit(solution)/shard_map/ppermute | solution.py:512
  93.9 10.8 %collective-permute-start.17 = (bf16[32,8192]{1,0:T(8,128)(2,1)S(1)}, bf16[32,8192]{1,0:T(8,128)(2,1)S(1)}, u32[]{:S(2)}, u32[]{:S(2)}) collective-permute-start(bf16[32,8192]{1,0:T(8,128)(2,1)S(1)} %broadcast_select_fusion.refs_1_), channel_id=1, source_target_pairs={{0,1},{1,0},{2,3},{3,2},{4,5},{5,4},{6,7},{7,6},{8,9},{9,8},{10,11... | collective-permute-start | bytes 1572872 | tf_op jit(solution)/shard_map/ppermute | solution.py:512
  103.2 17.2 %collective-permute-start.21 = (bf16[64,256]{1,0:T(8,128)(2,1)S(1)}, bf16[64,256]{1,0:T(8,128)(2,1)S(1)}, u32[]{:S(2)}, u32[]{:S(2)}) collective-permute-start(bf16[64,256]{1,0:T(8,128)(2,1)S(1)} %get-tuple-element.60.refs_8_), channel_id=1, source_target_pairs={{0,11},{1,10},{2,9},{3,8},{4,15},{5,14},{6,13},{7,12},{8,3},{9,2},... | collective-permute-start | bytes 98312 | tf_op jit(solution)/shard_map/ppermute | solution.py:531
  104.6 15.7 %collective-permute-start.22 = (bf16[64,256]{1,0:T(8,128)(2,1)S(1)}, bf16[64,256]{1,0:T(8,128)(2,1)S(1)}, u32[]{:S(2)}, u32[]{:S(2)}) collective-permute-start(bf16[64,256]{1,0:T(8,128)(2,1)S(1)} %get-tuple-element.59.refs_7_), channel_id=1, source_target_pairs={{0,12},{1,13},{2,14},{3,15},{4,8},{5,9},{6,10},{7,11},{8,4},{9,5},... | collective-permute-start | bytes 98312 | tf_op jit(solution)/shard_map/ppermute | solution.py:531
  109.5 10.8 %collective-permute-start.23 = (bf16[64,256]{1,0:T(8,128)(2,1)S(1)}, bf16[64,256]{1,0:T(8,128)(2,1)S(1)}, u32[]{:S(2)}, u32[]{:S(2)}) collective-permute-start(bf16[64,256]{1,0:T(8,128)(2,1)S(1)} %get-tuple-element.62.refs_10_), channel_id=1, source_target_pairs={{0,13},{1,12},{2,15},{3,14},{4,9},{5,8},{6,11},{7,10},{8,5},{9,4},... | collective-permute-start | bytes 98312 | tf_op jit(solution)/shard_map/ppermute | solution.py:531
  111.9 8.4 %collective-permute-start.24 = (bf16[64,256]{1,0:T(8,128)(2,1)S(1)}, bf16[64,256]{1,0:T(8,128)(2,1)S(1)}, u32[]{:S(2)}, u32[]{:S(2)}) collective-permute-start(bf16[64,256]{1,0:T(8,128)(2,1)S(1)} %get-tuple-element.61.refs_9_), channel_id=1, source_target_pairs={{0,14},{1,15},{2,12},{3,13},{4,10},{5,11},{6,8},{7,9},{8,6},{9,7},... | collective-permute-start | bytes 98312 | tf_op jit(solution)/shard_map/ppermute | solution.py:531
  112.4 7.9 %collective-permute-start.25 = (bf16[64,256]{1,0:T(8,128)(2,1)S(1)}, bf16[64,256]{1,0:T(8,128)(2,1)S(1)}, u32[]{:S(2)}, u32[]{:S(2)}) collective-permute-start(bf16[64,256]{1,0:T(8,128)(2,1)S(1)} %get-tuple-element.63.refs_11_), channel_id=1, source_target_pairs={{0,15},{1,14},{2,13},{3,12},{4,11},{5,10},{6,9},{7,8},{8,7},{9,6},... | collective-permute-start | bytes 98312 | tf_op jit(solution)/shard_map/ppermute | solution.py:531

commit v2 on v1

--- a/solution.py
+++ b/solution.py
@@ -259,27 +259,12 @@
     )(member, *queries, *kvs)
 
 
-def decode_old_kernel(
-    tables,
-    lengths,
-    slots,
-    query_ref,
-    own_ref,
-    pool,
-    acc_ref,
-    state_ref,
-    queries,
-    allowed,
-    limits,
-    scores,
-    own,
-):
+def decode_prepare_kernel(tables, lengths, slots, query_ref, queries, allowed, limits):
     rows, pages = tables.shape
     handed = slots.shape[1]
-    total_pages, page, width = pool.shape
+    page = allowed.shape[0] // handed
     columns = queries.shape[1]
     per_head = columns // KVH
-    scale = HD ** (-0.5) * LOG2E
     lane = lax.broadcasted_iota(jnp.int32, (1, columns), 1)
     lane_row = lane % rows
 
@@ -312,6 +297,36 @@
             lane // per_head == h, turned_q, jnp.zeros_like(turned_q)
         )
         queries[(2 * h + 1) * HD : (2 * h + 2) * HD, :] = jnp.zeros((HD, columns), jnp.bfloat16)
+
+
+def decode_prepare(pool, tables, lengths, slots, queries):
+    rows = tables.shape[0]
+    columns = KVH * GROUP * rows
+    total_pages, page, width = pool.shape
+    vmem = pl.BlockSpec(memory_space=pltpu.VMEM)
+    smem = pl.BlockSpec(memory_space=pltpu.SMEM)
+    return pl.pallas_call(
+        decode_prepare_kernel,
+        out_shape=[
+            jax.ShapeDtypeStruct((width, columns), jnp.bfloat16),
+            jax.ShapeDtypeStruct((slots.shape[1] * page, columns), jnp.float32),
+            jax.ShapeDtypeStruct((total_pages, columns), jnp.int32),
+        ],
+        in_specs=[smem, smem, smem, vmem],
+        out_specs=[vmem] * 3,
+        compiler_params=pltpu.CompilerParams(vmem_limit_bytes=VMEM_LIMIT),
+        cost_estimate=pl.CostEstimate(flops=10**10, bytes_accessed=1000, transcendentals=0),
+        name="decode_prepare",
+    )(tables, lengths, slots, queries)
+
+
+def decode_old_kernel(queries, limits, own_ref, pool, acc_ref, state_ref, scores, own):
+    rows = own_ref.shape[0]
+    total_pages, page, width = pool.shape
+    columns = queries.shape[1]
+    per_head = columns // KVH
+    scale = HD ** (-0.5) * LOG2E
+    lane_row = lax.broadcasted_iota(jnp.int32, (1, columns), 1) % rows
 
     own[...] = jnp.zeros_like(own)
     own[0:rows, :] = own_ref[...]
@@ -361,31 +376,27 @@
     state_ref[1:2, :] = total
 
 
-def decode_old(pool, tables, lengths, slots, queries, new_kv):
-    rows = tables.shape[0]
-    columns = KVH * GROUP * rows
+def decode_old(pool, queries, limits, new_kv):
+    rows = new_kv.shape[0]
+    columns = queries.shape[1]
     total_pages, page, width = pool.shape
     vmem = pl.BlockSpec(memory_space=pltpu.VMEM)
-    smem = pl.BlockSpec(memory_space=pltpu.SMEM)
     return pl.pallas_call(
         decode_old_kernel,
         out_shape=[
             jax.ShapeDtypeStruct((KVH, GROUP * rows, HD), jnp.float32),
             jax.ShapeDtypeStruct((2, columns), jnp.float32),
-            jax.ShapeDtypeStruct((width, columns), jnp.bfloat16),
-            jax.ShapeDtypeStruct((slots.shape[1] * page, columns), jnp.float32),
         ],
-        in_specs=[smem, smem, smem, vmem, vmem, vmem],
-        out_specs=[vmem] * 4,
+        in_specs=[vmem] * 4,
+        out_specs=[vmem] * 2,
         scratch_shapes=[
-            pltpu.VMEM((total_pages, columns), jnp.int32),
             pltpu.VMEM((total_pages * page, columns), jnp.float32),
             pltpu.VMEM((page, width), jnp.bfloat16),
         ],
         compiler_params=pltpu.CompilerParams(vmem_limit_bytes=VMEM_LIMIT),
-        cost_estimate=pl.CostEstimate(flops=5000000000, bytes_accessed=1000, transcendentals=0),
+        cost_estimate=pl.CostEstimate(flops=5 * 10**9, bytes_accessed=1000, transcendentals=0),
         name="decode_old",
-    )(tables, lengths, slots, queries, new_kv, pool)
+    )(queries, limits, new_kv, pool)
 
 
 def decode_new_kernel(heads_of, member, q_ref, allowed_ref, acc_ref, state_ref, *refs):
@@ -499,10 +510,8 @@
     kv_pair = kv_job[:4] + (2,)
     bar = lax.optimization_barrier
 
-    def old_state():
-        return decode_old(
-            kv_pool, page_table, cache_lengths, handoff_slot, dec_query, dec_new_kv
-        )
+    def prepared():
+        return decode_prepare(kv_pool, page_table, cache_lengths, handoff_slot, dec_query)
 
     if members == 8 and headmates == 1 and block_rows % 32 == 0:
         half = block_rows // 2
@@ -537,21 +546,18 @@
             y[c] = move(own[c], side)
             e1[c] = move(own[c], outer)
             e2[c] = move(own[c], inner)
-        state = old_state()
-        piece = {}
+        dec_heads, allowed, limits = prepared()
+        q0, kv0 = project([tokens], lambda m: [m * block_rows], member_ref, gain, [q_job, kv_job])
+        piece = {0: hand(kv0, 0)}
         for c in range(2):
             e1[c], e2[c], y[c] = bar((e1[c], e2[c], y[c]))
             e1[2 + c] = move(e2[c], outward)
             e2[2 + c] = move(e1[c], inner)
             y[2 + c] = move(e1[c], side)
-        qa, kv0, kv2, kv1 = project(
-            [*own, e1[0], e1[1], y[0], y[1]],
-            place((0, 2, 1)),
-            member_ref,
-            gain,
-            [q_job, kv_job[:4] + (3,)],
-        )
-        piece[0], piece[2], piece[1] = hand(kv0, 0), hand(kv2, 2), hand(kv1, 1)
+        qa, kv2, kv1 = project(
+            [e1[0], e1[1], y[0], y[1]], place((2, 1)), member_ref, gain, [q_job, kv_pair]
+        )
+        piece[2], piece[1] = hand(kv2, 2), hand(kv1, 1)
         two, three = {}, {}
         for c in range(2):
             e1[2 + c], e2[2 + c], y[2 + c] = bar((e1[2 + c], e2[2 + c], y[2 + c]))
@@ -569,6 +575,7 @@
                 e1[6] = move(y[4], outer)
             else:
                 y[6] = move(three[1], side)
+        state = decode_old(kv_pool, dec_heads, limits, dec_new_kv)
         qc, kv6, kv5 = project(
             [three[0], three[1], y[4], y[5]], place((6, 5)), member_ref, gain, [q_job, kv_pair]
         )
@@ -578,7 +585,7 @@
         piece[7] = hand(kv7, 7)
         (qd,) = project(last, place((7,)), member_ref, gain, [q_job], ready=normed)
         context = attend(
-            [qa, qb, qc, qd],
+            [q0, qa, qb, qc, qd],
             [kv0, kv2, kv1, kv4, kv3, kv6, kv5, kv7],
             [half] * (2 * members),
             place((0, 2, 1, 4, 3, 6, 5, 7)),
@@ -587,7 +594,8 @@
         pieces = [piece[k] for k in range(members)]
         heads_of = lambda m: [jnp.bitwise_xor(m, k) for k in range(members)]
     else:
-        state = old_state()
+        dec_heads, allowed, limits = prepared()
+        state = decode_old(kv_pool, dec_heads, limits, dec_new_kv)
         moving = tokens
         queries, local_kvs, order = [], [], []
         group, group_steps = [tokens], [0]
@@ -626,7 +634,7 @@
         pieces = [arrived[:, k * 2 * HD : (k + 1) * 2 * HD] for k in range(KVH)]
         heads_of = lambda m: list(range(KVH))
 
-    decoded = decode_new(pieces, heads_of, member_ref, rows, *state)
+    decoded = decode_new(pieces, heads_of, member_ref, rows, *state, dec_heads, allowed)
     return (context[None], decoded)
 
 

time: 122 us -> 136 us (1.11)
  local copies, waits for them, and re-layouts: 11.4 us -> 27.2 us
  starting transfers between devices: 38.9 us -> 35.7 us
  Pallas kernels: 32.1 us -> 34.8 us
  waiting for transfers between devices: 36.1 us -> 33.8 us
    unnamed x16 -> x32, local copies, waits for them, and re-layouts: 8.51 us -> 23.5 us
    ppermute x18, waiting for transfers between devices: 36 us -> 32.5 us  [move(): return lax.ppermute(value, 'tp', pairs)]
    pallas_call x5 -> x6, Pallas kernels: 22.3 us -> 24.9 us  [project(): pl.pallas_call(functools.partial(project_kernel, chunk_rows, [job[3] for...]
    ppermute x8, starting transfers between devices: 12.5 us -> 10.9 us  [hand(): return lax.ppermute(kv, ('role', 'tp'), pairs)]
    pallas_call x1, Pallas kernels: 4.84 us -> 3.25 us  [decode_old(): pl.pallas_call(decode_old_kernel, out_shape=[jax.ShapeDtypeStruct((KVH, G...]
    ppermute x18, starting transfers between devices: 26.4 us -> 24.8 us  [move(): return lax.ppermute(value, 'tp', pairs)]
    pallas_call x0 -> x1, Pallas kernels: none -> 1.54 us  [decode_prepare(): pl.pallas_call(decode_prepare_kernel, out_shape=[jax.ShapeDtypeStruct((wi...]
  transfers between devices with their start and end apart: 26 -> 26, of which waited for: 9 -> 6; matrix products, arithmetic and copies ran while one was open for 3% -> 3% of each run, Pallas kernels for 25% -> 25%
where the time goes in v2:
time: 136 us; the launch traced here: 135 us
  starting transfers between devices  35.7 us (26%)
  Pallas kernels  34.8 us (26%)
  waiting for transfers between devices  33.8 us (25%)
  local copies, waits for them, and re-layouts  27.2 us (20%)
  other arithmetic  2.32 us (2%)
    ppermute x18, waiting for transfers between devices, move(): return lax.ppermute(value, 'tp', pairs)  32.5 us
    pallas_call x6, Pallas kernels, project(): pl.pallas_call(functools.partial(project_kernel, chunk_rows, [job[3] for...  24.9 us
    ppermute x18, starting transfers between devices, move(): return lax.ppermute(value, 'tp', pairs)  24.8 us
    unnamed x32, local copies, waits for them, and re-layouts  23.5 us
    ppermute x8, starting transfers between devices, hand(): return lax.ppermute(kv, ('role', 'tp'), pairs)  10.9 us
    pallas_call x1, Pallas kernels, attend(): pl.pallas_call(functools.partial(attend_kernel, tuple(chunk_rows), len(qu...  3.69 us
    pallas_call x1, Pallas kernels, decode_old(): pl.pallas_call(decode_old_kernel, out_shape=[jax.ShapeDtypeStruct((KVH, G...  3.25 us
  transfers between devices with their start and end apart: 26, of which 6 were waited for; matrix products, arithmetic and copies ran while one was open for 3% of the time, Pallas kernels for 25%

profile of v2, /device:TPU:0, one launch (start us, length us, event | category | flops | bytes accessed | tf_op | source)
XLA Modules:
  0.0 134.7 jit_solution(9387933560724721413)
XLA Ops:
  0.6 1.9 %slice_bitcast_fusion = bf16[32,8192]{1,0:T(8,128)(2,1)} fusion(bf16[1,64,8192]{2,1,0:T(8,128)(2,1)} %param.10), kind=kLoop, calls=%fused_computation | loop fusion | bytes 1048576 | tf_op jit(solution)/shard_map/slice | solution.py:542
  2.5 3.1 %collective-permute-start = (bf16[32,8192]{1,0:T(8,128)(2,1)}, bf16[32,8192]{1,0:T(8,128)(2,1)}, u32[]{:S(2)}, u32[]{:S(2)}) collective-permute-start(bf16[32,8192]{1,0:T(8,128)(2,1)} %slice_bitcast_fusion), channel_id=1, source_target_pairs={{0,2},{1,3},{2,0},{3,1},{4,6},{5,7},{6,4},{7,5},{8,10},{9,11},{10,... | collective-permute-start | bytes 1572872 | tf_op jit(solution)/shard_map/ppermute | solution.py:521
  5.6 1.5 %collective-permute-start.1 = (bf16[32,8192]{1,0:T(8,128)(2,1)}, bf16[32,8192]{1,0:T(8,128)(2,1)}, u32[]{:S(2)}, u32[]{:S(2)}) collective-permute-start(bf16[32,8192]{1,0:T(8,128)(2,1)} %slice_bitcast_fusion), channel_id=1, source_target_pairs={{2,4},{3,5},{4,2},{5,3},{10,12},{11,13},{12,10},{13,11},{18,20},{1... | collective-permute-start | bytes 1572872 | tf_op jit(solution)/shard_map/ppermute | solution.py:521
  7.0 1.5 %collective-permute-start.2 = (bf16[32,8192]{1,0:T(8,128)(2,1)}, bf16[32,8192]{1,0:T(8,128)(2,1)}, u32[]{:S(2)}, u32[]{:S(2)}) collective-permute-start(bf16[32,8192]{1,0:T(8,128)(2,1)} %slice_bitcast_fusion), channel_id=1, source_target_pairs={{0,1},{1,0},{2,3},{3,2},{4,5},{5,4},{6,7},{7,6},{8,9},{9,8},{10,11... | collective-permute-start | bytes 1572872 | tf_op jit(solution)/shard_map/ppermute | solution.py:521
  8.5 1.9 %slice.11 = bf16[32,8192]{1,0:T(8,128)(2,1)} slice(bf16[64,8192]{1,0:T(8,128)(2,1)} %bitcast.5), slice={[32:64], [0:8192]} | slice | bytes 1048576 | tf_op jit(solution)/shard_map/slice | solution.py:543
  10.4 3.7 %collective-permute-start.3 = (bf16[32,8192]{1,0:T(8,128)(2,1)}, bf16[32,8192]{1,0:T(8,128)(2,1)S(1)}, u32[]{:S(2)}, u32[]{:S(2)}) collective-permute-start(bf16[32,8192]{1,0:T(8,128)(2,1)} %slice.11), channel_id=1, source_target_pairs={{0,2},{1,3},{2,0},{3,1},{4,6},{5,7},{6,4},{7,5},{8,10},{9,11},{10,... | collective-permute-start | bytes 1572872 | tf_op jit(solution)/shard_map/ppermute | solution.py:521
  14.1 1.5 %collective-permute-start.4 = (bf16[32,8192]{1,0:T(8,128)(2,1)}, bf16[32,8192]{1,0:T(8,128)(2,1)}, u32[]{:S(2)}, u32[]{:S(2)}) collective-permute-start(bf16[32,8192]{1,0:T(8,128)(2,1)} %slice.11), channel_id=1, source_target_pairs={{2,4},{3,5},{4,2},{5,3},{10,12},{11,13},{12,10},{13,11},{18,20},{1... | collective-permute-start | bytes 1572872 | tf_op jit(solution)/shard_map/ppermute | solution.py:521
  15.6 0.8 copy-done.6
  16.4 0.7 copy-done.8
  17.1 0.7 copy-done.9
  17.7 0.7 copy-done.10
  18.4 1.5 %decode_prepare.1 = (bf16[2048,256]{1,0:T(8,128)(2,1)S(1)}, f32[64,256]{1,0:T(8,128)S(1)}, s32[96,256]{1,0:T(8,128)S(1)}) custom-call(s32[4,24]{1,0:T(4,128)S(1)} %copy-done.8, s32[4]{0:T(128)S(1)} %copy-done.9, s32[1,4]{1,0:T(1,128)S(1)} %copy-done.10, bf16[4,8192]{1,0:T(4,128)(2,1)S(1)} %copy-done.6), custom_call_target="tpu_custom_call" | custom-call | flops 10000000000 | bytes 1000 | tf_op jit(solution)/shard_map/decode_prepare/pallas_call | solution.py:308
  20.0 1.0 fusion
  21.0 0.0 collective-permute-done.refs_0_
  21.0 0.6 collective-permute-start.5
  21.6 1.3 collective-permute-start.6
  22.9 0.0 copy-start.1
  22.9 5.8 %copy-done.1 = bf16[8192,1024]{1,0:T(8,128)(2,1)S(1)} copy-done((bf16[8192,1024]{1,0:T(8,128)(2,1)S(1)}, bf16[8192,1024]{1,0:T(8,128)(2,1)}, u32[]{:S(2)}) %copy-start.1) | copy-done | bytes 16777240
  28.7 2.2 %copy-done.4 = bf16[8192,256]{1,0:T(8,128)(2,1)S(1)} copy-done((bf16[8192,256]{1,0:T(8,128)(2,1)S(1)}, bf16[8192,256]{1,0:T(8,128)(2,1)}, u32[]{:S(2)}) %copy-start.4) | copy-done | bytes 4194328
  30.9 4.6 %project.6 = (bf16[64,1024]{1,0:T(8,128)(2,1)S(1)}, bf16[64,256]{1,0:T(8,128)(2,1)S(1)}) custom-call(s32[1]{0:T(128)} %bitcast.member, bf16[64,8192]{1,0:T(8,128)(2,1)S(1)} %bitcast.6, bf16[1,8192]{1,0:T(2,128)(2,1)S(1)} %reshape.56.refs_1_.refs_4_.refs_2_, bf16[8192,1024]{1,0:T(8,128)(2,1)S(1)} %copy-done.1, ...), custom_call_target="tpu_custom_call" | custom-call | flops 10000000000 | bytes 1000 | tf_op jit(solution)/shard_map/project/pallas_call | solution.py:165
  35.5 0.0 copy-start.3
  35.5 2.8 %copy-done.3 = bf16[96,16,2048]{2,1,0:T(8,128)(2,1)S(1)} copy-done((bf16[96,16,2048]{2,1,0:T(8,128)(2,1)S(1)}, bf16[96,16,2048]{2,1,0:T(8,128)(2,1)}, u32[]{:S(2)}) %copy-start.3) | copy-done | bytes 6291480
  38.2 3.2 %decode_old.1 = (f32[8,32,128]{2,1,0:T(8,128)S(1)}, f32[2,256]{1,0:T(2,128)S(1)}) custom-call(bf16[2048,256]{1,0:T(8,128)(2,1)S(1)} %get-tuple-element.67.queries.q_ref, s32[96,256]{1,0:T(8,128)S(1)} %get-tuple-element.69.limits, bf16[4,2048]{1,0:T(4,128)(2,1)S(1)} %copy-done.7, bf16[96,16,2048]{2,1,0:T(8,128)(2,1)S(1)} %copy-done.3), custom_call_target="tpu_custom_call" | custom-call | flops 5000000000 | bytes 1000 | tf_op jit(solution)/shard_map/decode_old/pallas_call | solution.py:384
  41.5 0.7 collective-permute-start.7
  42.2 1.6 %collective-permute-start.8 = (bf16[32,8192]{1,0:T(8,128)(2,1)}, bf16[32,8192]{1,0:T(8,128)(2,1)S(1)}, u32[]{:S(2)}, u32[]{:S(2)}) collective-permute-start(bf16[32,8192]{1,0:T(8,128)(2,1)} %collective-permute-done.refs_0_), channel_id=1, source_target_pairs={{0,1},{1,0},{2,3},{3,2},{4,5},{5,4},{6,7},{7,6},{8,9},{9,8},{10,11... | collective-permute-start | bytes 1572872 | tf_op jit(solution)/shard_map/ppermute | solution.py:521
  43.8 0.7 collective-permute-start.10
  44.5 0.6 collective-permute-start.11
  45.1 1.5 %collective-permute-start.9 = (bf16[32,8192]{1,0:T(8,128)(2,1)}, bf16[32,8192]{1,0:T(8,128)(2,1)S(1)}, u32[]{:S(2)}, u32[]{:S(2)}) collective-permute-start(bf16[32,8192]{1,0:T(8,128)(2,1)} %collective-permute-done.4), channel_id=1, source_target_pairs={{2,0},{3,1},{4,6},{5,7},{10,8},{11,9},{12,14},{13,15},{18,16},{19,... | collective-permute-start | bytes 1572872 | tf_op jit(solution)/shard_map/ppermute | solution.py:521
  46.5 0.0 copy-start.2
  46.6 5.8 %copy-done.2 = bf16[8192,1024]{1,0:T(8,128)(2,1)S(1)} copy-done((bf16[8192,1024]{1,0:T(8,128)(2,1)S(1)}, bf16[8192,1024]{1,0:T(8,128)(2,1)}, u32[]{:S(2)}) %copy-start.2) | copy-done | bytes 16777240
  52.3 6.1 %project.7 = (bf16[128,1024]{1,0:T(8,128)(2,1)S(1)}, bf16[64,256]{1,0:T(8,128)(2,1)S(1)}, bf16[64,256]{1,0:T(8,128)(2,1)S(1)}) custom-call(s32[1]{0:T(128)} %bitcast.member, bf16[32,8192]{1,0:T(8,128)(2,1)} %collective-permute-done.refs_0_, bf16[32,8192]{1,0:T(8,128)(2,1)S(1)} %collective-permute-done.3.refs_1_, ...), custom_call_target="tpu_custom_call" | custom-call | flops 10000000000 | bytes 1000 | tf_op jit(solution)/shard_map/project/pallas_call | solution.py:165
  58.4 0.1 collective-permute-start.18
  58.5 1.6 %collective-permute-start.19 = (bf16[64,256]{1,0:T(8,128)(2,1)S(1)}, bf16[64,256]{1,0:T(8,128)(2,1)S(1)}, u32[]{:S(2)}, u32[]{:S(2)}) collective-permute-start(bf16[64,256]{1,0:T(8,128)(2,1)S(1)} %get-tuple-element.61.refs_7_), channel_id=1, source_target_pairs={{0,9},{1,8},{2,11},{3,10},{4,13},{5,12},{6,15},{7,14},{8,1},{9,0},... | collective-permute-start | bytes 98312 | tf_op jit(solution)/shard_map/ppermute | solution.py:540
  60.1 3.5 %collective-permute-done.9 = bf16[32,8192]{1,0:T(8,128)(2,1)S(1)} collective-permute-done((bf16[32,8192]{1,0:T(8,128)(2,1)}, bf16[32,8192]{1,0:T(8,128)(2,1)S(1)}, u32[]{:S(2)}, u32[]{:S(2)}) %collective-permute-start.9) | collective-permute-done | bytes 524320 | tf_op jit(solution)/shard_map/ppermute | solution.py:521
  63.7 5.5 %collective-permute-start.20 = (bf16[64,256]{1,0:T(8,128)(2,1)S(1)}, bf16[64,256]{1,0:T(8,128)(2,1)S(1)}, u32[]{:S(2)}, u32[]{:S(2)}) collective-permute-start(bf16[64,256]{1,0:T(8,128)(2,1)S(1)} %get-tuple-element.60.refs_6_), channel_id=1, source_target_pairs={{0,10},{1,11},{2,8},{3,9},{4,14},{5,15},{6,12},{7,13},{8,2},{9,3},... | collective-permute-start | bytes 98312 | tf_op jit(solution)/shard_map/ppermute | solution.py:540
  69.1 1.3 collective-permute-start.12
  70.4 1.1 broadcast_select_fusion.3.refs_0_
  71.5 0.4 collective-permute-start.13
  72.0 0.1 broadcast_select_fusion.2.refs_1_
  72.0 4.8 %project.8 = (bf16[128,1024]{1,0:T(8,128)(2,1)S(1)}, bf16[64,256]{1,0:T(8,128)(2,1)S(1)}, bf16[64,256]{1,0:T(8,128)(2,1)S(1)}) custom-call(s32[1]{0:T(128)} %bitcast.member, bf16[32,8192]{1,0:T(8,128)(2,1)S(1)} %broadcast_select_fusion.3.refs_0_, bf16[32,8192]{1,0:T(8,128)(2,1)S(1)} %broadcast_select_fusion.2.refs_1_, ...), custom_call_target="tpu_custom_call" | custom-call | flops 10000000000 | bytes 1000 | tf_op jit(solution)/shard_map/project/pallas_call | solution.py:165
  76.8 8.5 %collective-permute-done.12 = bf16[32,8192]{1,0:T(8,128)(2,1)S(1)} collective-permute-done((bf16[32,8192]{1,0:T(8,128)(2,1)S(1)}, bf16[32,8192]{1,0:T(8,128)(2,1)S(1)}, u32[]{:S(2)}, u32[]{:S(2)}) %collective-permute-start.12) | collective-permute-done | bytes 524320 | tf_op jit(solution)/shard_map/ppermute | solution.py:521
  85.3 1.5 %collective-permute-start.14 = (bf16[32,8192]{1,0:T(8,128)(2,1)S(1)}, bf16[32,8192]{1,0:T(8,128)(2,1)S(1)}, u32[]{:S(2)}, u32[]{:S(2)}) collective-permute-start(bf16[32,8192]{1,0:T(8,128)(2,1)S(1)} %collective-permute-done.10), channel_id=1, source_target_pairs={{2,0},{3,1},{4,6},{5,7},{10,8},{11,9},{12,14},{13,15},{18,16},{19,... | collective-permute-start | bytes 1572872 | tf_op jit(solution)/shard_map/ppermute | solution.py:521
  86.8 0.1 collective-permute-start.15
  86.9 0.1 broadcast_select_fusion.1.refs_0_
  87.0 13.6 %collective-permute-done.14 = bf16[32,8192]{1,0:T(8,128)(2,1)S(1)} collective-permute-done((bf16[32,8192]{1,0:T(8,128)(2,1)S(1)}, bf16[32,8192]{1,0:T(8,128)(2,1)S(1)}, u32[]{:S(2)}, u32[]{:S(2)}) %collective-permute-start.14) | collective-permute-done | bytes 524320 | tf_op jit(solution)/shard_map/ppermute | solution.py:521
  100.5 0.1 broadcast_select_fusion.refs_1_
  100.6 3.2 %collective-permute-start.16 = (bf16[32,8192]{1,0:T(8,128)(2,1)S(1)}, bf16[32,8192]{1,0:T(8,128)(2,1)S(1)}, u32[]{:S(2)}, u32[]{:S(2)}) collective-permute-start(bf16[32,8192]{1,0:T(8,128)(2,1)S(1)} %collective-permute-done.13.refs_2_), channel_id=1, source_target_pairs={{0,2},{1,3},{2,0},{3,1},{4,6},{5,7},{6,4},{7,5},{8,10},{9,11},{10,... | collective-permute-start | bytes 1572872 | tf_op jit(solution)/shard_map/ppermute | solution.py:521
  103.8 0.3 collective-permute-start.17
  104.1 4.7 %project.9 = (bf16[128,1024]{1,0:T(8,128)(2,1)S(1)}, bf16[64,256]{1,0:T(8,128)(2,1)S(1)}, bf16[64,256]{1,0:T(8,128)(2,1)S(1)}) custom-call(s32[1]{0:T(128)} %bitcast.member, bf16[32,8192]{1,0:T(8,128)(2,1)S(1)} %broadcast_select_fusion.1.refs_0_, bf16[32,8192]{1,0:T(8,128)(2,1)S(1)} %broadcast_select_fusion.refs_1_, ...), custom_call_target="tpu_custom_call" | custom-call | flops 10000000000 | bytes 1000 | tf_op jit(solution)/shard_map/project/pallas_call | solution.py:165
  108.8 5.5 %collective-permute-done.16.refs_0_ = bf16[32,8192]{1,0:T(8,128)(2,1)S(1)} collective-permute-done((bf16[32,8192]{1,0:T(8,128)(2,1)S(1)}, bf16[32,8192]{1,0:T(8,128)(2,1)S(1)}, u32[]{:S(2)}, u32[]{:S(2)}) %collective-permute-start.16) | collective-permute-done | bytes 524320 | tf_op jit(solution)/shard_map/ppermute | solution.py:521
  114.3 1.5 %collective-permute-done.17.refs_1_ = bf16[32,8192]{1,0:T(8,128)(2,1)S(1)} collective-permute-done((bf16[32,8192]{1,0:T(8,128)(2,1)S(1)}, bf16[32,8192]{1,0:T(8,128)(2,1)S(1)}, u32[]{:S(2)}, u32[]{:S(2)}) %collective-permute-start.17) | collective-permute-done | bytes 524320 | tf_op jit(solution)/shard_map/ppermute | solution.py:521
  115.8 0.1 collective-permute-start.22
  115.9 1.6 %project.10 = (bf16[64,256]{1,0:T(8,128)(2,1)S(1)}, bf16[64,8192]{1,0:T(8,128)(2,1)S(1)}) custom-call(s32[1]{0:T(128)} %bitcast.member, bf16[32,8192]{1,0:T(8,128)(2,1)S(1)} %collective-permute-done.16.refs_0_, bf16[32,8192]{1,0:T(8,128)(2,1)S(1)} %collective-permute-done.17.refs_1_, bf16[1,8192]{1,0:T(2,128)(2,1)S(1)} %reshape.56.refs_1_.refs_4_.refs_2_, ...), custom_call_target="tpu_custom_call" | custom-call | flops 10000000000 | bytes 1000 | tf_op jit(solution)/shard_map/project/pallas_call | solution.py:165
  117.5 0.4 slice-done
  118.0 1.3 slice-done.1
  119.3 1.2 slice-done.2
  120.5 1.2 slice-done.3
  121.6 3.1 %project.11.refs_4_ = bf16[64,1024]{1,0:T(8,128)(2,1)S(1)} custom-call(s32[1]{0:T(128)} %bitcast.member, bf16[64,8192]{1,0:T(8,128)(2,1)S(1)} %get-tuple-element.58.refs_0_, bf16[1,8192]{1,0:T(2,128)(2,1)S(1)} %reshape.56.refs_1_.refs_4_.refs_2_, bf16[8192,1024]{1,0:T(8,128)(2,1)S(1)} %bitcast.8, ...), custom_call_target="tpu_custom_call" | custom-call | flops 10000000000 | bytes 1000 | tf_op jit(solution)/shard_map/project/pallas_call | solution.py:165
  124.8 0.1 collective-permute-start.23
  124.9 2.4 %collective-permute-start.24 = (bf16[64,256]{1,0:T(8,128)(2,1)S(1)}, bf16[64,256]{1,0:T(8,128)(2,1)S(1)}, u32[]{:S(2)}, u32[]{:S(2)}) collective-permute-start(bf16[64,256]{1,0:T(8,128)(2,1)S(1)} %get-tuple-element.64.refs_10_), channel_id=1, source_target_pairs={{0,14},{1,15},{2,12},{3,13},{4,10},{5,11},{6,8},{7,9},{8,6},{9,7},... | collective-permute-start | bytes 98312 | tf_op jit(solution)/shard_map/ppermute | solution.py:540
  127.3 1.2 collective-permute-start.25
  128.5 3.7 %attend.1 = bf16[512,1024]{1,0:T(8,128)(2,1)} custom-call(s32[1]{0:T(128)} %bitcast.member, bf16[64,1024]{1,0:T(8,128)(2,1)S(1)} %get-tuple-element.37.refs_0_, bf16[128,1024]{1,0:T(8,128)(2,1)S(1)} %get-tuple-element.43.refs_1_, bf16[128,1024]{1,0:T(8,128)(2,1)S(1)} %get-tuple-element.52.refs_2_, bf16[128,1024]{1,0:T(8,128)(2,1)S(1)} %get-tuple-element.57.refs_3_, ...), custom_call_target="tpu_custom_call" | custom-call | flops 5000000000 | bytes 1000 | tf_op jit(solution)/shard_map/attend/pallas_call | solution.py:243
  132.2 1.2 collective-permute-done.25.refs_7_
  133.4 1.3 decode_new.1
  (41 shorter events, 0.1 us)
Async XLA Ops:
  2.5 18.5 %collective-permute-start = (bf16[32,8192]{1,0:T(8,128)(2,1)}, bf16[32,8192]{1,0:T(8,128)(2,1)}, u32[]{:S(2)}, u32[]{:S(2)}) collective-permute-start(bf16[32,8192]{1,0:T(8,128)(2,1)} %slice_bitcast_fusion), channel_id=1, source_target_pairs={{0,2},{1,3},{2,0},{3,1},{4,6},{5,7},{6,4},{7,5},{8,10},{9,11},{10,... | collective-permute-start | bytes 1572872 | tf_op jit(solution)/shard_map/ppermute | solution.py:521
  5.6 16.0 %collective-permute-start.1 = (bf16[32,8192]{1,0:T(8,128)(2,1)}, bf16[32,8192]{1,0:T(8,128)(2,1)}, u32[]{:S(2)}, u32[]{:S(2)}) collective-permute-start(bf16[32,8192]{1,0:T(8,128)(2,1)} %slice_bitcast_fusion), channel_id=1, source_target_pairs={{2,4},{3,5},{4,2},{5,3},{10,12},{11,13},{12,10},{13,11},{18,20},{1... | collective-permute-start | bytes 1572872 | tf_op jit(solution)/shard_map/ppermute | solution.py:521
  7.0 14.6 %collective-permute-start.2 = (bf16[32,8192]{1,0:T(8,128)(2,1)}, bf16[32,8192]{1,0:T(8,128)(2,1)}, u32[]{:S(2)}, u32[]{:S(2)}) collective-permute-start(bf16[32,8192]{1,0:T(8,128)(2,1)} %slice_bitcast_fusion), channel_id=1, source_target_pairs={{0,1},{1,0},{2,3},{3,2},{4,5},{5,4},{6,7},{7,6},{8,9},{9,8},{10,11... | collective-permute-start | bytes 1572872 | tf_op jit(solution)/shard_map/ppermute | solution.py:521
  8.5 11.4 %copy-start.11 = (bf16[8192]{0:T(1024)(128)(2,1)S(1)}, bf16[8192]{0:T(1024)(128)(2,1)}, u32[]{:S(2)}) copy-start(bf16[8192]{0:T(1024)(128)(2,1)} %param.11) | copy-start | bytes 49156
  10.4 12.5 %copy-start = (bf16[1,64,8192]{2,1,0:T(8,128)(2,1)S(1)}, bf16[1,64,8192]{2,1,0:T(8,128)(2,1)}, u32[]{:S(2)}) copy-start(bf16[1,64,8192]{2,1,0:T(8,128)(2,1)} %param.10) | copy-start | bytes 3145732
  10.4 31.8 %collective-permute-start.3 = (bf16[32,8192]{1,0:T(8,128)(2,1)}, bf16[32,8192]{1,0:T(8,128)(2,1)S(1)}, u32[]{:S(2)}, u32[]{:S(2)}) collective-permute-start(bf16[32,8192]{1,0:T(8,128)(2,1)} %slice.11), channel_id=1, source_target_pairs={{0,2},{1,3},{2,0},{3,1},{4,6},{5,7},{6,4},{7,5},{8,10},{9,11},{10,... | collective-permute-start | bytes 1572872 | tf_op jit(solution)/shard_map/ppermute | solution.py:521
  14.1 29.7 %collective-permute-start.4 = (bf16[32,8192]{1,0:T(8,128)(2,1)}, bf16[32,8192]{1,0:T(8,128)(2,1)}, u32[]{:S(2)}, u32[]{:S(2)}) collective-permute-start(bf16[32,8192]{1,0:T(8,128)(2,1)} %slice.11), channel_id=1, source_target_pairs={{2,4},{3,5},{4,2},{5,3},{10,12},{11,13},{12,10},{13,11},{18,20},{1... | collective-permute-start | bytes 1572872 | tf_op jit(solution)/shard_map/ppermute | solution.py:521
  15.6 0.8 copy-start.6
  16.4 0.7 copy-start.8
  17.1 0.7 copy-start.9
  17.7 0.7 copy-start.10
  21.0 22.8 %collective-permute-start.5 = (bf16[32,8192]{1,0:T(8,128)(2,1)}, bf16[32,8192]{1,0:T(8,128)(2,1)}, u32[]{:S(2)}, u32[]{:S(2)}) collective-permute-start(bf16[32,8192]{1,0:T(8,128)(2,1)} %slice.11), channel_id=1, source_target_pairs={{0,1},{1,0},{2,3},{3,2},{4,5},{5,4},{6,7},{7,6},{8,9},{9,8},{10,11... | collective-permute-start | bytes 1572872 | tf_op jit(solution)/shard_map/ppermute | solution.py:521
  21.6 23.5 %collective-permute-start.6 = (bf16[32,8192]{1,0:T(8,128)(2,1)}, bf16[32,8192]{1,0:T(8,128)(2,1)}, u32[]{:S(2)}, u32[]{:S(2)}) collective-permute-start(bf16[32,8192]{1,0:T(8,128)(2,1)} %collective-permute-done.1), channel_id=1, source_target_pairs={{2,0},{3,1},{4,6},{5,7},{10,8},{11,9},{12,14},{13,15},{18,16},{19,... | collective-permute-start | bytes 1572872 | tf_op jit(solution)/shard_map/ppermute | solution.py:521
  22.9 5.8 %copy-start.1 = (bf16[8192,1024]{1,0:T(8,128)(2,1)S(1)}, bf16[8192,1024]{1,0:T(8,128)(2,1)}, u32[]{:S(2)}) copy-start(bf16[8192,1024]{1,0:T(8,128)(2,1)} %refs_2_.3) | copy-start | bytes 50331652
  28.7 2.2 %copy-start.4 = (bf16[8192,256]{1,0:T(8,128)(2,1)S(1)}, bf16[8192,256]{1,0:T(8,128)(2,1)}, u32[]{:S(2)}) copy-start(bf16[8192,256]{1,0:T(8,128)(2,1)} %refs_3_.1) | copy-start | bytes 12582916
  30.9 4.6 %copy-start.7 = (bf16[4,2048]{1,0:T(4,128)(2,1)S(1)}, bf16[4,2048]{1,0:T(4,128)(2,1)}, u32[]{:S(2)}) copy-start(bf16[4,2048]{1,0:T(4,128)(2,1)} %own_ref.1) | copy-start | bytes 49156
  35.5 2.8 %copy-start.3 = (bf16[96,16,2048]{2,1,0:T(8,128)(2,1)S(1)}, bf16[96,16,2048]{2,1,0:T(8,128)(2,1)}, u32[]{:S(2)}) copy-start(bf16[96,16,2048]{2,1,0:T(8,128)(2,1)} %pool.1) | copy-start | bytes 18874372
  38.2 8.3 %copy-start.5 = (bf16[8192,256]{1,0:T(8,128)(2,1)S(1)}, bf16[8192,256]{1,0:T(8,128)(2,1)}, u32[]{:S(2)}) copy-start(bf16[8192,256]{1,0:T(8,128)(2,1)} %refs_3_.1) | copy-start | bytes 12582916
  41.5 16.9 %collective-permute-start.7 = (bf16[32,8192]{1,0:T(8,128)(2,1)}, bf16[32,8192]{1,0:T(8,128)(2,1)S(1)}, u32[]{:S(2)}, u32[]{:S(2)}) collective-permute-start(bf16[32,8192]{1,0:T(8,128)(2,1)} %collective-permute-done.refs_0_), channel_id=1, source_target_pairs={{2,4},{3,5},{4,2},{5,3},{10,12},{11,13},{12,10},{13,11},{18,20},{1... | collective-permute-start | bytes 1572872 | tf_op jit(solution)/shard_map/ppermute | solution.py:521
  42.2 16.3 %collective-permute-start.8 = (bf16[32,8192]{1,0:T(8,128)(2,1)}, bf16[32,8192]{1,0:T(8,128)(2,1)S(1)}, u32[]{:S(2)}, u32[]{:S(2)}) collective-permute-start(bf16[32,8192]{1,0:T(8,128)(2,1)} %collective-permute-done.refs_0_), channel_id=1, source_target_pairs={{0,1},{1,0},{2,3},{3,2},{4,5},{5,4},{6,7},{7,6},{8,9},{9,8},{10,11... | collective-permute-start | bytes 1572872 | tf_op jit(solution)/shard_map/ppermute | solution.py:521
  43.8 25.3 %collective-permute-start.10 = (bf16[32,8192]{1,0:T(8,128)(2,1)S(1)}, bf16[32,8192]{1,0:T(8,128)(2,1)S(1)}, u32[]{:S(2)}, u32[]{:S(2)}) collective-permute-start(bf16[32,8192]{1,0:T(8,128)(2,1)S(1)} %collective-permute-done.3.refs_1_), channel_id=1, source_target_pairs={{2,4},{3,5},{4,2},{5,3},{10,12},{11,13},{12,10},{13,11},{18,20},{1... | collective-permute-start | bytes 1572872 | tf_op jit(solution)/shard_map/ppermute | solution.py:521
  44.5 24.6 %collective-permute-start.11 = (bf16[32,8192]{1,0:T(8,128)(2,1)S(1)}, bf16[32,8192]{1,0:T(8,128)(2,1)S(1)}, u32[]{:S(2)}, u32[]{:S(2)}) collective-permute-start(bf16[32,8192]{1,0:T(8,128)(2,1)S(1)} %collective-permute-done.3.refs_1_), channel_id=1, source_target_pairs={{0,1},{1,0},{2,3},{3,2},{4,5},{5,4},{6,7},{7,6},{8,9},{9,8},{10,11... | collective-permute-start | bytes 1572872 | tf_op jit(solution)/shard_map/ppermute | solution.py:521
  45.1 18.6 %collective-permute-start.9 = (bf16[32,8192]{1,0:T(8,128)(2,1)}, bf16[32,8192]{1,0:T(8,128)(2,1)S(1)}, u32[]{:S(2)}, u32[]{:S(2)}) collective-permute-start(bf16[32,8192]{1,0:T(8,128)(2,1)} %collective-permute-done.4), channel_id=1, source_target_pairs={{2,0},{3,1},{4,6},{5,7},{10,8},{11,9},{12,14},{13,15},{18,16},{19,... | collective-permute-start | bytes 1572872 | tf_op jit(solution)/shard_map/ppermute | solution.py:521
  46.5 5.8 %copy-start.2 = (bf16[8192,1024]{1,0:T(8,128)(2,1)S(1)}, bf16[8192,1024]{1,0:T(8,128)(2,1)}, u32[]{:S(2)}) copy-start(bf16[8192,1024]{1,0:T(8,128)(2,1)} %refs_2_.3) | copy-start | bytes 50331652
  58.4 66.4 %collective-permute-start.18 = (bf16[64,256]{1,0:T(8,128)(2,1)S(1)}, bf16[64,256]{1,0:T(8,128)(2,1)S(1)}, u32[]{:S(2)}, u32[]{:S(2)}) collective-permute-start(bf16[64,256]{1,0:T(8,128)(2,1)S(1)} %get-tuple-element.59.refs_5_), channel_id=1, source_target_pairs={{0,8},{1,9},{2,10},{3,11},{4,12},{5,13},{6,14},{7,15},{8,0},{9,1},... | collective-permute-start | bytes 98312 | tf_op jit(solution)/shard_map/ppermute | solution.py:540
  58.5 66.4 %collective-permute-start.19 = (bf16[64,256]{1,0:T(8,128)(2,1)S(1)}, bf16[64,256]{1,0:T(8,128)(2,1)S(1)}, u32[]{:S(2)}, u32[]{:S(2)}) collective-permute-start(bf16[64,256]{1,0:T(8,128)(2,1)S(1)} %get-tuple-element.61.refs_7_), channel_id=1, source_target_pairs={{0,9},{1,8},{2,11},{3,10},{4,13},{5,12},{6,15},{7,14},{8,1},{9,0},... | collective-permute-start | bytes 98312 | tf_op jit(solution)/shard_map/ppermute | solution.py:540
  63.7 63.6 %collective-permute-start.20 = (bf16[64,256]{1,0:T(8,128)(2,1)S(1)}, bf16[64,256]{1,0:T(8,128)(2,1)S(1)}, u32[]{:S(2)}, u32[]{:S(2)}) collective-permute-start(bf16[64,256]{1,0:T(8,128)(2,1)S(1)} %get-tuple-element.60.refs_6_), channel_id=1, source_target_pairs={{0,10},{1,11},{2,8},{3,9},{4,14},{5,15},{6,12},{7,13},{8,2},{9,3},... | collective-permute-start | bytes 98312 | tf_op jit(solution)/shard_map/ppermute | solution.py:540
  69.1 16.1 %collective-permute-start.12 = (bf16[32,8192]{1,0:T(8,128)(2,1)S(1)}, bf16[32,8192]{1,0:T(8,128)(2,1)S(1)}, u32[]{:S(2)}, u32[]{:S(2)}) collective-permute-start(bf16[32,8192]{1,0:T(8,128)(2,1)S(1)} %collective-permute-done.7), channel_id=1, source_target_pairs={{2,0},{3,1},{4,6},{5,7},{10,8},{11,9},{12,14},{13,15},{18,16},{19,... | collective-permute-start | bytes 1572872 | tf_op jit(solution)/shard_map/ppermute | solution.py:521
  71.5 15.2 %collective-permute-start.13 = (bf16[32,8192]{1,0:T(8,128)(2,1)S(1)}, bf16[32,8192]{1,0:T(8,128)(2,1)S(1)}, u32[]{:S(2)}, u32[]{:S(2)}) collective-permute-start(bf16[32,8192]{1,0:T(8,128)(2,1)S(1)} %broadcast_select_fusion.3.refs_0_), channel_id=1, source_target_pairs={{0,1},{1,0},{2,3},{3,2},{4,5},{5,4},{6,7},{7,6},{8,9},{9,8},{10,11... | collective-permute-start | bytes 1572872 | tf_op jit(solution)/shard_map/ppermute | solution.py:521
  85.3 15.3 %collective-permute-start.14 = (bf16[32,8192]{1,0:T(8,128)(2,1)S(1)}, bf16[32,8192]{1,0:T(8,128)(2,1)S(1)}, u32[]{:S(2)}, u32[]{:S(2)}) collective-permute-start(bf16[32,8192]{1,0:T(8,128)(2,1)S(1)} %collective-permute-done.10), channel_id=1, source_target_pairs={{2,0},{3,1},{4,6},{5,7},{10,8},{11,9},{12,14},{13,15},{18,16},{19,... | collective-permute-start | bytes 1572872 | tf_op jit(solution)/shard_map/ppermute | solution.py:521
  86.8 13.8 %collective-permute-start.15 = (bf16[32,8192]{1,0:T(8,128)(2,1)S(1)}, bf16[32,8192]{1,0:T(8,128)(2,1)S(1)}, u32[]{:S(2)}, u32[]{:S(2)}) collective-permute-start(bf16[32,8192]{1,0:T(8,128)(2,1)S(1)} %broadcast_select_fusion.2.refs_1_), channel_id=1, source_target_pairs={{0,1},{1,0},{2,3},{3,2},{4,5},{5,4},{6,7},{7,6},{8,9},{9,8},{10,11... | collective-permute-start | bytes 1572872 | tf_op jit(solution)/shard_map/ppermute | solution.py:521
  100.6 13.7 %collective-permute-start.16 = (bf16[32,8192]{1,0:T(8,128)(2,1)S(1)}, bf16[32,8192]{1,0:T(8,128)(2,1)S(1)}, u32[]{:S(2)}, u32[]{:S(2)}) collective-permute-start(bf16[32,8192]{1,0:T(8,128)(2,1)S(1)} %collective-permute-done.13.refs_2_), channel_id=1, source_target_pairs={{0,2},{1,3},{2,0},{3,1},{4,6},{5,7},{6,4},{7,5},{8,10},{9,11},{10,... | collective-permute-start | bytes 1572872 | tf_op jit(solution)/shard_map/ppermute | solution.py:521
  103.8 12.0 %collective-permute-start.17 = (bf16[32,8192]{1,0:T(8,128)(2,1)S(1)}, bf16[32,8192]{1,0:T(8,128)(2,1)S(1)}, u32[]{:S(2)}, u32[]{:S(2)}) collective-permute-start(bf16[32,8192]{1,0:T(8,128)(2,1)S(1)} %broadcast_select_fusion.refs_1_), channel_id=1, source_target_pairs={{0,1},{1,0},{2,3},{3,2},{4,5},{5,4},{6,7},{7,6},{8,9},{9,8},{10,11... | collective-permute-start | bytes 1572872 | tf_op jit(solution)/shard_map/ppermute | solution.py:521
  114.3 17.8 %collective-permute-start.21 = (bf16[64,256]{1,0:T(8,128)(2,1)S(1)}, bf16[64,256]{1,0:T(8,128)(2,1)S(1)}, u32[]{:S(2)}, u32[]{:S(2)}) collective-permute-start(bf16[64,256]{1,0:T(8,128)(2,1)S(1)} %get-tuple-element.63.refs_9_), channel_id=1, source_target_pairs={{0,11},{1,10},{2,9},{3,8},{4,15},{5,14},{6,13},{7,12},{8,3},{9,2},... | collective-permute-start | bytes 98312 | tf_op jit(solution)/shard_map/ppermute | solution.py:540
  115.8 2.2 %slice-start = ((s8[16777216]{0:T(1024)(128)(4,1)}), s8[4194304]{0:T(1024)(128)(4,1)S(1)}, s32[]{:S(2)}) async-start(s8[16777216]{0:T(1024)(128)(4,1)} %bitcast.7), calls=%async_computation | async-start | bytes 8388608
  115.8 3.5 %slice-start.1 = ((s8[16777216]{0:T(1024)(128)(4,1)}), s8[4194304]{0:T(1024)(128)(4,1)S(1)}, s32[]{:S(2)}) async-start(s8[16777216]{0:T(1024)(128)(4,1)} %bitcast.7), calls=%async_computation.1 | async-start | bytes 8388608
  115.8 4.7 %slice-start.2 = ((s8[16777216]{0:T(1024)(128)(4,1)}), s8[4194304]{0:T(1024)(128)(4,1)S(1)}, s32[]{:S(2)}) async-start(s8[16777216]{0:T(1024)(128)(4,1)} %bitcast.7), calls=%async_computation.2 | async-start | bytes 8388608
  115.8 5.8 %slice-start.3 = ((s8[16777216]{0:T(1024)(128)(4,1)}), s8[4194304]{0:T(1024)(128)(4,1)S(1)}, s32[]{:S(2)}) async-start(s8[16777216]{0:T(1024)(128)(4,1)} %bitcast.7), calls=%async_computation.3 | async-start | bytes 8388608
  115.8 16.4 %collective-permute-start.22 = (bf16[64,256]{1,0:T(8,128)(2,1)S(1)}, bf16[64,256]{1,0:T(8,128)(2,1)S(1)}, u32[]{:S(2)}, u32[]{:S(2)}) collective-permute-start(bf16[64,256]{1,0:T(8,128)(2,1)S(1)} %get-tuple-element.62.refs_8_), channel_id=1, source_target_pairs={{0,12},{1,13},{2,14},{3,15},{4,8},{5,9},{6,10},{7,11},{8,4},{9,5},... | collective-permute-start | bytes 98312 | tf_op jit(solution)/shard_map/ppermute | solution.py:540
  124.8 7.4 %collective-permute-start.23 = (bf16[64,256]{1,0:T(8,128)(2,1)S(1)}, bf16[64,256]{1,0:T(8,128)(2,1)S(1)}, u32[]{:S(2)}, u32[]{:S(2)}) collective-permute-start(bf16[64,256]{1,0:T(8,128)(2,1)S(1)} %get-tuple-element.65.refs_11_), channel_id=1, source_target_pairs={{0,13},{1,12},{2,15},{3,14},{4,9},{5,8},{6,11},{7,10},{8,5},{9,4},... | collective-permute-start | bytes 98312 | tf_op jit(solution)/shard_map/ppermute | solution.py:540
  124.9 7.3 %collective-permute-start.24 = (bf16[64,256]{1,0:T(8,128)(2,1)S(1)}, bf16[64,256]{1,0:T(8,128)(2,1)S(1)}, u32[]{:S(2)}, u32[]{:S(2)}) collective-permute-start(bf16[64,256]{1,0:T(8,128)(2,1)S(1)} %get-tuple-element.64.refs_10_), channel_id=1, source_target_pairs={{0,14},{1,15},{2,12},{3,13},{4,10},{5,11},{6,8},{7,9},{8,6},{9,7},... | collective-permute-start | bytes 98312 | tf_op jit(solution)/shard_map/ppermute | solution.py:540
  127.3 6.1 %collective-permute-start.25 = (bf16[64,256]{1,0:T(8,128)(2,1)S(1)}, bf16[64,256]{1,0:T(8,128)(2,1)S(1)}, u32[]{:S(2)}, u32[]{:S(2)}) collective-permute-start(bf16[64,256]{1,0:T(8,128)(2,1)S(1)} %get-tuple-element.66.refs_12_), channel_id=1, source_target_pairs={{0,15},{1,14},{2,13},{3,12},{4,11},{5,10},{6,9},{7,8},{8,7},{9,6},... | collective-permute-start | bytes 98312 | tf_op jit(solution)/shard_map/ppermute | solution.py:540

commit v3 on v2

--- a/solution.py
+++ b/solution.py
@@ -222,17 +222,17 @@
                 total = total + jnp.sum(body, axis=1, keepdims=True)
             share = 1.0 / total
             mixed = jnp.dot(
-                (edge * share).astype(jnp.bfloat16),
+                edge.astype(jnp.bfloat16),
                 kv_all[low:top, HD:],
                 preferred_element_type=jnp.float32,
             )
             if low:
                 mixed = mixed + jnp.dot(
-                    (body * share).astype(jnp.bfloat16),
+                    body.astype(jnp.bfloat16),
                     kv_all[:low, HD:],
                     preferred_element_type=jnp.float32,
                 )
-            out[low:top, h * HD : (h + 1) * HD] = mixed.astype(jnp.bfloat16)
+            out[low:top, h * HD : (h + 1) * HD] = (mixed * share).astype(jnp.bfloat16)
 
 
 def attend(queries, kvs, chunk_rows, place, member):
@@ -513,8 +513,8 @@
     def prepared():
         return decode_prepare(kv_pool, page_table, cache_lengths, handoff_slot, dec_query)
 
-    if members == 8 and headmates == 1 and block_rows % 32 == 0:
-        half = block_rows // 2
+    if members == 8 and headmates == 1 and block_rows % 64 == 0:
+        half, quarter = block_rows // 2, block_rows // 4
         side, outer, outward, inner = exchange_plan(members, subs)
 
         def move(value, pairs):
@@ -523,11 +523,9 @@
         row = member // 2
         at_end = (row == 0) | (row == 3)
 
-        def place(offsets):
+        def place(*chunks):
             return lambda m: [
-                jnp.bitwise_xor(m, offset) * block_rows + c * half
-                for offset in offsets
-                for c in range(2)
+                jnp.bitwise_xor(m, offset) * block_rows + first for offset, first in chunks
             ]
 
         def hand(kv, offset):
@@ -542,53 +540,74 @@
         own = [tokens[:half]]
         own.append(bar((tokens, own[0]))[0][half:])
         y, e1, e2 = {}, {}, {}
+        y[0] = move(tokens, side)
         for c in range(2):
-            y[c] = move(own[c], side)
             e1[c] = move(own[c], outer)
             e2[c] = move(own[c], inner)
         dec_heads, allowed, limits = prepared()
-        q0, kv0 = project([tokens], lambda m: [m * block_rows], member_ref, gain, [q_job, kv_job])
+        q0, kv0 = project([tokens], place((0, 0)), member_ref, gain, [q_job, kv_job])
         piece = {0: hand(kv0, 0)}
         for c in range(2):
-            e1[c], e2[c], y[c] = bar((e1[c], e2[c], y[c]))
+            if c == 0:
+                e1[0], e2[0] = bar((e1[0], e2[0]))
+            else:
+                e1[1], e2[1], y[0] = bar((e1[1], e2[1], y[0]))
             e1[2 + c] = move(e2[c], outward)
             e2[2 + c] = move(e1[c], inner)
             y[2 + c] = move(e1[c], side)
         qa, kv2, kv1 = project(
-            [e1[0], e1[1], y[0], y[1]], place((2, 1)), member_ref, gain, [q_job, kv_pair]
+            [e1[0], e1[1], y[0]],
+            place((2, 0), (2, half), (1, 0)),
+            member_ref,
+            gain,
+            [q_job, kv_pair],
         )
         piece[2], piece[1] = hand(kv2, 2), hand(kv1, 1)
         two, three = {}, {}
         for c in range(2):
             e1[2 + c], e2[2 + c], y[2 + c] = bar((e1[2 + c], e2[2 + c], y[2 + c]))
             two[c] = jnp.where(at_end, e1[2 + c], e2[2 + c])
-            e1[4 + c] = move(e2[2 + c], outward)
+            if c == 0:
+                e1[4] = move(e2[2], outward)
+            else:
+                e1["5a"] = move(e2[3][:quarter], outward)
+                e1["5b"] = move(e2[3][quarter:], outward)
             y[4 + c] = move(two[c], side)
         qb, kv4, kv3 = project(
-            [two[0], two[1], y[2], y[3]], place((4, 3)), member_ref, gain, [q_job, kv_pair]
+            [two[0], two[1], y[2], y[3]],
+            place((4, 0), (4, half), (3, 0), (3, half)),
+            member_ref,
+            gain,
+            [q_job, kv_pair],
         )
         piece[4], piece[3] = hand(kv4, 4), hand(kv3, 3)
-        for c in range(2):
-            e1[4 + c], y[4 + c] = bar((e1[4 + c], y[4 + c]))
-            three[c] = jnp.where(at_end, e1[4 + c], e2[c])
-            if c == 0:
-                e1[6] = move(y[4], outer)
-            else:
-                y[6] = move(three[1], side)
+        e1[4], y[4] = bar((e1[4], y[4]))
+        three[0] = jnp.where(at_end, e1[4], e2[0])
+        e1[6] = move(y[4], outer)
+        three[1] = jnp.where(at_end, e1["5a"], e2[1][:quarter])
+        y["6a"] = move(three[1], side)
         state = decode_old(kv_pool, dec_heads, limits, dec_new_kv)
+        e1["5b"], y[5], three[1] = bar((e1["5b"], y[5], three[1]))
+        three[2] = jnp.where(at_end, e1["5b"], e2[1][quarter:])
+        y["6b"] = move(three[2], side)
         qc, kv6, kv5 = project(
-            [three[0], three[1], y[4], y[5]], place((6, 5)), member_ref, gain, [q_job, kv_pair]
+            [three[0], three[1], three[2], y[4], y[5]],
+            place((6, 0), (6, half), (6, half + quarter), (5, 0), (5, half)),
+            member_ref,
+            gain,
+            [q_job, kv_pair],
         )
         piece[6], piece[5] = hand(kv6, 6), hand(kv5, 5)
-        last = [e1[6], y[6]]
-        kv7, normed = project(last, place((7,)), member_ref, gain, [kv_job], keep=True)
+        last = [e1[6], y["6a"], y["6b"]]
+        last_place = place((7, 0), (7, half), (7, half + quarter))
+        kv7, normed = project(last, last_place, member_ref, gain, [kv_job], keep=True)
         piece[7] = hand(kv7, 7)
-        (qd,) = project(last, place((7,)), member_ref, gain, [q_job], ready=normed)
+        (qd,) = project(last, last_place, member_ref, gain, [q_job], ready=normed)
         context = attend(
             [q0, qa, qb, qc, qd],
             [kv0, kv2, kv1, kv4, kv3, kv6, kv5, kv7],
-            [half] * (2 * members),
-            place((0, 2, 1, 4, 3, 6, 5, 7)),
+            [block_rows] * members,
+            place(*((offset, 0) for offset in (0, 2, 1, 4, 3, 6, 5, 7))),
             member_ref,
         )
         pieces = [piece[k] for k in range(members)]

time: 136 us -> 136 us (level)
  starting transfers between devices: 35.7 us -> 31.8 us
  waiting for transfers between devices: 33.8 us -> 36.1 us
  other arithmetic: 2.32 us -> 4.22 us
    ppermute x8, starting transfers between devices: 10.9 us -> 6.48 us  [hand(): return lax.ppermute(kv, ('role', 'tp'), pairs)]
    ppermute x18 -> x19, waiting for transfers between devices: 32.5 us -> 35.1 us  [move(): return lax.ppermute(value, 'tp', pairs)]
    select_n x2 -> x3, other arithmetic: 0.13 us -> 2.05 us  [the longest x1 0.99 us: local(): three[1] = jnp.where(at_end, e1['5a'], e2[1][:quarter])]
    pallas_call x6, Pallas kernels: 24.9 us -> 26.5 us  [project(): pl.pallas_call(functools.partial(project_kernel, chunk_rows, [job[3] for...]
    ppermute x18 -> x19, starting transfers between devices: 24.8 us -> 25.4 us  [move(): return lax.ppermute(value, 'tp', pairs)]
  transfers between devices with their start and end apart: 26 -> 27, of which waited for: 6 -> 9; matrix products, arithmetic and copies ran while one was open for 3% -> 5% of each run, Pallas kernels for 25% -> 26%
where the time goes in v3:
time: 136 us; the launch traced here: 135 us
  Pallas kernels  36.1 us (27%)
  waiting for transfers between devices  36.1 us (27%)
  starting transfers between devices  31.8 us (23%)
  local copies, waits for them, and re-layouts  26 us (19%)
  other arithmetic  4.22 us (3%)
    ppermute x19, waiting for transfers between devices, move(): return lax.ppermute(value, 'tp', pairs)  35.1 us
    pallas_call x6, Pallas kernels, project(): pl.pallas_call(functools.partial(project_kernel, chunk_rows, [job[3] for...  26.5 us
    ppermute x19, starting transfers between devices, move(): return lax.ppermute(value, 'tp', pairs)  25.4 us
    unnamed x32, local copies, waits for them, and re-layouts  22.2 us
    ppermute x8, starting transfers between devices, hand(): return lax.ppermute(kv, ('role', 'tp'), pairs)  6.48 us
    pallas_call x1, Pallas kernels, attend(): pl.pallas_call(functools.partial(attend_kernel, tuple(chunk_rows), len(qu...  3.45 us
    pallas_call x1, Pallas kernels, decode_old(): pl.pallas_call(decode_old_kernel, out_shape=[jax.ShapeDtypeStruct((KVH, G...  3.25 us
  transfers between devices with their start and end apart: 27, of which 9 were waited for; matrix products, arithmetic and copies ran while one was open for 5% of the time, Pallas kernels for 26%

profile of v3, /device:TPU:0, one launch (start us, length us, event | category | flops | bytes accessed | tf_op | source)
XLA Modules:
  0.0 135.2 jit_solution(1540394319959445415)
XLA Ops:
  0.6 1.9 %slice_bitcast_fusion = bf16[32,8192]{1,0:T(8,128)(2,1)} fusion(bf16[1,64,8192]{2,1,0:T(8,128)(2,1)} %param.10), kind=kLoop, calls=%fused_computation | loop fusion | bytes 1048576 | tf_op jit(solution)/shard_map/slice | solution.py:540
  2.5 3.1 %collective-permute-start = (bf16[32,8192]{1,0:T(8,128)(2,1)}, bf16[32,8192]{1,0:T(8,128)(2,1)}, u32[]{:S(2)}, u32[]{:S(2)}) collective-permute-start(bf16[32,8192]{1,0:T(8,128)(2,1)} %slice_bitcast_fusion), channel_id=1, source_target_pairs={{0,2},{1,3},{2,0},{3,1},{4,6},{5,7},{6,4},{7,5},{8,10},{9,11},{10,... | collective-permute-start | bytes 1572872 | tf_op jit(solution)/shard_map/ppermute | solution.py:521
  5.6 1.5 %collective-permute-start.1 = (bf16[32,8192]{1,0:T(8,128)(2,1)}, bf16[32,8192]{1,0:T(8,128)(2,1)}, u32[]{:S(2)}, u32[]{:S(2)}) collective-permute-start(bf16[32,8192]{1,0:T(8,128)(2,1)} %slice_bitcast_fusion), channel_id=1, source_target_pairs={{2,4},{3,5},{4,2},{5,3},{10,12},{11,13},{12,10},{13,11},{18,20},{1... | collective-permute-start | bytes 1572872 | tf_op jit(solution)/shard_map/ppermute | solution.py:521
  7.0 1.9 %slice.23 = bf16[32,8192]{1,0:T(8,128)(2,1)} slice(bf16[64,8192]{1,0:T(8,128)(2,1)} %bitcast.5), slice={[32:64], [0:8192]} | slice | bytes 1048576 | tf_op jit(solution)/shard_map/slice | solution.py:541
  8.9 3.6 %collective-permute-start.2 = (bf16[32,8192]{1,0:T(8,128)(2,1)}, bf16[32,8192]{1,0:T(8,128)(2,1)S(1)}, u32[]{:S(2)}, u32[]{:S(2)}) collective-permute-start(bf16[32,8192]{1,0:T(8,128)(2,1)} %slice.23), channel_id=1, source_target_pairs={{0,2},{1,3},{2,0},{3,1},{4,6},{5,7},{6,4},{7,5},{8,10},{9,11},{10,... | collective-permute-start | bytes 1572872 | tf_op jit(solution)/shard_map/ppermute | solution.py:521
  12.5 1.5 %collective-permute-start.3 = (bf16[32,8192]{1,0:T(8,128)(2,1)}, bf16[32,8192]{1,0:T(8,128)(2,1)}, u32[]{:S(2)}, u32[]{:S(2)}) collective-permute-start(bf16[32,8192]{1,0:T(8,128)(2,1)} %slice.23), channel_id=1, source_target_pairs={{2,4},{3,5},{4,2},{5,3},{10,12},{11,13},{12,10},{13,11},{18,20},{1... | collective-permute-start | bytes 1572872 | tf_op jit(solution)/shard_map/ppermute | solution.py:521
  14.0 1.5 %collective-permute-start.4 = (bf16[64,8192]{1,0:T(8,128)(2,1)}, bf16[64,8192]{1,0:T(8,128)(2,1)}, u32[]{:S(2)}, u32[]{:S(2)}) collective-permute-start(bf16[64,8192]{1,0:T(8,128)(2,1)} %bitcast.6), channel_id=1, source_target_pairs={{0,1},{1,0},{2,3},{3,2},{4,5},{5,4},{6,7},{7,6},{8,9},{9,8},{10,11... | collective-permute-start | bytes 3145736 | tf_op jit(solution)/shard_map/ppermute | solution.py:521
  15.5 0.8 copy-done.6
  16.3 0.7 copy-done.8
  17.0 0.7 copy-done.9
  17.7 0.7 copy-done.10
  18.3 1.5 %decode_prepare.1 = (bf16[2048,256]{1,0:T(8,128)(2,1)S(1)}, f32[64,256]{1,0:T(8,128)S(1)}, s32[96,256]{1,0:T(8,128)S(1)}) custom-call(s32[4,24]{1,0:T(4,128)S(1)} %copy-done.8, s32[4]{0:T(128)S(1)} %copy-done.9, s32[1,4]{1,0:T(1,128)S(1)} %copy-done.10, bf16[4,8192]{1,0:T(4,128)(2,1)S(1)} %copy-done.6), custom_call_target="tpu_custom_call" | custom-call | flops 10000000000 | bytes 1000 | tf_op jit(solution)/shard_map/decode_prepare/pallas_call | solution.py:308
  19.9 1.0 fusion
  20.9 1.5 %collective-permute-start.6 = (bf16[32,8192]{1,0:T(8,128)(2,1)}, bf16[32,8192]{1,0:T(8,128)(2,1)}, u32[]{:S(2)}, u32[]{:S(2)}) collective-permute-start(bf16[32,8192]{1,0:T(8,128)(2,1)} %collective-permute-done.refs_0_), channel_id=1, source_target_pairs={{2,4},{3,5},{4,2},{5,3},{10,12},{11,13},{12,10},{13,11},{18,20},{1... | collective-permute-start | bytes 1572872 | tf_op jit(solution)/shard_map/ppermute | solution.py:521
  22.4 0.5 collective-permute-start.7
  22.9 6.0 %collective-permute-done.2.refs_1_ = bf16[32,8192]{1,0:T(8,128)(2,1)S(1)} collective-permute-done((bf16[32,8192]{1,0:T(8,128)(2,1)}, bf16[32,8192]{1,0:T(8,128)(2,1)S(1)}, u32[]{:S(2)}, u32[]{:S(2)}) %collective-permute-start.2) | collective-permute-done | bytes 524320 | tf_op jit(solution)/shard_map/ppermute | solution.py:521
  28.9 1.3 collective-permute-start.5
  30.2 0.0 copy-start.1
  30.2 5.8 %copy-done.1 = bf16[8192,1024]{1,0:T(8,128)(2,1)S(1)} copy-done((bf16[8192,1024]{1,0:T(8,128)(2,1)S(1)}, bf16[8192,1024]{1,0:T(8,128)(2,1)}, u32[]{:S(2)}) %copy-start.1) | copy-done | bytes 16777240
  36.0 2.2 %copy-done.4 = bf16[8192,256]{1,0:T(8,128)(2,1)S(1)} copy-done((bf16[8192,256]{1,0:T(8,128)(2,1)S(1)}, bf16[8192,256]{1,0:T(8,128)(2,1)}, u32[]{:S(2)}) %copy-start.4) | copy-done | bytes 4194328
  38.2 4.6 %project.6 = (bf16[64,1024]{1,0:T(8,128)(2,1)S(1)}, bf16[64,256]{1,0:T(8,128)(2,1)S(1)}) custom-call(s32[1]{0:T(128)} %bitcast.member, bf16[64,8192]{1,0:T(8,128)(2,1)S(1)} %bitcast.7, bf16[1,8192]{1,0:T(2,128)(2,1)S(1)} %reshape.56.refs_1_.refs_3_.refs_4_.refs_5_, bf16[8192,1024]{1,0:T(8,128)(2,1)S(1)} %copy-done.1, ...), custom_call_target="tpu_custom_call" | custom-call | flops 10000000000 | bytes 1000 | tf_op jit(solution)/shard_map/project/pallas_call | solution.py:165
  42.8 0.0 copy-start.3
  42.8 2.8 %copy-done.3 = bf16[96,16,2048]{2,1,0:T(8,128)(2,1)S(1)} copy-done((bf16[96,16,2048]{2,1,0:T(8,128)(2,1)S(1)}, bf16[96,16,2048]{2,1,0:T(8,128)(2,1)}, u32[]{:S(2)}) %copy-start.3) | copy-done | bytes 6291480
  45.6 3.2 %decode_old.1 = (f32[8,32,128]{2,1,0:T(8,128)S(1)}, f32[2,256]{1,0:T(2,128)S(1)}) custom-call(bf16[2048,256]{1,0:T(8,128)(2,1)S(1)} %get-tuple-element.67.queries.q_ref, s32[96,256]{1,0:T(8,128)S(1)} %get-tuple-element.69.limits, bf16[4,2048]{1,0:T(4,128)(2,1)S(1)} %copy-done.7, bf16[96,16,2048]{2,1,0:T(8,128)(2,1)S(1)} %copy-done.3), custom_call_target="tpu_custom_call" | custom-call | flops 5000000000 | bytes 1000 | tf_op jit(solution)/shard_map/decode_old/pallas_call | solution.py:384
  48.8 0.1 collective-permute-start.19
  48.9 0.7 collective-permute-start.9
  49.6 1.8 %collective-permute-start.10 = (bf16[32,8192]{1,0:T(8,128)(2,1)S(1)}, bf16[32,8192]{1,0:T(8,128)(2,1)S(1)}, u32[]{:S(2)}, u32[]{:S(2)}) collective-permute-start(bf16[32,8192]{1,0:T(8,128)(2,1)S(1)} %collective-permute-done.2.refs_1_), channel_id=1, source_target_pairs={{0,1},{1,0},{2,3},{3,2},{4,5},{5,4},{6,7},{7,6},{8,9},{9,8},{10,11... | collective-permute-start | bytes 1572872 | tf_op jit(solution)/shard_map/ppermute | solution.py:521
  51.4 1.3 collective-permute-start.8
  52.7 1.5 %collective-permute-start.11 = (bf16[32,8192]{1,0:T(8,128)(2,1)}, bf16[32,8192]{1,0:T(8,128)(2,1)S(1)}, u32[]{:S(2)}, u32[]{:S(2)}) collective-permute-start(bf16[32,8192]{1,0:T(8,128)(2,1)} %collective-permute-done.6), channel_id=1, source_target_pairs={{2,0},{3,1},{4,6},{5,7},{10,8},{11,9},{12,14},{13,15},{18,16},{19,... | collective-permute-start | bytes 1572872 | tf_op jit(solution)/shard_map/ppermute | solution.py:521
  54.1 1.1 broadcast_select_fusion.2.refs_0_
  55.3 0.0 copy-start.2
  55.3 5.8 %copy-done.2 = bf16[8192,1024]{1,0:T(8,128)(2,1)S(1)} copy-done((bf16[8192,1024]{1,0:T(8,128)(2,1)S(1)}, bf16[8192,1024]{1,0:T(8,128)(2,1)}, u32[]{:S(2)}) %copy-start.2) | copy-done | bytes 16777240
  61.0 6.0 %project.7 = (bf16[128,1024]{1,0:T(8,128)(2,1)S(1)}, bf16[64,256]{1,0:T(8,128)(2,1)S(1)}, bf16[64,256]{1,0:T(8,128)(2,1)S(1)}) custom-call(s32[1]{0:T(128)} %bitcast.member, bf16[32,8192]{1,0:T(8,128)(2,1)} %collective-permute-done.refs_0_, bf16[32,8192]{1,0:T(8,128)(2,1)S(1)} %collective-permute-done.2.refs_1_, ...), custom_call_target="tpu_custom_call" | custom-call | flops 10000000000 | bytes 1000 | tf_op jit(solution)/shard_map/project/pallas_call | solution.py:165
  67.1 5.9 %collective-permute-done.8 = bf16[32,8192]{1,0:T(8,128)(2,1)S(1)} collective-permute-done((bf16[32,8192]{1,0:T(8,128)(2,1)}, bf16[32,8192]{1,0:T(8,128)(2,1)S(1)}, u32[]{:S(2)}, u32[]{:S(2)}) %collective-permute-start.8) | collective-permute-done | bytes 524320 | tf_op jit(solution)/shard_map/ppermute | solution.py:521
  73.0 0.5 collective-permute-start.12
  73.5 0.1 broadcast_select_fusion.1.refs_1_
  73.6 9.8 %collective-permute-done.11 = bf16[32,8192]{1,0:T(8,128)(2,1)S(1)} collective-permute-done((bf16[32,8192]{1,0:T(8,128)(2,1)}, bf16[32,8192]{1,0:T(8,128)(2,1)S(1)}, u32[]{:S(2)}, u32[]{:S(2)}) %collective-permute-start.11) | collective-permute-done | bytes 524320 | tf_op jit(solution)/shard_map/ppermute | solution.py:521
  83.4 2.3 %collective-permute-done.12.refs_3_ = bf16[32,8192]{1,0:T(8,128)(2,1)S(1)} collective-permute-done((bf16[32,8192]{1,0:T(8,128)(2,1)S(1)}, bf16[32,8192]{1,0:T(8,128)(2,1)S(1)}, u32[]{:S(2)}, u32[]{:S(2)}) %collective-permute-start.12) | collective-permute-done | bytes 524320 | tf_op jit(solution)/shard_map/ppermute | solution.py:521
  85.7 0.1 broadcast_select_fusion.refs_0_
  85.8 1.3 collective-permute-start.13
  87.1 0.6 collective-permute-start.14
  87.7 1.3 collective-permute-start.15
  89.0 5.8 %project.8 = (bf16[128,1024]{1,0:T(8,128)(2,1)S(1)}, bf16[64,256]{1,0:T(8,128)(2,1)S(1)}, bf16[64,256]{1,0:T(8,128)(2,1)S(1)}) custom-call(s32[1]{0:T(128)} %bitcast.member, bf16[32,8192]{1,0:T(8,128)(2,1)S(1)} %broadcast_select_fusion.2.refs_0_, bf16[32,8192]{1,0:T(8,128)(2,1)S(1)} %broadcast_select_fusion.1.refs_1_, ...), custom_call_target="tpu_custom_call" | custom-call | flops 10000000000 | bytes 1000 | tf_op jit(solution)/shard_map/project/pallas_call | solution.py:165
  94.8 7.1 %collective-permute-done.15 = bf16[16,8192]{1,0:T(8,128)(2,1)S(1)} collective-permute-done((bf16[16,8192]{1,0:T(8,128)(2,1)S(1)}, bf16[16,8192]{1,0:T(8,128)(2,1)S(1)}, u32[]{:S(2)}, u32[]{:S(2)}) %collective-permute-start.15) | collective-permute-done | bytes 262176 | tf_op jit(solution)/shard_map/ppermute | solution.py:521
  101.9 1.0 slice_select_fusion.1.refs_1_
  102.9 0.6 collective-permute-start.17
  103.4 1.0 slice_select_fusion.refs_2_
  104.4 1.6 %collective-permute-start.18 = (bf16[16,8192]{1,0:T(8,128)(2,1)S(1)}, bf16[16,8192]{1,0:T(8,128)(2,1)S(1)}, u32[]{:S(2)}, u32[]{:S(2)}) collective-permute-start(bf16[16,8192]{1,0:T(8,128)(2,1)S(1)} %slice_select_fusion.refs_2_), channel_id=1, source_target_pairs={{0,1},{1,0},{2,3},{3,2},{4,5},{5,4},{6,7},{7,6},{8,9},{9,8},{10,11... | collective-permute-start | bytes 786440 | tf_op jit(solution)/shard_map/ppermute | solution.py:521
  106.0 4.9 %project.9 = (bf16[128,1024]{1,0:T(8,128)(2,1)S(1)}, bf16[64,256]{1,0:T(8,128)(2,1)S(1)}, bf16[64,256]{1,0:T(8,128)(2,1)S(1)}) custom-call(s32[1]{0:T(128)} %bitcast.member, bf16[32,8192]{1,0:T(8,128)(2,1)S(1)} %broadcast_select_fusion.refs_0_, bf16[16,8192]{1,0:T(8,128)(2,1)S(1)} %slice_select_fusion.1.refs_1_, ...), custom_call_target="tpu_custom_call" | custom-call | flops 10000000000 | bytes 1000 | tf_op jit(solution)/shard_map/project/pallas_call | solution.py:165
  110.9 1.2 collective-permute-done.17.refs_1_
  112.1 1.7 %collective-permute-done.16.refs_0_ = bf16[32,8192]{1,0:T(8,128)(2,1)S(1)} collective-permute-done((bf16[32,8192]{1,0:T(8,128)(2,1)S(1)}, bf16[32,8192]{1,0:T(8,128)(2,1)S(1)}, u32[]{:S(2)}, u32[]{:S(2)}) %collective-permute-start.16) | collective-permute-done | bytes 524320 | tf_op jit(solution)/shard_map/ppermute | solution.py:521
  113.8 1.1 collective-permute-done.18.refs_2_
  114.9 1.0 collective-permute-start.23
  115.9 2.0 %project.10 = (bf16[64,256]{1,0:T(8,128)(2,1)S(1)}, bf16[64,8192]{1,0:T(8,128)(2,1)S(1)}) custom-call(s32[1]{0:T(128)} %bitcast.member, bf16[32,8192]{1,0:T(8,128)(2,1)S(1)} %collective-permute-done.16.refs_0_, bf16[16,8192]{1,0:T(8,128)(2,1)S(1)} %collective-permute-done.17.refs_1_, bf16[16,8192]{1,0:T(8,128)(2,1)S(1)} %collective-permute-done.18.refs_2_, ...), custom_call_target="tpu_custom_call" | custom-call | flops 10000000000 | bytes 1000 | tf_op jit(solution)/shard_map/project/pallas_call | solution.py:165
  117.9 0.4 slice-done.1
  118.4 1.2 slice-done.2
  119.5 1.2 slice-done.3
  120.7 3.2 %project.11.refs_4_ = bf16[64,1024]{1,0:T(8,128)(2,1)S(1)} custom-call(s32[1]{0:T(128)} %bitcast.member, bf16[64,8192]{1,0:T(8,128)(2,1)S(1)} %get-tuple-element.58.refs_0_, bf16[1,8192]{1,0:T(2,128)(2,1)S(1)} %reshape.56.refs_1_.refs_3_.refs_4_.refs_5_, bf16[8192,1024]{1,0:T(8,128)(2,1)S(1)} %bitcast.9, ...), custom_call_target="tpu_custom_call" | custom-call | flops 10000000000 | bytes 1000 | tf_op jit(solution)/shard_map/project/pallas_call | solution.py:165
  123.9 1.9 %collective-permute-start.24 = (bf16[64,256]{1,0:T(8,128)(2,1)S(1)}, bf16[64,256]{1,0:T(8,128)(2,1)S(1)}, u32[]{:S(2)}, u32[]{:S(2)}) collective-permute-start(bf16[64,256]{1,0:T(8,128)(2,1)S(1)} %get-tuple-element.65.refs_11_), channel_id=1, source_target_pairs={{0,13},{1,12},{2,15},{3,14},{4,9},{5,8},{6,11},{7,10},{8,5},{9,4},... | collective-permute-start | bytes 98312 | tf_op jit(solution)/shard_map/ppermute | solution.py:538
  125.9 1.9 %collective-permute-start.25 = (bf16[64,256]{1,0:T(8,128)(2,1)S(1)}, bf16[64,256]{1,0:T(8,128)(2,1)S(1)}, u32[]{:S(2)}, u32[]{:S(2)}) collective-permute-start(bf16[64,256]{1,0:T(8,128)(2,1)S(1)} %get-tuple-element.64.refs_10_), channel_id=1, source_target_pairs={{0,14},{1,15},{2,12},{3,13},{4,10},{5,11},{6,8},{7,9},{8,6},{9,7},... | collective-permute-start | bytes 98312 | tf_op jit(solution)/shard_map/ppermute | solution.py:538
  127.8 1.6 %collective-permute-start.26 = (bf16[64,256]{1,0:T(8,128)(2,1)S(1)}, bf16[64,256]{1,0:T(8,128)(2,1)S(1)}, u32[]{:S(2)}, u32[]{:S(2)}) collective-permute-start(bf16[64,256]{1,0:T(8,128)(2,1)S(1)} %get-tuple-element.66.refs_12_), channel_id=1, source_target_pairs={{0,15},{1,14},{2,13},{3,12},{4,11},{5,10},{6,9},{7,8},{8,7},{9,6},... | collective-permute-start | bytes 98312 | tf_op jit(solution)/shard_map/ppermute | solution.py:538
  129.4 3.4 %attend.1 = bf16[512,1024]{1,0:T(8,128)(2,1)} custom-call(s32[1]{0:T(128)} %bitcast.member, bf16[64,1024]{1,0:T(8,128)(2,1)S(1)} %get-tuple-element.37.refs_0_, bf16[128,1024]{1,0:T(8,128)(2,1)S(1)} %get-tuple-element.42.refs_1_, bf16[128,1024]{1,0:T(8,128)(2,1)S(1)} %get-tuple-element.51.refs_2_, bf16[128,1024]{1,0:T(8,128)(2,1)S(1)} %get-tuple-element.57.refs_3_, ...), custom_call_target="tpu_custom_call" | custom-call | flops 5000000000 | bytes 1000 | tf_op jit(solution)/shard_map/attend/pallas_call | solution.py:243
  132.8 1.0 collective-permute-done.26.refs_7_
  133.8 1.3 decode_new.1
  (45 shorter events, 0.2 us)
Async XLA Ops:
  2.5 18.4 %collective-permute-start = (bf16[32,8192]{1,0:T(8,128)(2,1)}, bf16[32,8192]{1,0:T(8,128)(2,1)}, u32[]{:S(2)}, u32[]{:S(2)}) collective-permute-start(bf16[32,8192]{1,0:T(8,128)(2,1)} %slice_bitcast_fusion), channel_id=1, source_target_pairs={{0,2},{1,3},{2,0},{3,1},{4,6},{5,7},{6,4},{7,5},{8,10},{9,11},{10,... | collective-permute-start | bytes 1572872 | tf_op jit(solution)/shard_map/ppermute | solution.py:521
  5.6 15.4 %collective-permute-start.1 = (bf16[32,8192]{1,0:T(8,128)(2,1)}, bf16[32,8192]{1,0:T(8,128)(2,1)}, u32[]{:S(2)}, u32[]{:S(2)}) collective-permute-start(bf16[32,8192]{1,0:T(8,128)(2,1)} %slice_bitcast_fusion), channel_id=1, source_target_pairs={{2,4},{3,5},{4,2},{5,3},{10,12},{11,13},{12,10},{13,11},{18,20},{1... | collective-permute-start | bytes 1572872 | tf_op jit(solution)/shard_map/ppermute | solution.py:521
  7.0 12.8 %copy-start.11 = (bf16[8192]{0:T(1024)(128)(2,1)S(1)}, bf16[8192]{0:T(1024)(128)(2,1)}, u32[]{:S(2)}) copy-start(bf16[8192]{0:T(1024)(128)(2,1)} %param.11) | copy-start | bytes 49156
  8.9 21.3 %copy-start = (bf16[1,64,8192]{2,1,0:T(8,128)(2,1)S(1)}, bf16[1,64,8192]{2,1,0:T(8,128)(2,1)}, u32[]{:S(2)}) copy-start(bf16[1,64,8192]{2,1,0:T(8,128)(2,1)} %param.10) | copy-start | bytes 3145732
  8.9 20.0 %collective-permute-start.2 = (bf16[32,8192]{1,0:T(8,128)(2,1)}, bf16[32,8192]{1,0:T(8,128)(2,1)S(1)}, u32[]{:S(2)}, u32[]{:S(2)}) collective-permute-start(bf16[32,8192]{1,0:T(8,128)(2,1)} %slice.23), channel_id=1, source_target_pairs={{0,2},{1,3},{2,0},{3,1},{4,6},{5,7},{6,4},{7,5},{8,10},{9,11},{10,... | collective-permute-start | bytes 1572872 | tf_op jit(solution)/shard_map/ppermute | solution.py:521
  12.5 36.3 %collective-permute-start.3 = (bf16[32,8192]{1,0:T(8,128)(2,1)}, bf16[32,8192]{1,0:T(8,128)(2,1)}, u32[]{:S(2)}, u32[]{:S(2)}) collective-permute-start(bf16[32,8192]{1,0:T(8,128)(2,1)} %slice.23), channel_id=1, source_target_pairs={{2,4},{3,5},{4,2},{5,3},{10,12},{11,13},{12,10},{13,11},{18,20},{1... | collective-permute-start | bytes 1572872 | tf_op jit(solution)/shard_map/ppermute | solution.py:521
  14.0 34.9 %collective-permute-start.4 = (bf16[64,8192]{1,0:T(8,128)(2,1)}, bf16[64,8192]{1,0:T(8,128)(2,1)}, u32[]{:S(2)}, u32[]{:S(2)}) collective-permute-start(bf16[64,8192]{1,0:T(8,128)(2,1)} %bitcast.6), channel_id=1, source_target_pairs={{0,1},{1,0},{2,3},{3,2},{4,5},{5,4},{6,7},{7,6},{8,9},{9,8},{10,11... | collective-permute-start | bytes 3145736 | tf_op jit(solution)/shard_map/ppermute | solution.py:521
  15.5 0.8 copy-start.6
  16.3 0.7 copy-start.8
  17.0 0.7 copy-start.9
  17.6 0.7 copy-start.10
  20.9 30.4 %collective-permute-start.6 = (bf16[32,8192]{1,0:T(8,128)(2,1)}, bf16[32,8192]{1,0:T(8,128)(2,1)}, u32[]{:S(2)}, u32[]{:S(2)}) collective-permute-start(bf16[32,8192]{1,0:T(8,128)(2,1)} %collective-permute-done.refs_0_), channel_id=1, source_target_pairs={{2,4},{3,5},{4,2},{5,3},{10,12},{11,13},{12,10},{13,11},{18,20},{1... | collective-permute-start | bytes 1572872 | tf_op jit(solution)/shard_map/ppermute | solution.py:521
  22.4 29.0 %collective-permute-start.7 = (bf16[32,8192]{1,0:T(8,128)(2,1)}, bf16[32,8192]{1,0:T(8,128)(2,1)}, u32[]{:S(2)}, u32[]{:S(2)}) collective-permute-start(bf16[32,8192]{1,0:T(8,128)(2,1)} %collective-permute-done.refs_0_), channel_id=1, source_target_pairs={{0,1},{1,0},{2,3},{3,2},{4,5},{5,4},{6,7},{7,6},{8,9},{9,8},{10,11... | collective-permute-start | bytes 1572872 | tf_op jit(solution)/shard_map/ppermute | solution.py:521
  28.9 20.7 %collective-permute-start.5 = (bf16[32,8192]{1,0:T(8,128)(2,1)}, bf16[32,8192]{1,0:T(8,128)(2,1)}, u32[]{:S(2)}, u32[]{:S(2)}) collective-permute-start(bf16[32,8192]{1,0:T(8,128)(2,1)} %collective-permute-done.1), channel_id=1, source_target_pairs={{2,0},{3,1},{4,6},{5,7},{10,8},{11,9},{12,14},{13,15},{18,16},{19,... | collective-permute-start | bytes 1572872 | tf_op jit(solution)/shard_map/ppermute | solution.py:521
  30.2 5.8 %copy-start.1 = (bf16[8192,1024]{1,0:T(8,128)(2,1)S(1)}, bf16[8192,1024]{1,0:T(8,128)(2,1)}, u32[]{:S(2)}) copy-start(bf16[8192,1024]{1,0:T(8,128)(2,1)} %refs_2_.3) | copy-start | bytes 50331652
  36.0 2.2 %copy-start.4 = (bf16[8192,256]{1,0:T(8,128)(2,1)S(1)}, bf16[8192,256]{1,0:T(8,128)(2,1)}, u32[]{:S(2)}) copy-start(bf16[8192,256]{1,0:T(8,128)(2,1)} %refs_4_.3) | copy-start | bytes 12582916
  38.2 4.6 %copy-start.7 = (bf16[4,2048]{1,0:T(4,128)(2,1)S(1)}, bf16[4,2048]{1,0:T(4,128)(2,1)}, u32[]{:S(2)}) copy-start(bf16[4,2048]{1,0:T(4,128)(2,1)} %own_ref.1) | copy-start | bytes 49156
  42.8 2.8 %copy-start.3 = (bf16[96,16,2048]{2,1,0:T(8,128)(2,1)S(1)}, bf16[96,16,2048]{2,1,0:T(8,128)(2,1)}, u32[]{:S(2)}) copy-start(bf16[96,16,2048]{2,1,0:T(8,128)(2,1)} %pool.1) | copy-start | bytes 18874372
  45.6 9.7 %copy-start.5 = (bf16[8192,256]{1,0:T(8,128)(2,1)S(1)}, bf16[8192,256]{1,0:T(8,128)(2,1)}, u32[]{:S(2)}) copy-start(bf16[8192,256]{1,0:T(8,128)(2,1)} %refs_4_.3) | copy-start | bytes 12582916
  48.8 75.1 %collective-permute-start.19 = (bf16[64,256]{1,0:T(8,128)(2,1)S(1)}, bf16[64,256]{1,0:T(8,128)(2,1)S(1)}, u32[]{:S(2)}, u32[]{:S(2)}) collective-permute-start(bf16[64,256]{1,0:T(8,128)(2,1)S(1)} %get-tuple-element.59.refs_5_), channel_id=1, source_target_pairs={{0,8},{1,9},{2,10},{3,11},{4,12},{5,13},{6,14},{7,15},{8,0},{9,1},... | collective-permute-start | bytes 98312 | tf_op jit(solution)/shard_map/ppermute | solution.py:538
  48.9 24.6 %collective-permute-start.9 = (bf16[32,8192]{1,0:T(8,128)(2,1)S(1)}, bf16[32,8192]{1,0:T(8,128)(2,1)S(1)}, u32[]{:S(2)}, u32[]{:S(2)}) collective-permute-start(bf16[32,8192]{1,0:T(8,128)(2,1)S(1)} %collective-permute-done.2.refs_1_), channel_id=1, source_target_pairs={{2,4},{3,5},{4,2},{5,3},{10,12},{11,13},{12,10},{13,11},{18,20},{1... | collective-permute-start | bytes 1572872 | tf_op jit(solution)/shard_map/ppermute | solution.py:521
  49.6 23.9 %collective-permute-start.10 = (bf16[32,8192]{1,0:T(8,128)(2,1)S(1)}, bf16[32,8192]{1,0:T(8,128)(2,1)S(1)}, u32[]{:S(2)}, u32[]{:S(2)}) collective-permute-start(bf16[32,8192]{1,0:T(8,128)(2,1)S(1)} %collective-permute-done.2.refs_1_), channel_id=1, source_target_pairs={{0,1},{1,0},{2,3},{3,2},{4,5},{5,4},{6,7},{7,6},{8,9},{9,8},{10,11... | collective-permute-start | bytes 1572872 | tf_op jit(solution)/shard_map/ppermute | solution.py:521
  51.4 21.6 %collective-permute-start.8 = (bf16[32,8192]{1,0:T(8,128)(2,1)}, bf16[32,8192]{1,0:T(8,128)(2,1)S(1)}, u32[]{:S(2)}, u32[]{:S(2)}) collective-permute-start(bf16[32,8192]{1,0:T(8,128)(2,1)} %collective-permute-done.3), channel_id=1, source_target_pairs={{2,0},{3,1},{4,6},{5,7},{10,8},{11,9},{12,14},{13,15},{18,16},{19,... | collective-permute-start | bytes 1572872 | tf_op jit(solution)/shard_map/ppermute | solution.py:521
  52.7 30.8 %collective-permute-start.11 = (bf16[32,8192]{1,0:T(8,128)(2,1)}, bf16[32,8192]{1,0:T(8,128)(2,1)S(1)}, u32[]{:S(2)}, u32[]{:S(2)}) collective-permute-start(bf16[32,8192]{1,0:T(8,128)(2,1)} %collective-permute-done.6), channel_id=1, source_target_pairs={{2,0},{3,1},{4,6},{5,7},{10,8},{11,9},{12,14},{13,15},{18,16},{19,... | collective-permute-start | bytes 1572872 | tf_op jit(solution)/shard_map/ppermute | solution.py:521
  55.3 5.8 %copy-start.2 = (bf16[8192,1024]{1,0:T(8,128)(2,1)S(1)}, bf16[8192,1024]{1,0:T(8,128)(2,1)}, u32[]{:S(2)}) copy-start(bf16[8192,1024]{1,0:T(8,128)(2,1)} %refs_2_.3) | copy-start | bytes 50331652
  73.0 12.8 %collective-permute-start.12 = (bf16[32,8192]{1,0:T(8,128)(2,1)S(1)}, bf16[32,8192]{1,0:T(8,128)(2,1)S(1)}, u32[]{:S(2)}, u32[]{:S(2)}) collective-permute-start(bf16[32,8192]{1,0:T(8,128)(2,1)S(1)} %broadcast_select_fusion.2.refs_0_), channel_id=1, source_target_pairs={{0,1},{1,0},{2,3},{3,2},{4,5},{5,4},{6,7},{7,6},{8,9},{9,8},{10,11... | collective-permute-start | bytes 1572872 | tf_op jit(solution)/shard_map/ppermute | solution.py:521
  73.5 52.4 %collective-permute-start.20 = (bf16[64,256]{1,0:T(8,128)(2,1)S(1)}, bf16[64,256]{1,0:T(8,128)(2,1)S(1)}, u32[]{:S(2)}, u32[]{:S(2)}) collective-permute-start(bf16[64,256]{1,0:T(8,128)(2,1)S(1)} %get-tuple-element.61.refs_7_), channel_id=1, source_target_pairs={{0,9},{1,8},{2,11},{3,10},{4,13},{5,12},{6,15},{7,14},{8,1},{9,0},... | collective-permute-start | bytes 98312 | tf_op jit(solution)/shard_map/ppermute | solution.py:538
  85.8 17.0 %collective-permute-start.13 = (bf16[16,8192]{1,0:T(8,128)(2,1)S(1)}, bf16[16,8192]{1,0:T(8,128)(2,1)S(1)}, u32[]{:S(2)}, u32[]{:S(2)}) collective-permute-start(bf16[16,8192]{1,0:T(8,128)(2,1)S(1)} %get-tuple-element.73), channel_id=1, source_target_pairs={{2,0},{3,1},{4,6},{5,7},{10,8},{11,9},{12,14},{13,15},{18,16},{19,... | collective-permute-start | bytes 786440 | tf_op jit(solution)/shard_map/ppermute | solution.py:521
  87.1 16.3 %collective-permute-start.14 = (bf16[32,8192]{1,0:T(8,128)(2,1)S(1)}, bf16[32,8192]{1,0:T(8,128)(2,1)S(1)}, u32[]{:S(2)}, u32[]{:S(2)}) collective-permute-start(bf16[32,8192]{1,0:T(8,128)(2,1)S(1)} %broadcast_select_fusion.1.refs_1_), channel_id=1, source_target_pairs={{0,1},{1,0},{2,3},{3,2},{4,5},{5,4},{6,7},{7,6},{8,9},{9,8},{10,11... | collective-permute-start | bytes 1572872 | tf_op jit(solution)/shard_map/ppermute | solution.py:521
  87.7 14.2 %collective-permute-start.15 = (bf16[16,8192]{1,0:T(8,128)(2,1)S(1)}, bf16[16,8192]{1,0:T(8,128)(2,1)S(1)}, u32[]{:S(2)}, u32[]{:S(2)}) collective-permute-start(bf16[16,8192]{1,0:T(8,128)(2,1)S(1)} %get-tuple-element.72), channel_id=1, source_target_pairs={{2,0},{3,1},{4,6},{5,7},{10,8},{11,9},{12,14},{13,15},{18,16},{19,... | collective-permute-start | bytes 786440 | tf_op jit(solution)/shard_map/ppermute | solution.py:521
  101.9 12.0 %collective-permute-start.16 = (bf16[32,8192]{1,0:T(8,128)(2,1)S(1)}, bf16[32,8192]{1,0:T(8,128)(2,1)S(1)}, u32[]{:S(2)}, u32[]{:S(2)}) collective-permute-start(bf16[32,8192]{1,0:T(8,128)(2,1)S(1)} %collective-permute-done.12.refs_3_), channel_id=1, source_target_pairs={{0,2},{1,3},{2,0},{3,1},{4,6},{5,7},{6,4},{7,5},{8,10},{9,11},{10,... | collective-permute-start | bytes 1572872 | tf_op jit(solution)/shard_map/ppermute | solution.py:521
  102.9 9.2 %collective-permute-start.17 = (bf16[16,8192]{1,0:T(8,128)(2,1)S(1)}, bf16[16,8192]{1,0:T(8,128)(2,1)S(1)}, u32[]{:S(2)}, u32[]{:S(2)}) collective-permute-start(bf16[16,8192]{1,0:T(8,128)(2,1)S(1)} %slice_select_fusion.1.refs_1_), channel_id=1, source_target_pairs={{0,1},{1,0},{2,3},{3,2},{4,5},{5,4},{6,7},{7,6},{8,9},{9,8},{10,11... | collective-permute-start | bytes 786440 | tf_op jit(solution)/shard_map/ppermute | solution.py:521
  104.4 10.5 %collective-permute-start.18 = (bf16[16,8192]{1,0:T(8,128)(2,1)S(1)}, bf16[16,8192]{1,0:T(8,128)(2,1)S(1)}, u32[]{:S(2)}, u32[]{:S(2)}) collective-permute-start(bf16[16,8192]{1,0:T(8,128)(2,1)S(1)} %slice_select_fusion.refs_2_), channel_id=1, source_target_pairs={{0,1},{1,0},{2,3},{3,2},{4,5},{5,4},{6,7},{7,6},{8,9},{9,8},{10,11... | collective-permute-start | bytes 786440 | tf_op jit(solution)/shard_map/ppermute | solution.py:521
  112.1 15.7 %collective-permute-start.21 = (bf16[64,256]{1,0:T(8,128)(2,1)S(1)}, bf16[64,256]{1,0:T(8,128)(2,1)S(1)}, u32[]{:S(2)}, u32[]{:S(2)}) collective-permute-start(bf16[64,256]{1,0:T(8,128)(2,1)S(1)} %get-tuple-element.60.refs_6_), channel_id=1, source_target_pairs={{0,10},{1,11},{2,8},{3,9},{4,14},{5,15},{6,12},{7,13},{8,2},{9,3},... | collective-permute-start | bytes 98312 | tf_op jit(solution)/shard_map/ppermute | solution.py:538
  113.8 19.0 %collective-permute-start.22 = (bf16[64,256]{1,0:T(8,128)(2,1)S(1)}, bf16[64,256]{1,0:T(8,128)(2,1)S(1)}, u32[]{:S(2)}, u32[]{:S(2)}) collective-permute-start(bf16[64,256]{1,0:T(8,128)(2,1)S(1)} %get-tuple-element.63.refs_9_), channel_id=1, source_target_pairs={{0,11},{1,10},{2,9},{3,8},{4,15},{5,14},{6,13},{7,12},{8,3},{9,2},... | collective-permute-start | bytes 98312 | tf_op jit(solution)/shard_map/ppermute | solution.py:538
  114.9 3.0 %slice-start = ((s8[16777216]{0:T(1024)(128)(4,1)}), s8[4194304]{0:T(1024)(128)(4,1)S(1)}, s32[]{:S(2)}) async-start(s8[16777216]{0:T(1024)(128)(4,1)} %bitcast.8), calls=%async_computation | async-start | bytes 8388608
  114.9 3.5 %slice-start.1 = ((s8[16777216]{0:T(1024)(128)(4,1)}), s8[4194304]{0:T(1024)(128)(4,1)S(1)}, s32[]{:S(2)}) async-start(s8[16777216]{0:T(1024)(128)(4,1)} %bitcast.8), calls=%async_computation.1 | async-start | bytes 8388608
  114.9 4.7 %slice-start.2 = ((s8[16777216]{0:T(1024)(128)(4,1)}), s8[4194304]{0:T(1024)(128)(4,1)S(1)}, s32[]{:S(2)}) async-start(s8[16777216]{0:T(1024)(128)(4,1)} %bitcast.8), calls=%async_computation.2 | async-start | bytes 8388608
  114.9 5.8 %slice-start.3 = ((s8[16777216]{0:T(1024)(128)(4,1)}), s8[4194304]{0:T(1024)(128)(4,1)S(1)}, s32[]{:S(2)}) async-start(s8[16777216]{0:T(1024)(128)(4,1)} %bitcast.8), calls=%async_computation.3 | async-start | bytes 8388608
  114.9 17.9 %collective-permute-start.23 = (bf16[64,256]{1,0:T(8,128)(2,1)S(1)}, bf16[64,256]{1,0:T(8,128)(2,1)S(1)}, u32[]{:S(2)}, u32[]{:S(2)}) collective-permute-start(bf16[64,256]{1,0:T(8,128)(2,1)S(1)} %get-tuple-element.62.refs_8_), channel_id=1, source_target_pairs={{0,12},{1,13},{2,14},{3,15},{4,8},{5,9},{6,10},{7,11},{8,4},{9,5},... | collective-permute-start | bytes 98312 | tf_op jit(solution)/shard_map/ppermute | solution.py:538
  123.9 8.9 %collective-permute-start.24 = (bf16[64,256]{1,0:T(8,128)(2,1)S(1)}, bf16[64,256]{1,0:T(8,128)(2,1)S(1)}, u32[]{:S(2)}, u32[]{:S(2)}) collective-permute-start(bf16[64,256]{1,0:T(8,128)(2,1)S(1)} %get-tuple-element.65.refs_11_), channel_id=1, source_target_pairs={{0,13},{1,12},{2,15},{3,14},{4,9},{5,8},{6,11},{7,10},{8,5},{9,4},... | collective-permute-start | bytes 98312 | tf_op jit(solution)/shard_map/ppermute | solution.py:538
  125.9 7.0 %collective-permute-start.25 = (bf16[64,256]{1,0:T(8,128)(2,1)S(1)}, bf16[64,256]{1,0:T(8,128)(2,1)S(1)}, u32[]{:S(2)}, u32[]{:S(2)}) collective-permute-start(bf16[64,256]{1,0:T(8,128)(2,1)S(1)} %get-tuple-element.64.refs_10_), channel_id=1, source_target_pairs={{0,14},{1,15},{2,12},{3,13},{4,10},{5,11},{6,8},{7,9},{8,6},{9,7},... | collective-permute-start | bytes 98312 | tf_op jit(solution)/shard_map/ppermute | solution.py:538
  127.8 6.0 %collective-permute-start.26 = (bf16[64,256]{1,0:T(8,128)(2,1)S(1)}, bf16[64,256]{1,0:T(8,128)(2,1)S(1)}, u32[]{:S(2)}, u32[]{:S(2)}) collective-permute-start(bf16[64,256]{1,0:T(8,128)(2,1)S(1)} %get-tuple-element.66.refs_12_), channel_id=1, source_target_pairs={{0,15},{1,14},{2,13},{3,12},{4,11},{5,10},{6,9},{7,8},{8,7},{9,6},... | collective-permute-start | bytes 98312 | tf_op jit(solution)/shard_map/ppermute | solution.py:538

commit v4 on v3

--- a/solution.py
+++ b/solution.py
@@ -537,8 +537,10 @@
             ]
             return lax.ppermute(kv, ("role", "tp"), pairs)
 
-        own = [tokens[:half]]
-        own.append(bar((tokens, own[0]))[0][half:])
+        own = []
+        for c in range(2):
+            source = bar((tokens, own[0]))[0] if c else tokens
+            own.append(source[c * half : (c + 1) * half])
         y, e1, e2 = {}, {}, {}
         y[0] = move(tokens, side)
         for c in range(2):
@@ -548,10 +550,6 @@
         q0, kv0 = project([tokens], place((0, 0)), member_ref, gain, [q_job, kv_job])
         piece = {0: hand(kv0, 0)}
         for c in range(2):
-            if c == 0:
-                e1[0], e2[0] = bar((e1[0], e2[0]))
-            else:
-                e1[1], e2[1], y[0] = bar((e1[1], e2[1], y[0]))
             e1[2 + c] = move(e2[c], outward)
             e2[2 + c] = move(e1[c], inner)
             y[2 + c] = move(e1[c], side)
@@ -565,7 +563,6 @@
         piece[2], piece[1] = hand(kv2, 2), hand(kv1, 1)
         two, three = {}, {}
         for c in range(2):
-            e1[2 + c], e2[2 + c], y[2 + c] = bar((e1[2 + c], e2[2 + c], y[2 + c]))
             two[c] = jnp.where(at_end, e1[2 + c], e2[2 + c])
             if c == 0:
                 e1[4] = move(e2[2], outward)
@@ -581,13 +578,12 @@
             [q_job, kv_pair],
         )
         piece[4], piece[3] = hand(kv4, 4), hand(kv3, 3)
-        e1[4], y[4] = bar((e1[4], y[4]))
         three[0] = jnp.where(at_end, e1[4], e2[0])
         e1[6] = move(y[4], outer)
         three[1] = jnp.where(at_end, e1["5a"], e2[1][:quarter])
         y["6a"] = move(three[1], side)
         state = decode_old(kv_pool, dec_heads, limits, dec_new_kv)
-        e1["5b"], y[5], three[1] = bar((e1["5b"], y[5], three[1]))
+        e1["5b"], three[1] = bar((e1["5b"], three[1]))
         three[2] = jnp.where(at_end, e1["5b"], e2[1][quarter:])
         y["6b"] = move(three[2], side)
         qc, kv6, kv5 = project(

time: 136 us -> 152 us (1.12)
  waiting for transfers between devices: 36.1 us -> 48.8 us
  starting transfers between devices: 31.8 us -> 36.2 us
    ppermute x19, waiting for transfers between devices: 35.1 us -> 48.8 us  [move(): return lax.ppermute(value, 'tp', pairs)]
    ppermute x19, starting transfers between devices: 25.4 us -> 27.6 us  [move(): return lax.ppermute(value, 'tp', pairs)]
    ppermute x8, starting transfers between devices: 6.48 us -> 8.62 us  [hand(): return lax.ppermute(kv, ('role', 'tp'), pairs)]
  transfers between devices with their start and end apart: 27 -> 27, of which waited for: 9 -> 6; matrix products, arithmetic and copies ran while one was open for 5% -> 5% of each run, Pallas kernels for 26% -> 22%
where the time goes in v4:
time: 152 us; the launch traced here: 151 us
  waiting for transfers between devices  48.8 us (32%)
  starting transfers between devices  36.2 us (24%)
  Pallas kernels  34.8 us (23%)
  local copies, waits for them, and re-layouts  26.3 us (17%)
  other arithmetic  4.22 us (3%)
    ppermute x19, waiting for transfers between devices, move(): return lax.ppermute(value, 'tp', pairs)  48.8 us
    ppermute x19, starting transfers between devices, move(): return lax.ppermute(value, 'tp', pairs)  27.6 us
    pallas_call x6, Pallas kernels, project(): pl.pallas_call(functools.partial(project_kernel, chunk_rows, [job[3] for...  25.2 us
    unnamed x32, local copies, waits for them, and re-layouts  21.4 us
    ppermute x8, starting transfers between devices, hand(): return lax.ppermute(kv, ('role', 'tp'), pairs)  8.62 us
    slice x2, local copies, waits for them, and re-layouts, local(): own.append(source[c * half:(c + 1) * half])  3.77 us
    pallas_call x1, Pallas kernels, attend(): pl.pallas_call(functools.partial(attend_kernel, tuple(chunk_rows), len(qu...  3.45 us
    pallas_call x1, Pallas kernels, decode_old(): pl.pallas_call(decode_old_kernel, out_shape=[jax.ShapeDtypeStruct((KVH, G...  3.25 us
  transfers between devices with their start and end apart: 27, of which 6 were waited for; matrix products, arithmetic and copies ran while one was open for 5% of the time, Pallas kernels for 22%

profile of v4, /device:TPU:0, one launch (start us, length us, event | category | flops | bytes accessed | tf_op | source)
XLA Modules:
  0.0 151.4 jit_solution(9138277469372476135)
XLA Ops:
  0.6 1.9 %slice_bitcast_fusion = bf16[32,8192]{1,0:T(8,128)(2,1)} fusion(bf16[1,64,8192]{2,1,0:T(8,128)(2,1)} %param.10), kind=kLoop, calls=%fused_computation | loop fusion | bytes 1048576 | tf_op jit(solution)/shard_map/slice | solution.py:543
  2.5 3.1 %collective-permute-start = (bf16[32,8192]{1,0:T(8,128)(2,1)}, bf16[32,8192]{1,0:T(8,128)(2,1)S(1)}, u32[]{:S(2)}, u32[]{:S(2)}) collective-permute-start(bf16[32,8192]{1,0:T(8,128)(2,1)} %slice_bitcast_fusion), channel_id=1, source_target_pairs={{0,2},{1,3},{2,0},{3,1},{4,6},{5,7},{6,4},{7,5},{8,10},{9,11},{10,... | collective-permute-start | bytes 1572872 | tf_op jit(solution)/shard_map/ppermute | solution.py:521
  5.6 1.5 collective-permute-start.3
  7.0 1.5 %collective-permute-start.2 = (bf16[64,8192]{1,0:T(8,128)(2,1)}, bf16[64,8192]{1,0:T(8,128)(2,1)}, u32[]{:S(2)}, u32[]{:S(2)}) collective-permute-start(bf16[64,8192]{1,0:T(8,128)(2,1)} %bitcast.5), channel_id=1, source_target_pairs={{0,1},{1,0},{2,3},{3,2},{4,5},{5,4},{6,7},{7,6},{8,9},{9,8},{10,11... | collective-permute-start | bytes 3145736 | tf_op jit(solution)/shard_map/ppermute | solution.py:521
  8.5 1.9 %slice.23 = bf16[32,8192]{1,0:T(8,128)(2,1)} slice(bf16[64,8192]{1,0:T(8,128)(2,1)} %bitcast.6), slice={[32:64], [0:8192]} | slice | bytes 1048576 | tf_op jit(solution)/shard_map/slice | solution.py:543
  10.4 3.7 %collective-permute-start.1 = (bf16[32,8192]{1,0:T(8,128)(2,1)}, bf16[32,8192]{1,0:T(8,128)(2,1)}, u32[]{:S(2)}, u32[]{:S(2)}) collective-permute-start(bf16[32,8192]{1,0:T(8,128)(2,1)} %slice.23), channel_id=1, source_target_pairs={{0,2},{1,3},{2,0},{3,1},{4,6},{5,7},{6,4},{7,5},{8,10},{9,11},{10,... | collective-permute-start | bytes 1572872 | tf_op jit(solution)/shard_map/ppermute | solution.py:521
  14.1 1.5 collective-permute-start.6
  15.6 0.8 copy-done.6
  16.4 0.7 copy-done.8
  17.1 0.7 copy-done.9
  17.7 0.7 copy-done.10
  18.4 1.5 %decode_prepare.1 = (bf16[2048,256]{1,0:T(8,128)(2,1)S(1)}, f32[64,256]{1,0:T(8,128)S(1)}, s32[96,256]{1,0:T(8,128)S(1)}) custom-call(s32[4,24]{1,0:T(4,128)S(1)} %copy-done.8, s32[4]{0:T(128)S(1)} %copy-done.9, s32[1,4]{1,0:T(1,128)S(1)} %copy-done.10, bf16[4,8192]{1,0:T(4,128)(2,1)S(1)} %copy-done.6), custom_call_target="tpu_custom_call" | custom-call | flops 10000000000 | bytes 1000 | tf_op jit(solution)/shard_map/decode_prepare/pallas_call | solution.py:308
  20.0 1.0 fusion
  21.0 1.3 collective-permute-start.7
  22.3 6.7 %collective-permute-done.1.refs_1_ = bf16[32,8192]{1,0:T(8,128)(2,1)} collective-permute-done((bf16[32,8192]{1,0:T(8,128)(2,1)}, bf16[32,8192]{1,0:T(8,128)(2,1)}, u32[]{:S(2)}, u32[]{:S(2)}) %collective-permute-start.1) | collective-permute-done | bytes 524320 | tf_op jit(solution)/shard_map/ppermute | solution.py:521
  29.0 1.5 collective-permute-start.8
  30.5 5.8 %copy-done.1 = bf16[8192,1024]{1,0:T(8,128)(2,1)S(1)} copy-done((bf16[8192,1024]{1,0:T(8,128)(2,1)S(1)}, bf16[8192,1024]{1,0:T(8,128)(2,1)}, u32[]{:S(2)}) %copy-start.1) | copy-done | bytes 16777240
  36.3 2.2 %copy-done.4 = bf16[8192,256]{1,0:T(8,128)(2,1)S(1)} copy-done((bf16[8192,256]{1,0:T(8,128)(2,1)S(1)}, bf16[8192,256]{1,0:T(8,128)(2,1)}, u32[]{:S(2)}) %copy-start.4) | copy-done | bytes 4194328
  38.4 4.6 %project.6 = (bf16[64,1024]{1,0:T(8,128)(2,1)S(1)}, bf16[64,256]{1,0:T(8,128)(2,1)S(1)}) custom-call(s32[1]{0:T(128)} %bitcast.member, bf16[64,8192]{1,0:T(8,128)(2,1)S(1)} %bitcast.7, bf16[1,8192]{1,0:T(2,128)(2,1)S(1)} %reshape.56.refs_1_.refs_3_.refs_4_.refs_5_, bf16[8192,1024]{1,0:T(8,128)(2,1)S(1)} %copy-done.1, ...), custom_call_target="tpu_custom_call" | custom-call | flops 10000000000 | bytes 1000 | tf_op jit(solution)/shard_map/project/pallas_call | solution.py:165
  43.0 0.0 copy-start.3
  43.1 2.8 %copy-done.3 = bf16[96,16,2048]{2,1,0:T(8,128)(2,1)S(1)} copy-done((bf16[96,16,2048]{2,1,0:T(8,128)(2,1)S(1)}, bf16[96,16,2048]{2,1,0:T(8,128)(2,1)}, u32[]{:S(2)}) %copy-start.3) | copy-done | bytes 6291480
  45.8 3.2 %decode_old.1 = (f32[8,32,128]{2,1,0:T(8,128)S(1)}, f32[2,256]{1,0:T(2,128)S(1)}) custom-call(bf16[2048,256]{1,0:T(8,128)(2,1)S(1)} %get-tuple-element.39.queries.q_ref, s32[96,256]{1,0:T(8,128)S(1)} %get-tuple-element.41.limits, bf16[4,2048]{1,0:T(4,128)(2,1)S(1)} %copy-done.7, bf16[96,16,2048]{2,1,0:T(8,128)(2,1)S(1)} %copy-done.3), custom_call_target="tpu_custom_call" | custom-call | flops 5000000000 | bytes 1000 | tf_op jit(solution)/shard_map/decode_old/pallas_call | solution.py:384
  49.1 0.1 collective-permute-start.19
  49.2 0.0 collective-permute-done.3
  49.2 0.7 collective-permute-start.5
  49.9 1.8 %collective-permute-start.9 = (bf16[32,8192]{1,0:T(8,128)(2,1)S(1)}, bf16[32,8192]{1,0:T(8,128)(2,1)S(1)}, u32[]{:S(2)}, u32[]{:S(2)}) collective-permute-start(bf16[32,8192]{1,0:T(8,128)(2,1)S(1)} %collective-permute-done.refs_0_), channel_id=1, source_target_pairs={{0,1},{1,0},{2,3},{3,2},{4,5},{5,4},{6,7},{7,6},{8,9},{9,8},{10,11... | collective-permute-start | bytes 1572872 | tf_op jit(solution)/shard_map/ppermute | solution.py:521
  51.6 1.3 collective-permute-start.4
  52.9 1.1 broadcast_select_fusion.1.refs_1_
  54.0 1.1 fusion.1
  55.1 20.4 %collective-permute-done.4 = bf16[32,8192]{1,0:T(8,128)(2,1)S(1)} collective-permute-done((bf16[32,8192]{1,0:T(8,128)(2,1)}, bf16[32,8192]{1,0:T(8,128)(2,1)S(1)}, u32[]{:S(2)}, u32[]{:S(2)}) %collective-permute-start.4) | collective-permute-done | bytes 524320 | tf_op jit(solution)/shard_map/ppermute | solution.py:521
  75.5 0.5 collective-permute-start.10
  76.0 1.3 collective-permute-start.12
  77.3 0.1 broadcast_select_fusion.2.refs_0_
  77.4 1.5 collective-permute-start.13
  78.9 0.0 copy-start.2
  78.9 5.8 %copy-done.2 = bf16[8192,1024]{1,0:T(8,128)(2,1)S(1)} copy-done((bf16[8192,1024]{1,0:T(8,128)(2,1)S(1)}, bf16[8192,1024]{1,0:T(8,128)(2,1)}, u32[]{:S(2)}) %copy-start.2) | copy-done | bytes 16777240
  84.6 6.0 %project.7 = (bf16[128,1024]{1,0:T(8,128)(2,1)S(1)}, bf16[64,256]{1,0:T(8,128)(2,1)S(1)}, bf16[64,256]{1,0:T(8,128)(2,1)S(1)}) custom-call(s32[1]{0:T(128)} %bitcast.member, bf16[32,8192]{1,0:T(8,128)(2,1)S(1)} %collective-permute-done.refs_0_, bf16[32,8192]{1,0:T(8,128)(2,1)} %collective-permute-done.1.refs_1_, ...), custom_call_target="tpu_custom_call" | custom-call | flops 10000000000 | bytes 1000 | tf_op jit(solution)/shard_map/project/pallas_call | solution.py:165
  90.7 1.6 %collective-permute-start.14 = (bf16[32,8192]{1,0:T(8,128)(2,1)S(1)}, bf16[32,8192]{1,0:T(8,128)(2,1)S(1)}, u32[]{:S(2)}, u32[]{:S(2)}) collective-permute-start(bf16[32,8192]{1,0:T(8,128)(2,1)S(1)} %broadcast_select_fusion.2.refs_0_), channel_id=1, source_target_pairs={{0,1},{1,0},{2,3},{3,2},{4,5},{5,4},{6,7},{7,6},{8,9},{9,8},{10,11... | collective-permute-start | bytes 1572872 | tf_op jit(solution)/shard_map/ppermute | solution.py:521
  92.3 0.5 collective-permute-start.15
  92.8 4.8 %project.8 = (bf16[128,1024]{1,0:T(8,128)(2,1)S(1)}, bf16[64,256]{1,0:T(8,128)(2,1)S(1)}, bf16[64,256]{1,0:T(8,128)(2,1)S(1)}) custom-call(s32[1]{0:T(128)} %bitcast.member, bf16[32,8192]{1,0:T(8,128)(2,1)S(1)} %broadcast_select_fusion.2.refs_0_, bf16[32,8192]{1,0:T(8,128)(2,1)S(1)} %broadcast_select_fusion.1.refs_1_, ...), custom_call_target="tpu_custom_call" | custom-call | flops 10000000000 | bytes 1000 | tf_op jit(solution)/shard_map/project/pallas_call | solution.py:165
  97.5 0.1 collective-permute-start.20
  97.6 1.0 slice_select_fusion.1.refs_1_
  98.6 1.5 collective-permute-start.11
  100.1 1.0 slice_select_fusion.refs_2_
  101.1 13.3 %collective-permute-done.11 = bf16[32,8192]{1,0:T(8,128)(2,1)S(1)} collective-permute-done((bf16[32,8192]{1,0:T(8,128)(2,1)S(1)}, bf16[32,8192]{1,0:T(8,128)(2,1)S(1)}, u32[]{:S(2)}, u32[]{:S(2)}) %collective-permute-start.11) | collective-permute-done | bytes 524320 | tf_op jit(solution)/shard_map/ppermute | solution.py:521
  114.4 2.4 %collective-permute-start.17 = (bf16[16,8192]{1,0:T(8,128)(2,1)S(1)}, bf16[16,8192]{1,0:T(8,128)(2,1)S(1)}, u32[]{:S(2)}, u32[]{:S(2)}) collective-permute-start(bf16[16,8192]{1,0:T(8,128)(2,1)S(1)} %slice_select_fusion.1.refs_1_), channel_id=1, source_target_pairs={{0,1},{1,0},{2,3},{3,2},{4,5},{5,4},{6,7},{7,6},{8,9},{9,8},{10,11... | collective-permute-start | bytes 786440 | tf_op jit(solution)/shard_map/ppermute | solution.py:521
  116.8 0.1 broadcast_select_fusion.refs_0_
  116.8 0.1 collective-permute-start.18
  116.9 0.7 collective-permute-start.16
  117.6 4.9 %project.9 = (bf16[128,1024]{1,0:T(8,128)(2,1)S(1)}, bf16[64,256]{1,0:T(8,128)(2,1)S(1)}, bf16[64,256]{1,0:T(8,128)(2,1)S(1)}) custom-call(s32[1]{0:T(128)} %bitcast.member, bf16[32,8192]{1,0:T(8,128)(2,1)S(1)} %broadcast_select_fusion.refs_0_, bf16[16,8192]{1,0:T(8,128)(2,1)S(1)} %slice_select_fusion.1.refs_1_, ...), custom_call_target="tpu_custom_call" | custom-call | flops 10000000000 | bytes 1000 | tf_op jit(solution)/shard_map/project/pallas_call | solution.py:165
  122.5 1.4 collective-permute-done.17.refs_1_
  123.9 5.2 %collective-permute-done.18.refs_2_ = bf16[16,8192]{1,0:T(8,128)(2,1)S(1)} collective-permute-done((bf16[16,8192]{1,0:T(8,128)(2,1)S(1)}, bf16[16,8192]{1,0:T(8,128)(2,1)S(1)}, u32[]{:S(2)}, u32[]{:S(2)}) %collective-permute-start.18) | collective-permute-done | bytes 262176 | tf_op jit(solution)/shard_map/ppermute | solution.py:521
  129.2 0.2 collective-permute-start.22
  129.3 1.8 %collective-permute-done.16.refs_0_ = bf16[32,8192]{1,0:T(8,128)(2,1)S(1)} collective-permute-done((bf16[32,8192]{1,0:T(8,128)(2,1)S(1)}, bf16[32,8192]{1,0:T(8,128)(2,1)S(1)}, u32[]{:S(2)}, u32[]{:S(2)}) %collective-permute-start.16) | collective-permute-done | bytes 524320 | tf_op jit(solution)/shard_map/ppermute | solution.py:521
  131.1 1.9 %collective-permute-start.23 = (bf16[64,256]{1,0:T(8,128)(2,1)S(1)}, bf16[64,256]{1,0:T(8,128)(2,1)S(1)}, u32[]{:S(2)}, u32[]{:S(2)}) collective-permute-start(bf16[64,256]{1,0:T(8,128)(2,1)S(1)} %get-tuple-element.34.refs_8_), channel_id=1, source_target_pairs={{0,12},{1,13},{2,14},{3,15},{4,8},{5,9},{6,10},{7,11},{8,4},{9,5},... | collective-permute-start | bytes 98312 | tf_op jit(solution)/shard_map/ppermute | solution.py:538
  133.1 1.8 %project.10 = (bf16[64,256]{1,0:T(8,128)(2,1)S(1)}, bf16[64,8192]{1,0:T(8,128)(2,1)S(1)}) custom-call(s32[1]{0:T(128)} %bitcast.member, bf16[32,8192]{1,0:T(8,128)(2,1)S(1)} %collective-permute-done.16.refs_0_, bf16[16,8192]{1,0:T(8,128)(2,1)S(1)} %collective-permute-done.17.refs_1_, bf16[16,8192]{1,0:T(8,128)(2,1)S(1)} %collective-permute-done.18.refs_2_, ...), custom_call_target="tpu_custom_call" | custom-call | flops 10000000000 | bytes 1000 | tf_op jit(solution)/shard_map/project/pallas_call | solution.py:165
  134.9 0.9 slice-done.2
  135.8 1.2 slice-done.3
  137.0 3.2 %project.11.refs_4_ = bf16[64,1024]{1,0:T(8,128)(2,1)S(1)} custom-call(s32[1]{0:T(128)} %bitcast.member, bf16[64,8192]{1,0:T(8,128)(2,1)S(1)} %get-tuple-element.30.refs_0_, bf16[1,8192]{1,0:T(2,128)(2,1)S(1)} %reshape.56.refs_1_.refs_3_.refs_4_.refs_5_, bf16[8192,1024]{1,0:T(8,128)(2,1)S(1)} %bitcast.9, ...), custom_call_target="tpu_custom_call" | custom-call | flops 10000000000 | bytes 1000 | tf_op jit(solution)/shard_map/project/pallas_call | solution.py:165
  140.2 1.9 %collective-permute-start.24 = (bf16[64,256]{1,0:T(8,128)(2,1)S(1)}, bf16[64,256]{1,0:T(8,128)(2,1)S(1)}, u32[]{:S(2)}, u32[]{:S(2)}) collective-permute-start(bf16[64,256]{1,0:T(8,128)(2,1)S(1)} %get-tuple-element.37.refs_11_), channel_id=1, source_target_pairs={{0,13},{1,12},{2,15},{3,14},{4,9},{5,8},{6,11},{7,10},{8,5},{9,4},... | collective-permute-start | bytes 98312 | tf_op jit(solution)/shard_map/ppermute | solution.py:538
  142.1 1.7 %collective-permute-start.25 = (bf16[64,256]{1,0:T(8,128)(2,1)S(1)}, bf16[64,256]{1,0:T(8,128)(2,1)S(1)}, u32[]{:S(2)}, u32[]{:S(2)}) collective-permute-start(bf16[64,256]{1,0:T(8,128)(2,1)S(1)} %get-tuple-element.36.refs_10_), channel_id=1, source_target_pairs={{0,14},{1,15},{2,12},{3,13},{4,10},{5,11},{6,8},{7,9},{8,6},{9,7},... | collective-permute-start | bytes 98312 | tf_op jit(solution)/shard_map/ppermute | solution.py:538
  143.8 2.7 %collective-permute-start.26 = (bf16[64,256]{1,0:T(8,128)(2,1)S(1)}, bf16[64,256]{1,0:T(8,128)(2,1)S(1)}, u32[]{:S(2)}, u32[]{:S(2)}) collective-permute-start(bf16[64,256]{1,0:T(8,128)(2,1)S(1)} %get-tuple-element.38.refs_12_), channel_id=1, source_target_pairs={{0,15},{1,14},{2,13},{3,12},{4,11},{5,10},{6,9},{7,8},{8,7},{9,6},... | collective-permute-start | bytes 98312 | tf_op jit(solution)/shard_map/ppermute | solution.py:538
  146.6 3.4 %attend.1 = bf16[512,1024]{1,0:T(8,128)(2,1)} custom-call(s32[1]{0:T(128)} %bitcast.member, bf16[64,1024]{1,0:T(8,128)(2,1)S(1)} %get-tuple-element.23.refs_0_, bf16[128,1024]{1,0:T(8,128)(2,1)S(1)} %get-tuple-element.25.refs_1_, bf16[128,1024]{1,0:T(8,128)(2,1)S(1)} %get-tuple-element.26.refs_2_, bf16[128,1024]{1,0:T(8,128)(2,1)S(1)} %get-tuple-element.29.refs_3_, ...), custom_call_target="tpu_custom_call" | custom-call | flops 5000000000 | bytes 1000 | tf_op jit(solution)/shard_map/attend/pallas_call | solution.py:243
  150.0 1.3 decode_new.1
  (45 shorter events, 0.1 us)
Async XLA Ops:
  2.5 46.6 %collective-permute-start = (bf16[32,8192]{1,0:T(8,128)(2,1)}, bf16[32,8192]{1,0:T(8,128)(2,1)S(1)}, u32[]{:S(2)}, u32[]{:S(2)}) collective-permute-start(bf16[32,8192]{1,0:T(8,128)(2,1)} %slice_bitcast_fusion), channel_id=1, source_target_pairs={{0,2},{1,3},{2,0},{3,1},{4,6},{5,7},{6,4},{7,5},{8,10},{9,11},{10,... | collective-permute-start | bytes 1572872 | tf_op jit(solution)/shard_map/ppermute | solution.py:521
  5.6 43.6 %collective-permute-start.3 = (bf16[32,8192]{1,0:T(8,128)(2,1)}, bf16[32,8192]{1,0:T(8,128)(2,1)}, u32[]{:S(2)}, u32[]{:S(2)}) collective-permute-start(bf16[32,8192]{1,0:T(8,128)(2,1)} %slice_bitcast_fusion), channel_id=1, source_target_pairs={{2,4},{3,5},{4,2},{5,3},{10,12},{11,13},{12,10},{13,11},{18,20},{1... | collective-permute-start | bytes 1572872 | tf_op jit(solution)/shard_map/ppermute | solution.py:521
  7.0 70.3 %collective-permute-start.2 = (bf16[64,8192]{1,0:T(8,128)(2,1)}, bf16[64,8192]{1,0:T(8,128)(2,1)}, u32[]{:S(2)}, u32[]{:S(2)}) collective-permute-start(bf16[64,8192]{1,0:T(8,128)(2,1)} %bitcast.5), channel_id=1, source_target_pairs={{0,1},{1,0},{2,3},{3,2},{4,5},{5,4},{6,7},{7,6},{8,9},{9,8},{10,11... | collective-permute-start | bytes 3145736 | tf_op jit(solution)/shard_map/ppermute | solution.py:521
  8.5 11.4 %copy-start.11 = (bf16[8192]{0:T(1024)(128)(2,1)S(1)}, bf16[8192]{0:T(1024)(128)(2,1)}, u32[]{:S(2)}) copy-start(bf16[8192]{0:T(1024)(128)(2,1)} %param.11) | copy-start | bytes 49156
  10.4 20.0 %copy-start = (bf16[1,64,8192]{2,1,0:T(8,128)(2,1)S(1)}, bf16[1,64,8192]{2,1,0:T(8,128)(2,1)}, u32[]{:S(2)}) copy-start(bf16[1,64,8192]{2,1,0:T(8,128)(2,1)} %param.10) | copy-start | bytes 3145732
  10.4 18.6 %collective-permute-start.1 = (bf16[32,8192]{1,0:T(8,128)(2,1)}, bf16[32,8192]{1,0:T(8,128)(2,1)}, u32[]{:S(2)}, u32[]{:S(2)}) collective-permute-start(bf16[32,8192]{1,0:T(8,128)(2,1)} %slice.23), channel_id=1, source_target_pairs={{0,2},{1,3},{2,0},{3,1},{4,6},{5,7},{6,4},{7,5},{8,10},{9,11},{10,... | collective-permute-start | bytes 1572872 | tf_op jit(solution)/shard_map/ppermute | solution.py:521
  14.1 6.9 %collective-permute-start.6 = (bf16[32,8192]{1,0:T(8,128)(2,1)}, bf16[32,8192]{1,0:T(8,128)(2,1)}, u32[]{:S(2)}, u32[]{:S(2)}) collective-permute-start(bf16[32,8192]{1,0:T(8,128)(2,1)} %slice.23), channel_id=1, source_target_pairs={{2,4},{3,5},{4,2},{5,3},{10,12},{11,13},{12,10},{13,11},{18,20},{1... | collective-permute-start | bytes 1572872 | tf_op jit(solution)/shard_map/ppermute | solution.py:521
  15.6 0.8 copy-start.6
  16.4 0.7 copy-start.8
  17.1 0.7 copy-start.9
  17.7 0.7 copy-start.10
  21.0 28.8 %collective-permute-start.7 = (bf16[32,8192]{1,0:T(8,128)(2,1)}, bf16[32,8192]{1,0:T(8,128)(2,1)}, u32[]{:S(2)}, u32[]{:S(2)}) collective-permute-start(bf16[32,8192]{1,0:T(8,128)(2,1)} %collective-permute-done.6), channel_id=1, source_target_pairs={{2,0},{3,1},{4,6},{5,7},{10,8},{11,9},{12,14},{13,15},{18,16},{19,... | collective-permute-start | bytes 1572872 | tf_op jit(solution)/shard_map/ppermute | solution.py:521
  29.0 22.6 %collective-permute-start.8 = (bf16[32,8192]{1,0:T(8,128)(2,1)}, bf16[32,8192]{1,0:T(8,128)(2,1)}, u32[]{:S(2)}, u32[]{:S(2)}) collective-permute-start(bf16[32,8192]{1,0:T(8,128)(2,1)} %collective-permute-done.1.refs_1_), channel_id=1, source_target_pairs={{2,4},{3,5},{4,2},{5,3},{10,12},{11,13},{12,10},{13,11},{18,20},{1... | collective-permute-start | bytes 1572872 | tf_op jit(solution)/shard_map/ppermute | solution.py:521
  30.5 5.8 %copy-start.1 = (bf16[8192,1024]{1,0:T(8,128)(2,1)S(1)}, bf16[8192,1024]{1,0:T(8,128)(2,1)}, u32[]{:S(2)}) copy-start(bf16[8192,1024]{1,0:T(8,128)(2,1)} %refs_2_.3) | copy-start | bytes 50331652
  36.3 2.2 %copy-start.4 = (bf16[8192,256]{1,0:T(8,128)(2,1)S(1)}, bf16[8192,256]{1,0:T(8,128)(2,1)}, u32[]{:S(2)}) copy-start(bf16[8192,256]{1,0:T(8,128)(2,1)} %refs_4_.3) | copy-start | bytes 12582916
  38.4 4.6 %copy-start.7 = (bf16[4,2048]{1,0:T(4,128)(2,1)S(1)}, bf16[4,2048]{1,0:T(4,128)(2,1)}, u32[]{:S(2)}) copy-start(bf16[4,2048]{1,0:T(4,128)(2,1)} %own_ref.1) | copy-start | bytes 49156
  43.0 2.8 %copy-start.3 = (bf16[96,16,2048]{2,1,0:T(8,128)(2,1)S(1)}, bf16[96,16,2048]{2,1,0:T(8,128)(2,1)}, u32[]{:S(2)}) copy-start(bf16[96,16,2048]{2,1,0:T(8,128)(2,1)} %pool.1) | copy-start | bytes 18874372
  45.8 33.0 %copy-start.5 = (bf16[8192,256]{1,0:T(8,128)(2,1)S(1)}, bf16[8192,256]{1,0:T(8,128)(2,1)}, u32[]{:S(2)}) copy-start(bf16[8192,256]{1,0:T(8,128)(2,1)} %refs_4_.3) | copy-start | bytes 12582916
  49.1 91.1 %collective-permute-start.19 = (bf16[64,256]{1,0:T(8,128)(2,1)S(1)}, bf16[64,256]{1,0:T(8,128)(2,1)S(1)}, u32[]{:S(2)}, u32[]{:S(2)}) collective-permute-start(bf16[64,256]{1,0:T(8,128)(2,1)S(1)} %get-tuple-element.31.refs_5_), channel_id=1, source_target_pairs={{0,8},{1,9},{2,10},{3,11},{4,12},{5,13},{6,14},{7,15},{8,0},{9,1},... | collective-permute-start | bytes 98312 | tf_op jit(solution)/shard_map/ppermute | solution.py:538
  49.2 26.8 %collective-permute-start.5 = (bf16[32,8192]{1,0:T(8,128)(2,1)S(1)}, bf16[32,8192]{1,0:T(8,128)(2,1)S(1)}, u32[]{:S(2)}, u32[]{:S(2)}) collective-permute-start(bf16[32,8192]{1,0:T(8,128)(2,1)S(1)} %collective-permute-done.refs_0_), channel_id=1, source_target_pairs={{2,4},{3,5},{4,2},{5,3},{10,12},{11,13},{12,10},{13,11},{18,20},{1... | collective-permute-start | bytes 1572872 | tf_op jit(solution)/shard_map/ppermute | solution.py:521
  49.9 40.8 %collective-permute-start.9 = (bf16[32,8192]{1,0:T(8,128)(2,1)S(1)}, bf16[32,8192]{1,0:T(8,128)(2,1)S(1)}, u32[]{:S(2)}, u32[]{:S(2)}) collective-permute-start(bf16[32,8192]{1,0:T(8,128)(2,1)S(1)} %collective-permute-done.refs_0_), channel_id=1, source_target_pairs={{0,1},{1,0},{2,3},{3,2},{4,5},{5,4},{6,7},{7,6},{8,9},{9,8},{10,11... | collective-permute-start | bytes 1572872 | tf_op jit(solution)/shard_map/ppermute | solution.py:521
  51.6 23.9 %collective-permute-start.4 = (bf16[32,8192]{1,0:T(8,128)(2,1)}, bf16[32,8192]{1,0:T(8,128)(2,1)S(1)}, u32[]{:S(2)}, u32[]{:S(2)}) collective-permute-start(bf16[32,8192]{1,0:T(8,128)(2,1)} %collective-permute-done.3), channel_id=1, source_target_pairs={{2,0},{3,1},{4,6},{5,7},{10,8},{11,9},{12,14},{13,15},{18,16},{19,... | collective-permute-start | bytes 1572872 | tf_op jit(solution)/shard_map/ppermute | solution.py:521
  75.5 16.8 %collective-permute-start.10 = (bf16[32,8192]{1,0:T(8,128)(2,1)}, bf16[32,8192]{1,0:T(8,128)(2,1)S(1)}, u32[]{:S(2)}, u32[]{:S(2)}) collective-permute-start(bf16[32,8192]{1,0:T(8,128)(2,1)} %collective-permute-done.1.refs_1_), channel_id=1, source_target_pairs={{0,1},{1,0},{2,3},{3,2},{4,5},{5,4},{6,7},{7,6},{8,9},{9,8},{10,11... | collective-permute-start | bytes 1572872 | tf_op jit(solution)/shard_map/ppermute | solution.py:521
  76.0 22.6 %collective-permute-start.12 = (bf16[16,8192]{1,0:T(8,128)(2,1)S(1)}, bf16[16,8192]{1,0:T(8,128)(2,1)S(1)}, u32[]{:S(2)}, u32[]{:S(2)}) collective-permute-start(bf16[16,8192]{1,0:T(8,128)(2,1)S(1)} %get-tuple-element.45), channel_id=1, source_target_pairs={{2,0},{3,1},{4,6},{5,7},{10,8},{11,9},{12,14},{13,15},{18,16},{19,... | collective-permute-start | bytes 786440 | tf_op jit(solution)/shard_map/ppermute | solution.py:521
  77.4 20.2 %collective-permute-start.13 = (bf16[16,8192]{1,0:T(8,128)(2,1)S(1)}, bf16[16,8192]{1,0:T(8,128)(2,1)S(1)}, u32[]{:S(2)}, u32[]{:S(2)}) collective-permute-start(bf16[16,8192]{1,0:T(8,128)(2,1)S(1)} %get-tuple-element.44), channel_id=1, source_target_pairs={{2,0},{3,1},{4,6},{5,7},{10,8},{11,9},{12,14},{13,15},{18,16},{19,... | collective-permute-start | bytes 786440 | tf_op jit(solution)/shard_map/ppermute | solution.py:521
  78.9 5.8 %copy-start.2 = (bf16[8192,1024]{1,0:T(8,128)(2,1)S(1)}, bf16[8192,1024]{1,0:T(8,128)(2,1)}, u32[]{:S(2)}) copy-start(bf16[8192,1024]{1,0:T(8,128)(2,1)} %refs_2_.3) | copy-start | bytes 50331652
  90.7 26.2 %collective-permute-start.14 = (bf16[32,8192]{1,0:T(8,128)(2,1)S(1)}, bf16[32,8192]{1,0:T(8,128)(2,1)S(1)}, u32[]{:S(2)}, u32[]{:S(2)}) collective-permute-start(bf16[32,8192]{1,0:T(8,128)(2,1)S(1)} %broadcast_select_fusion.2.refs_0_), channel_id=1, source_target_pairs={{0,1},{1,0},{2,3},{3,2},{4,5},{5,4},{6,7},{7,6},{8,9},{9,8},{10,11... | collective-permute-start | bytes 1572872 | tf_op jit(solution)/shard_map/ppermute | solution.py:521
  92.3 24.7 %collective-permute-start.15 = (bf16[32,8192]{1,0:T(8,128)(2,1)S(1)}, bf16[32,8192]{1,0:T(8,128)(2,1)S(1)}, u32[]{:S(2)}, u32[]{:S(2)}) collective-permute-start(bf16[32,8192]{1,0:T(8,128)(2,1)S(1)} %broadcast_select_fusion.1.refs_1_), channel_id=1, source_target_pairs={{0,1},{1,0},{2,3},{3,2},{4,5},{5,4},{6,7},{7,6},{8,9},{9,8},{10,11... | collective-permute-start | bytes 1572872 | tf_op jit(solution)/shard_map/ppermute | solution.py:521
  97.5 44.6 %collective-permute-start.20 = (bf16[64,256]{1,0:T(8,128)(2,1)S(1)}, bf16[64,256]{1,0:T(8,128)(2,1)S(1)}, u32[]{:S(2)}, u32[]{:S(2)}) collective-permute-start(bf16[64,256]{1,0:T(8,128)(2,1)S(1)} %get-tuple-element.33.refs_7_), channel_id=1, source_target_pairs={{0,9},{1,8},{2,11},{3,10},{4,13},{5,12},{6,15},{7,14},{8,1},{9,0},... | collective-permute-start | bytes 98312 | tf_op jit(solution)/shard_map/ppermute | solution.py:538
  98.6 15.8 %collective-permute-start.11 = (bf16[32,8192]{1,0:T(8,128)(2,1)S(1)}, bf16[32,8192]{1,0:T(8,128)(2,1)S(1)}, u32[]{:S(2)}, u32[]{:S(2)}) collective-permute-start(bf16[32,8192]{1,0:T(8,128)(2,1)S(1)} %collective-permute-done.5), channel_id=1, source_target_pairs={{2,0},{3,1},{4,6},{5,7},{10,8},{11,9},{12,14},{13,15},{18,16},{19,... | collective-permute-start | bytes 1572872 | tf_op jit(solution)/shard_map/ppermute | solution.py:521
  114.4 9.5 %collective-permute-start.17 = (bf16[16,8192]{1,0:T(8,128)(2,1)S(1)}, bf16[16,8192]{1,0:T(8,128)(2,1)S(1)}, u32[]{:S(2)}, u32[]{:S(2)}) collective-permute-start(bf16[16,8192]{1,0:T(8,128)(2,1)S(1)} %slice_select_fusion.1.refs_1_), channel_id=1, source_target_pairs={{0,1},{1,0},{2,3},{3,2},{4,5},{5,4},{6,7},{7,6},{8,9},{9,8},{10,11... | collective-permute-start | bytes 786440 | tf_op jit(solution)/shard_map/ppermute | solution.py:521
  116.8 12.3 %collective-permute-start.18 = (bf16[16,8192]{1,0:T(8,128)(2,1)S(1)}, bf16[16,8192]{1,0:T(8,128)(2,1)S(1)}, u32[]{:S(2)}, u32[]{:S(2)}) collective-permute-start(bf16[16,8192]{1,0:T(8,128)(2,1)S(1)} %slice_select_fusion.refs_2_), channel_id=1, source_target_pairs={{0,1},{1,0},{2,3},{3,2},{4,5},{5,4},{6,7},{7,6},{8,9},{9,8},{10,11... | collective-permute-start | bytes 786440 | tf_op jit(solution)/shard_map/ppermute | solution.py:521
  116.9 14.2 %collective-permute-start.16 = (bf16[32,8192]{1,0:T(8,128)(2,1)S(1)}, bf16[32,8192]{1,0:T(8,128)(2,1)S(1)}, u32[]{:S(2)}, u32[]{:S(2)}) collective-permute-start(bf16[32,8192]{1,0:T(8,128)(2,1)S(1)} %collective-permute-done.14.refs_3_), channel_id=1, source_target_pairs={{0,2},{1,3},{2,0},{3,1},{4,6},{5,7},{6,4},{7,5},{8,10},{9,11},{10,... | collective-permute-start | bytes 1572872 | tf_op jit(solution)/shard_map/ppermute | solution.py:521
  123.9 19.9 %collective-permute-start.21 = (bf16[64,256]{1,0:T(8,128)(2,1)S(1)}, bf16[64,256]{1,0:T(8,128)(2,1)S(1)}, u32[]{:S(2)}, u32[]{:S(2)}) collective-permute-start(bf16[64,256]{1,0:T(8,128)(2,1)S(1)} %get-tuple-element.32.refs_6_), channel_id=1, source_target_pairs={{0,10},{1,11},{2,8},{3,9},{4,14},{5,15},{6,12},{7,13},{8,2},{9,3},... | collective-permute-start | bytes 98312 | tf_op jit(solution)/shard_map/ppermute | solution.py:538
  129.2 20.8 %collective-permute-start.22 = (bf16[64,256]{1,0:T(8,128)(2,1)S(1)}, bf16[64,256]{1,0:T(8,128)(2,1)S(1)}, u32[]{:S(2)}, u32[]{:S(2)}) collective-permute-start(bf16[64,256]{1,0:T(8,128)(2,1)S(1)} %get-tuple-element.35.refs_9_), channel_id=1, source_target_pairs={{0,11},{1,10},{2,9},{3,8},{4,15},{5,14},{6,13},{7,12},{8,3},{9,2},... | collective-permute-start | bytes 98312 | tf_op jit(solution)/shard_map/ppermute | solution.py:538
  131.1 3.7 %slice-start = ((s8[16777216]{0:T(1024)(128)(4,1)}), s8[4194304]{0:T(1024)(128)(4,1)S(1)}, s32[]{:S(2)}) async-start(s8[16777216]{0:T(1024)(128)(4,1)} %bitcast.8), calls=%async_computation | async-start | bytes 8388608
  131.1 3.8 %slice-start.1 = ((s8[16777216]{0:T(1024)(128)(4,1)}), s8[4194304]{0:T(1024)(128)(4,1)S(1)}, s32[]{:S(2)}) async-start(s8[16777216]{0:T(1024)(128)(4,1)} %bitcast.8), calls=%async_computation.1 | async-start | bytes 8388608
  131.1 4.7 %slice-start.2 = ((s8[16777216]{0:T(1024)(128)(4,1)}), s8[4194304]{0:T(1024)(128)(4,1)S(1)}, s32[]{:S(2)}) async-start(s8[16777216]{0:T(1024)(128)(4,1)} %bitcast.8), calls=%async_computation.2 | async-start | bytes 8388608
  131.1 5.8 %slice-start.3 = ((s8[16777216]{0:T(1024)(128)(4,1)}), s8[4194304]{0:T(1024)(128)(4,1)S(1)}, s32[]{:S(2)}) async-start(s8[16777216]{0:T(1024)(128)(4,1)} %bitcast.8), calls=%async_computation.3 | async-start | bytes 8388608
  131.1 18.9 %collective-permute-start.23 = (bf16[64,256]{1,0:T(8,128)(2,1)S(1)}, bf16[64,256]{1,0:T(8,128)(2,1)S(1)}, u32[]{:S(2)}, u32[]{:S(2)}) collective-permute-start(bf16[64,256]{1,0:T(8,128)(2,1)S(1)} %get-tuple-element.34.refs_8_), channel_id=1, source_target_pairs={{0,12},{1,13},{2,14},{3,15},{4,8},{5,9},{6,10},{7,11},{8,4},{9,5},... | collective-permute-start | bytes 98312 | tf_op jit(solution)/shard_map/ppermute | solution.py:538
  140.2 9.8 %collective-permute-start.24 = (bf16[64,256]{1,0:T(8,128)(2,1)S(1)}, bf16[64,256]{1,0:T(8,128)(2,1)S(1)}, u32[]{:S(2)}, u32[]{:S(2)}) collective-permute-start(bf16[64,256]{1,0:T(8,128)(2,1)S(1)} %get-tuple-element.37.refs_11_), channel_id=1, source_target_pairs={{0,13},{1,12},{2,15},{3,14},{4,9},{5,8},{6,11},{7,10},{8,5},{9,4},... | collective-permute-start | bytes 98312 | tf_op jit(solution)/shard_map/ppermute | solution.py:538
  142.1 7.9 %collective-permute-start.25 = (bf16[64,256]{1,0:T(8,128)(2,1)S(1)}, bf16[64,256]{1,0:T(8,128)(2,1)S(1)}, u32[]{:S(2)}, u32[]{:S(2)}) collective-permute-start(bf16[64,256]{1,0:T(8,128)(2,1)S(1)} %get-tuple-element.36.refs_10_), channel_id=1, source_target_pairs={{0,14},{1,15},{2,12},{3,13},{4,10},{5,11},{6,8},{7,9},{8,6},{9,7},... | collective-permute-start | bytes 98312 | tf_op jit(solution)/shard_map/ppermute | solution.py:538
  143.8 6.2 %collective-permute-start.26 = (bf16[64,256]{1,0:T(8,128)(2,1)S(1)}, bf16[64,256]{1,0:T(8,128)(2,1)S(1)}, u32[]{:S(2)}, u32[]{:S(2)}) collective-permute-start(bf16[64,256]{1,0:T(8,128)(2,1)S(1)} %get-tuple-element.38.refs_12_), channel_id=1, source_target_pairs={{0,15},{1,14},{2,13},{3,12},{4,11},{5,10},{6,9},{7,8},{8,7},{9,6},... | collective-permute-start | bytes 98312 | tf_op jit(solution)/shard_map/ppermute | solution.py:538

commit v5 on v4

--- a/solution.py
+++ b/solution.py
@@ -542,23 +542,20 @@
             source = bar((tokens, own[0]))[0] if c else tokens
             own.append(source[c * half : (c + 1) * half])
         y, e1, e2 = {}, {}, {}
+        e1[0] = move(tokens, outer)
         y[0] = move(tokens, side)
         for c in range(2):
-            e1[c] = move(own[c], outer)
             e2[c] = move(own[c], inner)
         dec_heads, allowed, limits = prepared()
         q0, kv0 = project([tokens], place((0, 0)), member_ref, gain, [q_job, kv_job])
         piece = {0: hand(kv0, 0)}
+        y[2] = move(e1[0], side)
         for c in range(2):
             e1[2 + c] = move(e2[c], outward)
-            e2[2 + c] = move(e1[c], inner)
-            y[2 + c] = move(e1[c], side)
+            passed = e1[0][c * half : (c + 1) * half]
+            e2[2 + c] = move(passed, inner)
         qa, kv2, kv1 = project(
-            [e1[0], e1[1], y[0]],
-            place((2, 0), (2, half), (1, 0)),
-            member_ref,
-            gain,
-            [q_job, kv_pair],
+            [e1[0], y[0]], place((2, 0), (1, 0)), member_ref, gain, [q_job, kv_pair]
         )
         piece[2], piece[1] = hand(kv2, 2), hand(kv1, 1)
         two, three = {}, {}
@@ -571,8 +568,8 @@
                 e1["5b"] = move(e2[3][quarter:], outward)
             y[4 + c] = move(two[c], side)
         qb, kv4, kv3 = project(
-            [two[0], two[1], y[2], y[3]],
-            place((4, 0), (4, half), (3, 0), (3, half)),
+            [two[0], two[1], y[2]],
+            place((4, 0), (4, half), (3, 0)),
             member_ref,
             gain,
             [q_job, kv_pair],

time: 152 us -> 150 us (0.987)
  starting transfers between devices: 36.2 us -> 31.1 us
  waiting for transfers between devices: 48.8 us -> 52.9 us
    ppermute x19 -> x17, starting transfers between devices: 27.6 us -> 23.6 us  [move(): return lax.ppermute(value, 'tp', pairs)]
    ppermute x19 -> x17, waiting for transfers between devices: 48.8 us -> 51.3 us  [move(): return lax.ppermute(value, 'tp', pairs)]
    ppermute x8, waiting for transfers between devices: 0.02 us -> 1.57 us  [hand(): return lax.ppermute(kv, ('role', 'tp'), pairs)]
    unnamed x32 -> x30, local copies, waits for them, and re-layouts: 21.4 us -> 21.5 us
  transfers between devices with their start and end apart: 27 -> 25, of which waited for: 6 -> 7; matrix products, arithmetic and copies ran while one was open for 5% -> 5% of each run, Pallas kernels for 22% -> 22%
where the time goes in v5:
time: 150 us; the launch traced here: 149 us
  waiting for transfers between devices  52.9 us (35%)
  Pallas kernels  34.7 us (23%)
  starting transfers between devices  31.1 us (21%)
  local copies, waits for them, and re-layouts  26.1 us (17%)
  other arithmetic  3.16 us (2%)
    ppermute x17, waiting for transfers between devices, move(): return lax.ppermute(value, 'tp', pairs)  51.3 us
    pallas_call x6, Pallas kernels, project(): pl.pallas_call(functools.partial(project_kernel, chunk_rows, [job[3] for...  25.1 us
    ppermute x17, starting transfers between devices, move(): return lax.ppermute(value, 'tp', pairs)  23.6 us
    unnamed x30, local copies, waits for them, and re-layouts  21.5 us
    ppermute x8, starting transfers between devices, hand(): return lax.ppermute(kv, ('role', 'tp'), pairs)  7.49 us
    slice x2, local copies, waits for them, and re-layouts, local(): own.append(source[c * half:(c + 1) * half])  3.77 us
    pallas_call x1, Pallas kernels, attend(): pl.pallas_call(functools.partial(attend_kernel, tuple(chunk_rows), len(qu...  3.45 us
    pallas_call x1, Pallas kernels, decode_old(): pl.pallas_call(decode_old_kernel, out_shape=[jax.ShapeDtypeStruct((KVH, G...  3.24 us
  transfers between devices with their start and end apart: 25, of which 7 were waited for; matrix products, arithmetic and copies ran while one was open for 5% of the time, Pallas kernels for 22%

profile of v5, /device:TPU:0, one launch (start us, length us, event | category | flops | bytes accessed | tf_op | source)
XLA Modules:
  0.0 149.0 jit_solution(5799676726211108199)
XLA Ops:
  0.6 3.1 %collective-permute-start = (bf16[64,8192]{1,0:T(8,128)(2,1)}, bf16[64,8192]{1,0:T(8,128)(2,1)S(1)}, u32[]{:S(2)}, u32[]{:S(2)}) collective-permute-start(bf16[64,8192]{1,0:T(8,128)(2,1)} %bitcast.5), channel_id=1, source_target_pairs={{0,2},{1,3},{2,0},{3,1},{4,6},{5,7},{6,4},{7,5},{8,10},{9,11},{10,... | collective-permute-start | bytes 3145736 | tf_op jit(solution)/shard_map/ppermute | solution.py:521
  3.7 1.5 %collective-permute-start.1 = (bf16[64,8192]{1,0:T(8,128)(2,1)}, bf16[64,8192]{1,0:T(8,128)(2,1)}, u32[]{:S(2)}, u32[]{:S(2)}) collective-permute-start(bf16[64,8192]{1,0:T(8,128)(2,1)} %bitcast.6), channel_id=1, source_target_pairs={{0,1},{1,0},{2,3},{3,2},{4,5},{5,4},{6,7},{7,6},{8,9},{9,8},{10,11... | collective-permute-start | bytes 3145736 | tf_op jit(solution)/shard_map/ppermute | solution.py:521
  5.3 1.9 %slice_bitcast_fusion = bf16[32,8192]{1,0:T(8,128)(2,1)} fusion(bf16[1,64,8192]{2,1,0:T(8,128)(2,1)} %param.10), kind=kLoop, calls=%fused_computation | loop fusion | bytes 1048576 | tf_op jit(solution)/shard_map/slice | solution.py:543
  7.2 0.7 collective-permute-start.2
  7.9 1.9 %slice.30 = bf16[32,8192]{1,0:T(8,128)(2,1)} slice(bf16[64,8192]{1,0:T(8,128)(2,1)} %bitcast.7), slice={[32:64], [0:8192]} | slice | bytes 1048576 | tf_op jit(solution)/shard_map/slice | solution.py:543
  9.7 1.5 collective-permute-start.5
  11.2 0.7 reshape.56.refs_1_.refs_2_.refs_3_.refs_5_
  12.0 1.0 fusion
  13.0 0.0 copy-start
  13.0 1.2 copy-done
  14.2 5.8 %copy-done.1 = bf16[8192,1024]{1,0:T(8,128)(2,1)S(1)} copy-done((bf16[8192,1024]{1,0:T(8,128)(2,1)S(1)}, bf16[8192,1024]{1,0:T(8,128)(2,1)}, u32[]{:S(2)}) %copy-start.1) | copy-done | bytes 16777240
  20.0 2.2 %copy-done.4 = bf16[8192,256]{1,0:T(8,128)(2,1)S(1)} copy-done((bf16[8192,256]{1,0:T(8,128)(2,1)S(1)}, bf16[8192,256]{1,0:T(8,128)(2,1)}, u32[]{:S(2)}) %copy-start.4) | copy-done | bytes 4194328
  22.2 4.6 %project.6 = (bf16[64,1024]{1,0:T(8,128)(2,1)S(1)}, bf16[64,256]{1,0:T(8,128)(2,1)S(1)}) custom-call(s32[1]{0:T(128)} %bitcast.member, bf16[64,8192]{1,0:T(8,128)(2,1)S(1)} %bitcast.8, bf16[1,8192]{1,0:T(2,128)(2,1)S(1)} %reshape.56.refs_1_.refs_2_.refs_3_.refs_5_, bf16[8192,1024]{1,0:T(8,128)(2,1)S(1)} %copy-done.1, ...), custom_call_target="tpu_custom_call" | custom-call | flops 10000000000 | bytes 1000 | tf_op jit(solution)/shard_map/project/pallas_call | solution.py:165
  26.7 0.0 copy-start.7
  26.8 0.1 collective-permute-start.17
  26.9 1.5 %decode_prepare.1 = (bf16[2048,256]{1,0:T(8,128)(2,1)S(1)}, f32[64,256]{1,0:T(8,128)S(1)}, s32[96,256]{1,0:T(8,128)S(1)}) custom-call(s32[4,24]{1,0:T(4,128)S(1)} %copy-done.8, s32[4]{0:T(128)S(1)} %copy-done.9, s32[1,4]{1,0:T(1,128)S(1)} %copy-done.10, bf16[4,8192]{1,0:T(4,128)(2,1)S(1)} %copy-done.6), custom_call_target="tpu_custom_call" | custom-call | flops 10000000000 | bytes 1000 | tf_op jit(solution)/shard_map/decode_prepare/pallas_call | solution.py:308
  28.5 0.0 copy-start.3
  28.5 2.8 %copy-done.3 = bf16[96,16,2048]{2,1,0:T(8,128)(2,1)S(1)} copy-done((bf16[96,16,2048]{2,1,0:T(8,128)(2,1)S(1)}, bf16[96,16,2048]{2,1,0:T(8,128)(2,1)}, u32[]{:S(2)}) %copy-start.3) | copy-done | bytes 6291480
  31.2 3.2 %decode_old.1 = (f32[8,32,128]{2,1,0:T(8,128)S(1)}, f32[2,256]{1,0:T(2,128)S(1)}) custom-call(bf16[2048,256]{1,0:T(8,128)(2,1)S(1)} %get-tuple-element.39.queries.q_ref, s32[96,256]{1,0:T(8,128)S(1)} %get-tuple-element.41.limits, bf16[4,2048]{1,0:T(4,128)(2,1)S(1)} %copy-done.7, bf16[96,16,2048]{2,1,0:T(8,128)(2,1)S(1)} %copy-done.3), custom_call_target="tpu_custom_call" | custom-call | flops 5000000000 | bytes 1000 | tf_op jit(solution)/shard_map/decode_old/pallas_call | solution.py:384
  34.5 1.3 collective-permute-start.3
  35.8 1.3 collective-permute-start.6
  37.1 0.1 fusion.1
  37.2 0.7 collective-permute-start.4
  37.9 0.7 collective-permute-start.7
  38.6 0.0 copy-start.2
  38.6 5.8 %copy-done.2 = bf16[8192,1024]{1,0:T(8,128)(2,1)S(1)} copy-done((bf16[8192,1024]{1,0:T(8,128)(2,1)S(1)}, bf16[8192,1024]{1,0:T(8,128)(2,1)}, u32[]{:S(2)}) %copy-start.2) | copy-done | bytes 16777240
  44.4 5.8 %project.7 = (bf16[128,1024]{1,0:T(8,128)(2,1)S(1)}, bf16[64,256]{1,0:T(8,128)(2,1)S(1)}, bf16[64,256]{1,0:T(8,128)(2,1)S(1)}) custom-call(s32[1]{0:T(128)} %bitcast.member, bf16[64,8192]{1,0:T(8,128)(2,1)S(1)} %collective-permute-done.refs_0_, bf16[64,8192]{1,0:T(8,128)(2,1)} %collective-permute-done.1.refs_1_, ...), custom_call_target="tpu_custom_call" | custom-call | flops 10000000000 | bytes 1000 | tf_op jit(solution)/shard_map/project/pallas_call | solution.py:165
  50.1 14.2 %collective-permute-done.6 = bf16[32,8192]{1,0:T(8,128)(2,1)S(1)} collective-permute-done((bf16[32,8192]{1,0:T(8,128)(2,1)}, bf16[32,8192]{1,0:T(8,128)(2,1)S(1)}, u32[]{:S(2)}, u32[]{:S(2)}) %collective-permute-start.6) | collective-permute-done | bytes 524320 | tf_op jit(solution)/shard_map/ppermute | solution.py:521
  64.4 1.5 %collective-permute-start.8 = (bf16[64,8192]{1,0:T(8,128)(2,1)S(1)}, bf16[64,8192]{1,0:T(8,128)(2,1)S(1)}, u32[]{:S(2)}, u32[]{:S(2)}) collective-permute-start(bf16[64,8192]{1,0:T(8,128)(2,1)S(1)} %collective-permute-done.refs_0_), channel_id=1, source_target_pairs={{0,1},{1,0},{2,3},{3,2},{4,5},{5,4},{6,7},{7,6},{8,9},{9,8},{10,11... | collective-permute-start | bytes 3145736 | tf_op jit(solution)/shard_map/ppermute | solution.py:521
  65.9 0.1 broadcast_select_fusion.1.refs_1_
  66.0 1.5 collective-permute-start.10
  67.5 1.3 collective-permute-start.11
  68.8 0.1 broadcast_select_fusion.2.refs_0_
  68.9 14.5 %collective-permute-done.11 = bf16[16,8192]{1,0:T(8,128)(2,1)S(1)} collective-permute-done((bf16[16,8192]{1,0:T(8,128)(2,1)S(1)}, bf16[16,8192]{1,0:T(8,128)(2,1)S(1)}, u32[]{:S(2)}, u32[]{:S(2)}) %collective-permute-start.11) | collective-permute-done | bytes 262176 | tf_op jit(solution)/shard_map/ppermute | solution.py:521
  83.4 1.5 %collective-permute-start.12 = (bf16[32,8192]{1,0:T(8,128)(2,1)S(1)}, bf16[32,8192]{1,0:T(8,128)(2,1)S(1)}, u32[]{:S(2)}, u32[]{:S(2)}) collective-permute-start(bf16[32,8192]{1,0:T(8,128)(2,1)S(1)} %broadcast_select_fusion.2.refs_0_), channel_id=1, source_target_pairs={{0,1},{1,0},{2,3},{3,2},{4,5},{5,4},{6,7},{7,6},{8,9},{9,8},{10,11... | collective-permute-start | bytes 1572872 | tf_op jit(solution)/shard_map/ppermute | solution.py:521
  84.9 1.0 slice_select_fusion.1.refs_1_
  85.9 1.3 collective-permute-start.9
  87.2 1.0 slice_select_fusion.refs_2_
  88.2 12.2 %collective-permute-done.9 = bf16[32,8192]{1,0:T(8,128)(2,1)S(1)} collective-permute-done((bf16[32,8192]{1,0:T(8,128)(2,1)S(1)}, bf16[32,8192]{1,0:T(8,128)(2,1)S(1)}, u32[]{:S(2)}, u32[]{:S(2)}) %collective-permute-start.9) | collective-permute-done | bytes 524320 | tf_op jit(solution)/shard_map/ppermute | solution.py:521
  100.4 0.5 collective-permute-start.13
  100.9 0.1 broadcast_select_fusion.refs_0_
  101.0 1.6 %collective-permute-start.15 = (bf16[16,8192]{1,0:T(8,128)(2,1)S(1)}, bf16[16,8192]{1,0:T(8,128)(2,1)S(1)}, u32[]{:S(2)}, u32[]{:S(2)}) collective-permute-start(bf16[16,8192]{1,0:T(8,128)(2,1)S(1)} %slice_select_fusion.1.refs_1_), channel_id=1, source_target_pairs={{0,1},{1,0},{2,3},{3,2},{4,5},{5,4},{6,7},{7,6},{8,9},{9,8},{10,11... | collective-permute-start | bytes 786440 | tf_op jit(solution)/shard_map/ppermute | solution.py:521
  102.5 4.7 %project.8 = (bf16[128,1024]{1,0:T(8,128)(2,1)S(1)}, bf16[64,256]{1,0:T(8,128)(2,1)S(1)}, bf16[64,256]{1,0:T(8,128)(2,1)S(1)}) custom-call(s32[1]{0:T(128)} %bitcast.member, bf16[32,8192]{1,0:T(8,128)(2,1)S(1)} %broadcast_select_fusion.2.refs_0_, bf16[32,8192]{1,0:T(8,128)(2,1)S(1)} %broadcast_select_fusion.1.refs_1_, ...), custom_call_target="tpu_custom_call" | custom-call | flops 10000000000 | bytes 1000 | tf_op jit(solution)/shard_map/project/pallas_call | solution.py:165
  107.2 0.6 collective-permute-start.16
  107.8 7.4 %collective-permute-done.13.refs_4_ = bf16[32,8192]{1,0:T(8,128)(2,1)S(1)} collective-permute-done((bf16[32,8192]{1,0:T(8,128)(2,1)S(1)}, bf16[32,8192]{1,0:T(8,128)(2,1)S(1)}, u32[]{:S(2)}, u32[]{:S(2)}) %collective-permute-start.13) | collective-permute-done | bytes 524320 | tf_op jit(solution)/shard_map/ppermute | solution.py:521
  115.2 3.1 %collective-permute-start.14 = (bf16[32,8192]{1,0:T(8,128)(2,1)S(1)}, bf16[32,8192]{1,0:T(8,128)(2,1)S(1)}, u32[]{:S(2)}, u32[]{:S(2)}) collective-permute-start(bf16[32,8192]{1,0:T(8,128)(2,1)S(1)} %collective-permute-done.12.refs_3_), channel_id=1, source_target_pairs={{0,2},{1,3},{2,0},{3,1},{4,6},{5,7},{6,4},{7,5},{8,10},{9,11},{10,... | collective-permute-start | bytes 1572872 | tf_op jit(solution)/shard_map/ppermute | solution.py:521
  118.3 4.9 %project.9 = (bf16[128,1024]{1,0:T(8,128)(2,1)S(1)}, bf16[64,256]{1,0:T(8,128)(2,1)S(1)}, bf16[64,256]{1,0:T(8,128)(2,1)S(1)}) custom-call(s32[1]{0:T(128)} %bitcast.member, bf16[32,8192]{1,0:T(8,128)(2,1)S(1)} %broadcast_select_fusion.refs_0_, bf16[16,8192]{1,0:T(8,128)(2,1)S(1)} %slice_select_fusion.1.refs_1_, ...), custom_call_target="tpu_custom_call" | custom-call | flops 10000000000 | bytes 1000 | tf_op jit(solution)/shard_map/project/pallas_call | solution.py:165
  123.2 0.1 collective-permute-start.19
  123.3 1.0 collective-permute-done.16.refs_2_
  124.3 2.8 %collective-permute-start.20 = (bf16[64,256]{1,0:T(8,128)(2,1)S(1)}, bf16[64,256]{1,0:T(8,128)(2,1)S(1)}, u32[]{:S(2)}, u32[]{:S(2)}) collective-permute-start(bf16[64,256]{1,0:T(8,128)(2,1)S(1)} %get-tuple-element.35.refs_9_), channel_id=1, source_target_pairs={{0,11},{1,10},{2,9},{3,8},{4,15},{5,14},{6,13},{7,12},{8,3},{9,2},... | collective-permute-start | bytes 98312 | tf_op jit(solution)/shard_map/ppermute | solution.py:538
  127.0 2.0 %collective-permute-done.14.refs_0_ = bf16[32,8192]{1,0:T(8,128)(2,1)S(1)} collective-permute-done((bf16[32,8192]{1,0:T(8,128)(2,1)S(1)}, bf16[32,8192]{1,0:T(8,128)(2,1)S(1)}, u32[]{:S(2)}, u32[]{:S(2)}) %collective-permute-start.14) | collective-permute-done | bytes 524320 | tf_op jit(solution)/shard_map/ppermute | solution.py:521
  129.0 0.1 collective-permute-start.21
  129.1 2.0 %project.10 = (bf16[64,256]{1,0:T(8,128)(2,1)S(1)}, bf16[64,8192]{1,0:T(8,128)(2,1)S(1)}) custom-call(s32[1]{0:T(128)} %bitcast.member, bf16[32,8192]{1,0:T(8,128)(2,1)S(1)} %collective-permute-done.14.refs_0_, bf16[16,8192]{1,0:T(8,128)(2,1)S(1)} %collective-permute-done.15.refs_1_, bf16[16,8192]{1,0:T(8,128)(2,1)S(1)} %collective-permute-done.16.refs_2_, ...), custom_call_target="tpu_custom_call" | custom-call | flops 10000000000 | bytes 1000 | tf_op jit(solution)/shard_map/project/pallas_call | solution.py:165
  131.2 0.1 slice-done
  131.2 1.3 slice-done.1
  132.5 1.2 slice-done.2
  133.7 1.2 slice-done.3
  134.9 3.2 %project.11.refs_4_ = bf16[64,1024]{1,0:T(8,128)(2,1)S(1)} custom-call(s32[1]{0:T(128)} %bitcast.member, bf16[64,8192]{1,0:T(8,128)(2,1)S(1)} %get-tuple-element.30.refs_0_, bf16[1,8192]{1,0:T(2,128)(2,1)S(1)} %reshape.56.refs_1_.refs_2_.refs_3_.refs_5_, bf16[8192,1024]{1,0:T(8,128)(2,1)S(1)} %bitcast.10, ...), custom_call_target="tpu_custom_call" | custom-call | flops 10000000000 | bytes 1000 | tf_op jit(solution)/shard_map/project/pallas_call | solution.py:165
  138.1 0.1 collective-permute-start.22
  138.2 3.4 %collective-permute-start.23 = (bf16[64,256]{1,0:T(8,128)(2,1)S(1)}, bf16[64,256]{1,0:T(8,128)(2,1)S(1)}, u32[]{:S(2)}, u32[]{:S(2)}) collective-permute-start(bf16[64,256]{1,0:T(8,128)(2,1)S(1)} %get-tuple-element.36.refs_10_), channel_id=1, source_target_pairs={{0,14},{1,15},{2,12},{3,13},{4,10},{5,11},{6,8},{7,9},{8,6},{9,7},... | collective-permute-start | bytes 98312 | tf_op jit(solution)/shard_map/ppermute | solution.py:538
  141.6 1.0 collective-permute-start.24
  142.6 3.4 %attend.1 = bf16[512,1024]{1,0:T(8,128)(2,1)} custom-call(s32[1]{0:T(128)} %bitcast.member, bf16[64,1024]{1,0:T(8,128)(2,1)S(1)} %get-tuple-element.23.refs_0_, bf16[128,1024]{1,0:T(8,128)(2,1)S(1)} %get-tuple-element.24.refs_1_, bf16[128,1024]{1,0:T(8,128)(2,1)S(1)} %get-tuple-element.26.refs_2_, bf16[128,1024]{1,0:T(8,128)(2,1)S(1)} %get-tuple-element.29.refs_3_, ...), custom_call_target="tpu_custom_call" | custom-call | flops 5000000000 | bytes 1000 | tf_op jit(solution)/shard_map/attend/pallas_call | solution.py:243
  146.1 1.6 %collective-permute-done.24.refs_7_ = bf16[64,256]{1,0:T(8,128)(2,1)S(1)} collective-permute-done((bf16[64,256]{1,0:T(8,128)(2,1)S(1)}, bf16[64,256]{1,0:T(8,128)(2,1)S(1)}, u32[]{:S(2)}, u32[]{:S(2)}) %collective-permute-start.24) | collective-permute-done | bytes 32800 | tf_op jit(solution)/shard_map/ppermute | solution.py:538
  147.6 1.3 decode_new.1
  (40 shorter events, 0.1 us)
Async XLA Ops:
  0.6 36.5 %collective-permute-start = (bf16[64,8192]{1,0:T(8,128)(2,1)}, bf16[64,8192]{1,0:T(8,128)(2,1)S(1)}, u32[]{:S(2)}, u32[]{:S(2)}) collective-permute-start(bf16[64,8192]{1,0:T(8,128)(2,1)} %bitcast.5), channel_id=1, source_target_pairs={{0,2},{1,3},{2,0},{3,1},{4,6},{5,7},{6,4},{7,5},{8,10},{9,11},{10,... | collective-permute-start | bytes 3145736 | tf_op jit(solution)/shard_map/ppermute | solution.py:521
  3.7 34.1 %collective-permute-start.1 = (bf16[64,8192]{1,0:T(8,128)(2,1)}, bf16[64,8192]{1,0:T(8,128)(2,1)}, u32[]{:S(2)}, u32[]{:S(2)}) collective-permute-start(bf16[64,8192]{1,0:T(8,128)(2,1)} %bitcast.6), channel_id=1, source_target_pairs={{0,1},{1,0},{2,3},{3,2},{4,5},{5,4},{6,7},{7,6},{8,9},{9,8},{10,11... | collective-permute-start | bytes 3145736 | tf_op jit(solution)/shard_map/ppermute | solution.py:521
  7.2 27.3 %collective-permute-start.2 = (bf16[32,8192]{1,0:T(8,128)(2,1)}, bf16[32,8192]{1,0:T(8,128)(2,1)S(1)}, u32[]{:S(2)}, u32[]{:S(2)}) collective-permute-start(bf16[32,8192]{1,0:T(8,128)(2,1)} %slice_bitcast_fusion), channel_id=1, source_target_pairs={{2,4},{3,5},{4,2},{5,3},{10,12},{11,13},{12,10},{13,11},{18,20},{1... | collective-permute-start | bytes 1572872 | tf_op jit(solution)/shard_map/ppermute | solution.py:521
  9.7 26.1 %collective-permute-start.5 = (bf16[32,8192]{1,0:T(8,128)(2,1)}, bf16[32,8192]{1,0:T(8,128)(2,1)}, u32[]{:S(2)}, u32[]{:S(2)}) collective-permute-start(bf16[32,8192]{1,0:T(8,128)(2,1)} %slice.30), channel_id=1, source_target_pairs={{2,4},{3,5},{4,2},{5,3},{10,12},{11,13},{12,10},{13,11},{18,20},{1... | collective-permute-start | bytes 1572872 | tf_op jit(solution)/shard_map/ppermute | solution.py:521
  13.0 1.2 copy-start
  14.2 5.8 %copy-start.1 = (bf16[8192,1024]{1,0:T(8,128)(2,1)S(1)}, bf16[8192,1024]{1,0:T(8,128)(2,1)}, u32[]{:S(2)}) copy-start(bf16[8192,1024]{1,0:T(8,128)(2,1)} %refs_2_.3) | copy-start | bytes 50331652
  20.0 2.2 %copy-start.4 = (bf16[8192,256]{1,0:T(8,128)(2,1)S(1)}, bf16[8192,256]{1,0:T(8,128)(2,1)}, u32[]{:S(2)}) copy-start(bf16[8192,256]{1,0:T(8,128)(2,1)} %refs_4_.3) | copy-start | bytes 12582916
  22.1 4.7 %copy-start.6 = (bf16[4,8192]{1,0:T(4,128)(2,1)S(1)}, bf16[4,8192]{1,0:T(4,128)(2,1)}, u32[]{:S(2)}) copy-start(bf16[4,8192]{1,0:T(4,128)(2,1)} %query_ref.1) | copy-start | bytes 196612
  22.2 4.7 %copy-start.8 = (s32[4,24]{1,0:T(4,128)S(1)}, s32[4,24]{1,0:T(4,128)}, u32[]{:S(2)}) copy-start(s32[4,24]{1,0:T(4,128)} %tables.1) | copy-start | bytes 1156
  22.2 4.7 %copy-start.9 = (s32[4]{0:T(128)S(1)}, s32[4]{0:T(128)}, u32[]{:S(2)}) copy-start(s32[4]{0:T(128)} %lengths.1) | copy-start | bytes 52
  22.2 4.7 %copy-start.10 = (s32[1,4]{1,0:T(1,128)S(1)}, s32[1,4]{1,0:T(1,128)}, u32[]{:S(2)}) copy-start(s32[1,4]{1,0:T(1,128)} %slots.1) | copy-start | bytes 52
  26.7 1.7 %copy-start.7 = (bf16[4,2048]{1,0:T(4,128)(2,1)S(1)}, bf16[4,2048]{1,0:T(4,128)(2,1)}, u32[]{:S(2)}) copy-start(bf16[4,2048]{1,0:T(4,128)(2,1)} %own_ref.1) | copy-start | bytes 49156
  26.8 111.3 %collective-permute-start.17 = (bf16[64,256]{1,0:T(8,128)(2,1)S(1)}, bf16[64,256]{1,0:T(8,128)(2,1)S(1)}, u32[]{:S(2)}, u32[]{:S(2)}) collective-permute-start(bf16[64,256]{1,0:T(8,128)(2,1)S(1)} %get-tuple-element.31.refs_5_), channel_id=1, source_target_pairs={{0,8},{1,9},{2,10},{3,11},{4,12},{5,13},{6,14},{7,15},{8,0},{9,1},... | collective-permute-start | bytes 98312 | tf_op jit(solution)/shard_map/ppermute | solution.py:538
  28.5 2.8 %copy-start.3 = (bf16[96,16,2048]{2,1,0:T(8,128)(2,1)S(1)}, bf16[96,16,2048]{2,1,0:T(8,128)(2,1)}, u32[]{:S(2)}) copy-start(bf16[96,16,2048]{2,1,0:T(8,128)(2,1)} %pool.1) | copy-start | bytes 18874372
  31.2 7.4 %copy-start.5 = (bf16[8192,256]{1,0:T(8,128)(2,1)S(1)}, bf16[8192,256]{1,0:T(8,128)(2,1)}, u32[]{:S(2)}) copy-start(bf16[8192,256]{1,0:T(8,128)(2,1)} %refs_4_.3) | copy-start | bytes 12582916
  34.5 31.5 %collective-permute-start.3 = (bf16[32,8192]{1,0:T(8,128)(2,1)S(1)}, bf16[32,8192]{1,0:T(8,128)(2,1)S(1)}, u32[]{:S(2)}, u32[]{:S(2)}) collective-permute-start(bf16[32,8192]{1,0:T(8,128)(2,1)S(1)} %collective-permute-done.2), channel_id=1, source_target_pairs={{2,0},{3,1},{4,6},{5,7},{10,8},{11,9},{12,14},{13,15},{18,16},{19,... | collective-permute-start | bytes 1572872 | tf_op jit(solution)/shard_map/ppermute | solution.py:521
  35.8 28.6 %collective-permute-start.6 = (bf16[32,8192]{1,0:T(8,128)(2,1)}, bf16[32,8192]{1,0:T(8,128)(2,1)S(1)}, u32[]{:S(2)}, u32[]{:S(2)}) collective-permute-start(bf16[32,8192]{1,0:T(8,128)(2,1)} %collective-permute-done.5), channel_id=1, source_target_pairs={{2,0},{3,1},{4,6},{5,7},{10,8},{11,9},{12,14},{13,15},{18,16},{19,... | collective-permute-start | bytes 1572872 | tf_op jit(solution)/shard_map/ppermute | solution.py:521
  37.2 30.3 %collective-permute-start.4 = (bf16[32,8192]{1,0:T(8,128)(2,1)S(1)}, bf16[32,8192]{1,0:T(8,128)(2,1)S(1)}, u32[]{:S(2)}, u32[]{:S(2)}) collective-permute-start(bf16[32,8192]{1,0:T(8,128)(2,1)S(1)} %get-tuple-element.45), channel_id=1, source_target_pairs={{2,4},{3,5},{4,2},{5,3},{10,12},{11,13},{12,10},{13,11},{18,20},{1... | collective-permute-start | bytes 1572872 | tf_op jit(solution)/shard_map/ppermute | solution.py:521
  37.9 26.5 %collective-permute-start.7 = (bf16[32,8192]{1,0:T(8,128)(2,1)S(1)}, bf16[32,8192]{1,0:T(8,128)(2,1)S(1)}, u32[]{:S(2)}, u32[]{:S(2)}) collective-permute-start(bf16[32,8192]{1,0:T(8,128)(2,1)S(1)} %get-tuple-element.44), channel_id=1, source_target_pairs={{2,4},{3,5},{4,2},{5,3},{10,12},{11,13},{12,10},{13,11},{18,20},{1... | collective-permute-start | bytes 1572872 | tf_op jit(solution)/shard_map/ppermute | solution.py:521
  38.6 5.8 %copy-start.2 = (bf16[8192,1024]{1,0:T(8,128)(2,1)S(1)}, bf16[8192,1024]{1,0:T(8,128)(2,1)}, u32[]{:S(2)}) copy-start(bf16[8192,1024]{1,0:T(8,128)(2,1)} %refs_2_.3) | copy-start | bytes 50331652
  64.4 73.8 %collective-permute-start.18 = (bf16[64,256]{1,0:T(8,128)(2,1)S(1)}, bf16[64,256]{1,0:T(8,128)(2,1)S(1)}, u32[]{:S(2)}, u32[]{:S(2)}) collective-permute-start(bf16[64,256]{1,0:T(8,128)(2,1)S(1)} %get-tuple-element.33.refs_7_), channel_id=1, source_target_pairs={{0,9},{1,8},{2,11},{3,10},{4,13},{5,12},{6,15},{7,14},{8,1},{9,0},... | collective-permute-start | bytes 98312 | tf_op jit(solution)/shard_map/ppermute | solution.py:538
  64.4 36.6 %collective-permute-start.8 = (bf16[64,8192]{1,0:T(8,128)(2,1)S(1)}, bf16[64,8192]{1,0:T(8,128)(2,1)S(1)}, u32[]{:S(2)}, u32[]{:S(2)}) collective-permute-start(bf16[64,8192]{1,0:T(8,128)(2,1)S(1)} %collective-permute-done.refs_0_), channel_id=1, source_target_pairs={{0,1},{1,0},{2,3},{3,2},{4,5},{5,4},{6,7},{7,6},{8,9},{9,8},{10,11... | collective-permute-start | bytes 3145736 | tf_op jit(solution)/shard_map/ppermute | solution.py:521
  66.0 19.9 %collective-permute-start.10 = (bf16[16,8192]{1,0:T(8,128)(2,1)S(1)}, bf16[16,8192]{1,0:T(8,128)(2,1)S(1)}, u32[]{:S(2)}, u32[]{:S(2)}) collective-permute-start(bf16[16,8192]{1,0:T(8,128)(2,1)S(1)} %get-tuple-element.47), channel_id=1, source_target_pairs={{2,0},{3,1},{4,6},{5,7},{10,8},{11,9},{12,14},{13,15},{18,16},{19,... | collective-permute-start | bytes 786440 | tf_op jit(solution)/shard_map/ppermute | solution.py:521
  67.5 15.9 %collective-permute-start.11 = (bf16[16,8192]{1,0:T(8,128)(2,1)S(1)}, bf16[16,8192]{1,0:T(8,128)(2,1)S(1)}, u32[]{:S(2)}, u32[]{:S(2)}) collective-permute-start(bf16[16,8192]{1,0:T(8,128)(2,1)S(1)} %get-tuple-element.46), channel_id=1, source_target_pairs={{2,0},{3,1},{4,6},{5,7},{10,8},{11,9},{12,14},{13,15},{18,16},{19,... | collective-permute-start | bytes 786440 | tf_op jit(solution)/shard_map/ppermute | solution.py:521
  83.4 23.8 %collective-permute-start.12 = (bf16[32,8192]{1,0:T(8,128)(2,1)S(1)}, bf16[32,8192]{1,0:T(8,128)(2,1)S(1)}, u32[]{:S(2)}, u32[]{:S(2)}) collective-permute-start(bf16[32,8192]{1,0:T(8,128)(2,1)S(1)} %broadcast_select_fusion.2.refs_0_), channel_id=1, source_target_pairs={{0,1},{1,0},{2,3},{3,2},{4,5},{5,4},{6,7},{7,6},{8,9},{9,8},{10,11... | collective-permute-start | bytes 1572872 | tf_op jit(solution)/shard_map/ppermute | solution.py:521
  85.9 14.5 %collective-permute-start.9 = (bf16[32,8192]{1,0:T(8,128)(2,1)S(1)}, bf16[32,8192]{1,0:T(8,128)(2,1)S(1)}, u32[]{:S(2)}, u32[]{:S(2)}) collective-permute-start(bf16[32,8192]{1,0:T(8,128)(2,1)S(1)} %collective-permute-done.4), channel_id=1, source_target_pairs={{2,0},{3,1},{4,6},{5,7},{10,8},{11,9},{12,14},{13,15},{18,16},{19,... | collective-permute-start | bytes 1572872 | tf_op jit(solution)/shard_map/ppermute | solution.py:521
  100.4 14.8 %collective-permute-start.13 = (bf16[32,8192]{1,0:T(8,128)(2,1)S(1)}, bf16[32,8192]{1,0:T(8,128)(2,1)S(1)}, u32[]{:S(2)}, u32[]{:S(2)}) collective-permute-start(bf16[32,8192]{1,0:T(8,128)(2,1)S(1)} %broadcast_select_fusion.1.refs_1_), channel_id=1, source_target_pairs={{0,1},{1,0},{2,3},{3,2},{4,5},{5,4},{6,7},{7,6},{8,9},{9,8},{10,11... | collective-permute-start | bytes 1572872 | tf_op jit(solution)/shard_map/ppermute | solution.py:521
  101.0 22.2 %collective-permute-start.15 = (bf16[16,8192]{1,0:T(8,128)(2,1)S(1)}, bf16[16,8192]{1,0:T(8,128)(2,1)S(1)}, u32[]{:S(2)}, u32[]{:S(2)}) collective-permute-start(bf16[16,8192]{1,0:T(8,128)(2,1)S(1)} %slice_select_fusion.1.refs_1_), channel_id=1, source_target_pairs={{0,1},{1,0},{2,3},{3,2},{4,5},{5,4},{6,7},{7,6},{8,9},{9,8},{10,11... | collective-permute-start | bytes 786440 | tf_op jit(solution)/shard_map/ppermute | solution.py:521
  107.2 17.1 %collective-permute-start.16 = (bf16[16,8192]{1,0:T(8,128)(2,1)S(1)}, bf16[16,8192]{1,0:T(8,128)(2,1)S(1)}, u32[]{:S(2)}, u32[]{:S(2)}) collective-permute-start(bf16[16,8192]{1,0:T(8,128)(2,1)S(1)} %slice_select_fusion.refs_2_), channel_id=1, source_target_pairs={{0,1},{1,0},{2,3},{3,2},{4,5},{5,4},{6,7},{7,6},{8,9},{9,8},{10,11... | collective-permute-start | bytes 786440 | tf_op jit(solution)/shard_map/ppermute | solution.py:521
  115.2 13.9 %collective-permute-start.14 = (bf16[32,8192]{1,0:T(8,128)(2,1)S(1)}, bf16[32,8192]{1,0:T(8,128)(2,1)S(1)}, u32[]{:S(2)}, u32[]{:S(2)}) collective-permute-start(bf16[32,8192]{1,0:T(8,128)(2,1)S(1)} %collective-permute-done.12.refs_3_), channel_id=1, source_target_pairs={{0,2},{1,3},{2,0},{3,1},{4,6},{5,7},{6,4},{7,5},{8,10},{9,11},{10,... | collective-permute-start | bytes 1572872 | tf_op jit(solution)/shard_map/ppermute | solution.py:521
  123.2 18.4 %collective-permute-start.19 = (bf16[64,256]{1,0:T(8,128)(2,1)S(1)}, bf16[64,256]{1,0:T(8,128)(2,1)S(1)}, u32[]{:S(2)}, u32[]{:S(2)}) collective-permute-start(bf16[64,256]{1,0:T(8,128)(2,1)S(1)} %get-tuple-element.32.refs_6_), channel_id=1, source_target_pairs={{0,10},{1,11},{2,8},{3,9},{4,14},{5,15},{6,12},{7,13},{8,2},{9,3},... | collective-permute-start | bytes 98312 | tf_op jit(solution)/shard_map/ppermute | solution.py:538
  124.3 21.8 %collective-permute-start.20 = (bf16[64,256]{1,0:T(8,128)(2,1)S(1)}, bf16[64,256]{1,0:T(8,128)(2,1)S(1)}, u32[]{:S(2)}, u32[]{:S(2)}) collective-permute-start(bf16[64,256]{1,0:T(8,128)(2,1)S(1)} %get-tuple-element.35.refs_9_), channel_id=1, source_target_pairs={{0,11},{1,10},{2,9},{3,8},{4,15},{5,14},{6,13},{7,12},{8,3},{9,2},... | collective-permute-start | bytes 98312 | tf_op jit(solution)/shard_map/ppermute | solution.py:538
  129.0 2.2 %slice-start = ((s8[16777216]{0:T(1024)(128)(4,1)}), s8[4194304]{0:T(1024)(128)(4,1)S(1)}, s32[]{:S(2)}) async-start(s8[16777216]{0:T(1024)(128)(4,1)} %bitcast.9), calls=%async_computation | async-start | bytes 8388608
  129.0 3.5 %slice-start.1 = ((s8[16777216]{0:T(1024)(128)(4,1)}), s8[4194304]{0:T(1024)(128)(4,1)S(1)}, s32[]{:S(2)}) async-start(s8[16777216]{0:T(1024)(128)(4,1)} %bitcast.9), calls=%async_computation.1 | async-start | bytes 8388608
  129.0 4.7 %slice-start.2 = ((s8[16777216]{0:T(1024)(128)(4,1)}), s8[4194304]{0:T(1024)(128)(4,1)S(1)}, s32[]{:S(2)}) async-start(s8[16777216]{0:T(1024)(128)(4,1)} %bitcast.9), calls=%async_computation.2 | async-start | bytes 8388608
  129.0 5.8 %slice-start.3 = ((s8[16777216]{0:T(1024)(128)(4,1)}), s8[4194304]{0:T(1024)(128)(4,1)S(1)}, s32[]{:S(2)}) async-start(s8[16777216]{0:T(1024)(128)(4,1)} %bitcast.9), calls=%async_computation.3 | async-start | bytes 8388608
  129.0 17.0 %collective-permute-start.21 = (bf16[64,256]{1,0:T(8,128)(2,1)S(1)}, bf16[64,256]{1,0:T(8,128)(2,1)S(1)}, u32[]{:S(2)}, u32[]{:S(2)}) collective-permute-start(bf16[64,256]{1,0:T(8,128)(2,1)S(1)} %get-tuple-element.34.refs_8_), channel_id=1, source_target_pairs={{0,12},{1,13},{2,14},{3,15},{4,8},{5,9},{6,10},{7,11},{8,4},{9,5},... | collective-permute-start | bytes 98312 | tf_op jit(solution)/shard_map/ppermute | solution.py:538
  138.1 8.0 %collective-permute-start.22 = (bf16[64,256]{1,0:T(8,128)(2,1)S(1)}, bf16[64,256]{1,0:T(8,128)(2,1)S(1)}, u32[]{:S(2)}, u32[]{:S(2)}) collective-permute-start(bf16[64,256]{1,0:T(8,128)(2,1)S(1)} %get-tuple-element.37.refs_11_), channel_id=1, source_target_pairs={{0,13},{1,12},{2,15},{3,14},{4,9},{5,8},{6,11},{7,10},{8,5},{9,4},... | collective-permute-start | bytes 98312 | tf_op jit(solution)/shard_map/ppermute | solution.py:538
  138.2 7.9 %collective-permute-start.23 = (bf16[64,256]{1,0:T(8,128)(2,1)S(1)}, bf16[64,256]{1,0:T(8,128)(2,1)S(1)}, u32[]{:S(2)}, u32[]{:S(2)}) collective-permute-start(bf16[64,256]{1,0:T(8,128)(2,1)S(1)} %get-tuple-element.36.refs_10_), channel_id=1, source_target_pairs={{0,14},{1,15},{2,12},{3,13},{4,10},{5,11},{6,8},{7,9},{8,6},{9,7},... | collective-permute-start | bytes 98312 | tf_op jit(solution)/shard_map/ppermute | solution.py:538
  141.6 6.0 %collective-permute-start.24 = (bf16[64,256]{1,0:T(8,128)(2,1)S(1)}, bf16[64,256]{1,0:T(8,128)(2,1)S(1)}, u32[]{:S(2)}, u32[]{:S(2)}) collective-permute-start(bf16[64,256]{1,0:T(8,128)(2,1)S(1)} %get-tuple-element.38.refs_12_), channel_id=1, source_target_pairs={{0,15},{1,14},{2,13},{3,12},{4,11},{5,10},{6,9},{7,8},{8,7},{9,6},... | collective-permute-start | bytes 98312 | tf_op jit(solution)/shard_map/ppermute | solution.py:538
